TPU v7x, 32 devices: a whole 2x2x4 slice. The times are simulated.
32 devices in a mesh: dp: 4 (over y, core), tensor: 8 (over z, x).
Axes of the slice: x: 2, y: 2, z: 4, core: 2. Of those that a mesh axis runs over, the one named last changes fastest.
Arguments:
- patches: bfloat16 [32, 256, 1152], P('dp'), may hold values from -6 to 6
- conditioning: bfloat16 [32, 1152], P('dp'), may hold values from -6 to 6
- keep_count: int32 [32], P('dp'), may hold values from 64 to 192, as said below
- keep_index: int32 [32, 192], P('dp'), may hold values from 0 to 255, as said below
- mod_weight: bfloat16 [1152, 6912], P(None, 'tensor'), may hold values from -0.1875 to 0.1875
- mod_bias: bfloat16 [6912], P('tensor'), may hold values from -3 to 3
- qkv_weight: bfloat16 [3, 1152, 1152], P(None, None, 'tensor'), may hold values from -0.1875 to 0.1875
- qv_bias: bfloat16 [2, 1152], P(None, 'tensor'), may hold values from -3 to 3
- out_weight: bfloat16 [1152, 1152], P('tensor'), may hold values from -1.25 to 1.25
- out_bias: bfloat16 [1152], replicated, may hold values from -2 to 2
- up_weight: bfloat16 [1152, 4608], P(None, 'tensor'), may hold values from -0.1875 to 0.1875
- up_bias: bfloat16 [4608], P('tensor'), may hold values from -3 to 3
- down_weight: bfloat16 [4608, 1152], P('tensor'), may hold values from -0.09375 to 0.09375
- down_bias: bfloat16 [1152], replicated, may hold values from -2 to 2
- out_cotangent: bfloat16 [32, 192, 1152], P('dp'), may hold values from -6 to 6
Outputs:
- block_out: bfloat16 [32, 192, 1152], P('dp')
- grad_patches: bfloat16 [32, 256, 1152], P('dp')
- grad_conditioning: bfloat16 [32, 1152], P('dp')
- mod_weight_grad: float32 [1152, 6912], P(None, 'tensor')
- mod_bias_grad: float32 [6912], P('tensor')
- qkv_weight_grad: float32 [3, 1152, 1152], P(None, None, 'tensor')
- qv_bias_grad: float32 [2, 1152], P(None, 'tensor')
- out_weight_grad: float32 [1152, 1152], P('tensor')
- out_bias_grad: float32 [1152], replicated
- up_weight_grad: float32 [1152, 4608], P(None, 'tensor')
- up_bias_grad: float32 [4608], P('tensor')
- down_weight_grad: float32 [4608, 1152], P('tensor')
- down_bias_grad: float32 [1152], replicated
Inputs may be any that keep to these rules, and one draw needn't show every extreme that they name: `keep_count`: some image keeps 192 tokens and some keeps 64. A row of keep_index lists 192 different patch positions; the first keep_count of them are the image's kept tokens, the others are not read.
All inputs are finite; a program needn't handle non-finite values.
Results may differ from a plain program's by a relative error of at most 0.014.
The roundings to bfloat16 on the way count: a program that leaves them out, or rounds other values in their place, can miss the bound.
Values may be sent and summed in bfloat16 or wider, within the bound.
A program may use at most 192 MiB of HBM per device.

v0:
```python
import jax
import jax.numpy as jnp
from jax import lax
from jax.sharding import PartitionSpec as P

HD = 72


def layer_norm(inputs):
    centred = inputs - jnp.mean(inputs, axis=-1, keepdims=True)
    return centred * lax.rsqrt(jnp.mean(centred * centred, axis=-1, keepdims=True) + 1e-06)


def on_device(
    patches,
    conditioning,
    keep_count,
    keep_index,
    mod_weight,
    mod_bias,
    qkv_weight,
    qv_bias,
    out_weight,
    out_bias,
    up_weight,
    up_bias,
    down_weight,
    down_bias,
    out_cotangent,
):
    images, kept_rows = keep_index.shape
    model_width = patches.shape[2]
    local_width = qkv_weight.shape[2]
    local_heads = local_width // HD
    count_rows = images * kept_rows
    share_rows = kept_rows // lax.axis_size("tensor")
    share_start = lax.axis_index("tensor") * share_rows
    score_scale = HD ** (-0.5)
    live_rows = (jnp.arange(kept_rows, dtype=jnp.int32)[None, :] < keep_count[:, None]).astype(
        jnp.float32
    )[:, :, None]
    tokens = (
        jnp.take_along_axis(patches, keep_index[:, :, None], axis=1).astype(jnp.float32) * live_rows
    )
    cond_float = conditioning.astype(jnp.float32)
    silu_low = jax.nn.silu(cond_float).astype(jnp.bfloat16)
    mod_local = (
        jnp.dot(silu_low, mod_weight, preferred_element_type=jnp.float32)
        + mod_bias.astype(jnp.float32)
    ).astype(jnp.bfloat16)
    mod_full = lax.all_gather(mod_local, "tensor", axis=1, tiled=True).astype(jnp.float32)
    blocks = [
        mod_full[:, None, member * model_width : (member + 1) * model_width] for member in range(6)
    ]
    shift_one, scale_one, gate_one, shift_two, scale_two, gate_two = blocks
    norm_one = layer_norm(tokens)
    normed_one = (
        (norm_one * (1.0 + scale_one) + shift_one)
        .astype(jnp.bfloat16)
        .reshape(count_rows, model_width)
    )
    projected = jnp.einsum(
        "rd,tdh->trh", normed_one, qkv_weight, preferred_element_type=jnp.float32
    )
    bias_rows = jnp.stack([qv_bias[0], jnp.zeros_like(qv_bias[0]), qv_bias[1]]).astype(jnp.float32)[
        :, None, :
    ]
    qkv_rows = (projected + bias_rows).astype(jnp.bfloat16)
    queries, key_rows, value_rows = [
        qkv_rows[member].reshape(images, kept_rows, local_heads, HD) for member in range(3)
    ]
    key_live = live_rows[:, :, 0][:, None, None, :] > 0
    scores = (
        jnp.einsum("bqhd,bkhd->bhqk", queries, key_rows, preferred_element_type=jnp.float32)
        * score_scale
    )
    scores = jnp.where(key_live, scores, -1e30)
    row_top = jnp.max(scores, axis=-1, keepdims=True)
    exp_scores = jnp.exp(scores - row_top)
    row_total = jnp.sum(exp_scores, axis=-1, keepdims=True)
    log_total = row_top + jnp.log(row_total)
    weights_low = (exp_scores / row_total).astype(jnp.bfloat16)
    attended = jnp.einsum(
        "bhqk,bkhd->bqhd", weights_low, value_rows, preferred_element_type=jnp.float32
    )
    attended = attended.astype(jnp.bfloat16).reshape(count_rows, local_width)
    branch_part = jnp.dot(attended, out_weight, preferred_element_type=jnp.float32).reshape(
        images, kept_rows, model_width
    )
    out_bias_float = out_bias.astype(jnp.float32)
    branch = lax.psum(branch_part, "tensor") + out_bias_float
    middle = tokens + gate_one * branch
    norm_two = layer_norm(middle)
    normed_two = (norm_two * (1.0 + scale_two) + shift_two).astype(jnp.bfloat16)
    branch_share = lax.dynamic_slice_in_dim(branch, share_start, share_rows, 1)
    normed_rows = normed_two.reshape(count_rows, model_width)
    pre_act = jnp.dot(normed_rows, up_weight, preferred_element_type=jnp.float32) + up_bias.astype(
        jnp.float32
    )
    hidden = jax.nn.gelu(pre_act, approximate=True).astype(jnp.bfloat16)
    mlp_part = jnp.dot(hidden, down_weight, preferred_element_type=jnp.float32).reshape(
        images, kept_rows, model_width
    )
    down_bias_float = down_bias.astype(jnp.float32)
    mlp_out = (
        lax.psum(mlp_part.astype(jnp.bfloat16), "tensor").astype(jnp.float32) + down_bias_float
    )
    block_out = ((middle + gate_two * mlp_out) * live_rows).astype(jnp.bfloat16)
    mlp_share = lax.dynamic_slice_in_dim(mlp_out, share_start, share_rows, 1)
    grad_out = out_cotangent.astype(jnp.float32) * live_rows
    grad_share = lax.dynamic_slice_in_dim(grad_out, share_start, share_rows, 1)
    grad_gate_two = jnp.sum(grad_share * mlp_share, axis=1)
    grad_mlp = (gate_two * grad_out).astype(jnp.bfloat16).reshape(count_rows, model_width)
    down_bias_grad = jnp.sum(grad_mlp.astype(jnp.float32), axis=0)
    down_weight_grad = jnp.einsum("rf,rd->fd", hidden, grad_mlp, preferred_element_type=jnp.float32)
    grad_hidden = jnp.einsum("rd,fd->rf", grad_mlp, down_weight, preferred_element_type=jnp.float32)
    gelu_pull = jax.vjp(lambda inputs: jax.nn.gelu(inputs, approximate=True), pre_act)[1]
    grad_pre = gelu_pull(grad_hidden)[0].astype(jnp.bfloat16)
    up_bias_grad = jnp.sum(grad_pre.astype(jnp.float32), axis=0)
    up_weight_grad = jnp.einsum(
        "rd,rf->df", normed_rows, grad_pre, preferred_element_type=jnp.float32
    )
    grad_normed_two = jnp.einsum(
        "rf,df->rd", grad_pre, up_weight, preferred_element_type=jnp.float32
    ).reshape(images, kept_rows, model_width)
    grad_shift_two = jnp.sum(grad_normed_two, axis=1)
    grad_scale_two = jnp.sum(grad_normed_two * norm_two, axis=1)
    second_pull = jax.vjp(layer_norm, middle)[1]
    second_term = second_pull(grad_normed_two * (1.0 + scale_two))[0]
    grad_middle = grad_out + lax.psum(second_term, "tensor")
    grad_mid_share = lax.dynamic_slice_in_dim(grad_middle, share_start, share_rows, 1)
    grad_branch = (gate_one * grad_middle).astype(jnp.bfloat16)
    grad_gate_one = jnp.sum(grad_mid_share * branch_share, axis=1)
    grad_branch = grad_branch.reshape(count_rows, model_width)
    out_bias_grad = jnp.sum(grad_branch.astype(jnp.float32), axis=0)
    out_weight_grad = jnp.einsum(
        "rh,rd->hd", attended, grad_branch, preferred_element_type=jnp.float32
    )
    grad_att = jnp.einsum("rd,hd->rh", grad_branch, out_weight, preferred_element_type=jnp.float32)
    grad_att = grad_att.astype(jnp.bfloat16).reshape(images, kept_rows, local_heads, HD)
    scores_again = (
        jnp.einsum("bqhd,bkhd->bhqk", queries, key_rows, preferred_element_type=jnp.float32)
        * score_scale
    )
    weights_again = jnp.where(key_live, jnp.exp(scores_again - log_total), 0.0)
    grad_weights = jnp.einsum(
        "bqhd,bkhd->bhqk", grad_att, value_rows, preferred_element_type=jnp.float32
    )
    row_inner = jnp.sum(weights_again * grad_weights, axis=-1, keepdims=True)
    grad_scores = (weights_again * (grad_weights - row_inner)).astype(jnp.bfloat16)
    grad_values = jnp.einsum(
        "bhqk,bqhd->bkhd",
        weights_again.astype(jnp.bfloat16),
        grad_att,
        preferred_element_type=jnp.float32,
    )
    grad_queries = (
        jnp.einsum("bhqk,bkhd->bqhd", grad_scores, key_rows, preferred_element_type=jnp.float32)
        * score_scale
    )
    grad_keys = (
        jnp.einsum("bhqk,bqhd->bkhd", grad_scores, queries, preferred_element_type=jnp.float32)
        * score_scale
    )
    grad_qkv = jnp.stack(
        [
            member.reshape(count_rows, local_width)
            for member in (grad_queries, grad_keys, grad_values)
        ]
    ).astype(jnp.bfloat16)
    qkv_weight_grad = jnp.einsum(
        "rd,trh->tdh", normed_one, grad_qkv, preferred_element_type=jnp.float32
    )
    qv_bias_grad = jnp.stack(
        [
            jnp.sum(grad_qkv[0].astype(jnp.float32), axis=0),
            jnp.sum(grad_qkv[2].astype(jnp.float32), axis=0),
        ]
    )
    grad_normed_one = jnp.einsum(
        "trh,tdh->rd", grad_qkv, qkv_weight, preferred_element_type=jnp.float32
    ).reshape(images, kept_rows, model_width)
    grad_shift_one = jnp.sum(grad_normed_one, axis=1)
    grad_scale_one = jnp.sum(grad_normed_one * norm_one, axis=1)
    first_pull = jax.vjp(layer_norm, tokens)[1]
    first_term = first_pull(grad_normed_one * (1.0 + scale_one))[0]
    grad_tokens = (grad_middle + lax.psum(first_term, "tensor")) * live_rows
    grad_token_low = grad_tokens.astype(jnp.bfloat16)
    empty_grads = jnp.zeros(patches.shape, jnp.bfloat16)
    grad_patches = jax.vmap(
        lambda row_block, index_row, grad_block: row_block.at[index_row].set(grad_block)
    )(empty_grads, keep_index, grad_token_low)
    grad_mod_part = jnp.concatenate(
        [
            grad_shift_one,
            grad_scale_one,
            grad_gate_one,
            grad_shift_two,
            grad_scale_two,
            grad_gate_two,
        ],
        axis=1,
    )
    grad_mod = lax.psum_scatter(grad_mod_part, "tensor", scatter_dimension=1, tiled=True)
    silu_float = silu_low.astype(jnp.float32)
    mod_weight_grad = jnp.einsum("bd,bm->dm", silu_float, grad_mod, precision=lax.Precision.HIGHEST)
    mod_bias_grad = jnp.sum(grad_mod, axis=0)
    silu_term = jnp.einsum(
        "bm,dm->bd", grad_mod, mod_weight.astype(jnp.float32), precision=lax.Precision.HIGHEST
    )
    grad_silu = lax.psum(silu_term, "tensor")
    silu_pull = jax.vjp(jax.nn.silu, cond_float)[1]
    grad_conditioning = silu_pull(grad_silu)[0].astype(jnp.bfloat16)
    summed = (
        lax.psum(mod_weight_grad.astype(jnp.bfloat16), "dp").astype(jnp.float32),
        lax.psum(mod_bias_grad.astype(jnp.bfloat16), "dp").astype(jnp.float32),
        lax.psum(qkv_weight_grad.astype(jnp.bfloat16), "dp").astype(jnp.float32),
        lax.psum(qv_bias_grad.astype(jnp.bfloat16), "dp").astype(jnp.float32),
        lax.psum(out_weight_grad.astype(jnp.bfloat16), "dp").astype(jnp.float32),
        lax.psum(out_bias_grad.astype(jnp.bfloat16), "dp").astype(jnp.float32),
        lax.psum(up_weight_grad.astype(jnp.bfloat16), "dp").astype(jnp.float32),
        lax.psum(up_bias_grad.astype(jnp.bfloat16), "dp").astype(jnp.float32),
        lax.psum(down_weight_grad.astype(jnp.bfloat16), "dp").astype(jnp.float32),
        lax.psum(down_bias_grad.astype(jnp.bfloat16), "dp").astype(jnp.float32),
    )
    return (block_out, grad_patches, grad_conditioning) + tuple(summed)


def solution(mesh):
    placed = (
        P("dp", None, None),
        P("dp", None),
        P("dp"),
        P("dp", None),
        P(None, "tensor"),
        P("tensor"),
        P(None, None, "tensor"),
        P(None, "tensor"),
        P("tensor", None),
        P(),
        P(None, "tensor"),
        P("tensor"),
        P("tensor", None),
        P(),
        P("dp", None, None),
    )
    return jax.shard_map(
        on_device,
        mesh=mesh,
        in_specs=placed,
        out_specs=(
            P("dp", None, None),
            P("dp", None, None),
            P("dp", None),
            P(None, "tensor"),
            P("tensor"),
            P(None, None, "tensor"),
            P(None, "tensor"),
            P("tensor", None),
            P(),
            P(None, "tensor"),
            P("tensor"),
            P("tensor", None),
            P(),
        ),
        check_vma=False,
    )
```

profile of v0, /device:TPU:0, one launch (start us, length us, event | category | flops | bytes accessed | tf_op | source)
XLA Modules:
  0.0 1267.2 jit_solution(10761815162576918113)
XLA Ops:
  9.1 32.2 %gather_fusion = bf16[1536,1152]{1,0:T(8,128)(2,1)} fusion(bf16[8,256,1152]{2,1,0:T(8,128)(2,1)} %param.15, s32[1536]{0:T(1024)S(1)} %reshape.255), kind=kCustom, calls=%fused_computation | custom fusion | bytes 7090176 | tf_op jit(solution)/shard_map/jit(take_along_axis)/gather | solution.py:43
  48.2 32.4 %all-gather = bf16[8,864,8]{1,2,0:T(8,128)(2,1)S(1)} all-gather(bf16[1,864,8]{1,2,0:T(8,128)(2,1)S(1)} %fusion.46), channel_id=1, replica_groups=mesh['dp'=4,'tensor'=8] {'tensor'}, dimensions={0}, use_global_device_ids=true | all-gather | bytes 124416 | tf_op jit(solution)/shard_map/all_gather | solution.py:51
  81.0 4.4 fusion.3
  95.5 4.2 fusion.61
  105.6 4.3 fusion.91
  109.8 222.4 %all-reduce.8.cloned.1.call-done = f32[8,192,1152]{2,1,0:T(8,128)} async-done(((f32[8,192,1152]{2,1,0:T(8,128)}), f32[8,192,1152]{2,1,0:T(8,128)}) %all-reduce.8.cloned.1.call-update) | async-done | bytes 7077904 | tf_op jit(solution)/shard_map/psum | solution.py:91
  332.2 6.9 fusion.85
  344.4 5.8 fusion.81
  350.2 4.8 convolution_convert_fusion
  355.7 5.1 fusion.92
  360.8 6.3 multiply_reduce_fusion.3
  367.2 5.4 multiply_reduce_fusion
  372.6 120.3 %all-reduce.10.cloned.1.call-done = bf16[8,192,1152]{2,1,0:T(8,128)(2,1)} async-done(((bf16[8,192,1152]{2,1,0:T(8,128)(2,1)}), bf16[8,192,1152]{2,1,0:T(8,128)(2,1)}) %all-reduce.10.cloned.1.call-update) | async-done | bytes 3538960 | tf_op jit(solution)/shard_map/psum | solution.py:106
  493.0 17.5 %broadcast_add_fusion = (f32[8,192,1152]{2,1,0:T(8,128)}, bf16[8,192,1152]{2,1,0:T(8,128)(2,1)}, f32[8,192,1152]{2,1,0:T(8,128)}, f32[8,192,1152]{2,1,0:T(8,128)}) fusion(f32[8,192]{1,0:T(8,128)S(1)} %negate_multiply_fusion.1, f32[8,192]{1,0:T(8,128)S(1)} %multiply_multiply_fusion.4, f32[8,192,1152]{2,1,0:T(8,128)} %copy-done.1, ...), kind=kLoop, calls=%fused_computation.41 | loop fusion | flops 26542080 | bytes 46115328 | tf_op jit(solution)/shard_map/transpose(jvp())/add_any | solution.py:10
  512.2 6.2 convolution_convert_fusion.2
  518.4 4.2 convolution_convert_fusion.3
  524.2 217.0 %all-reduce.12.cloned.1.call-done = f32[8,192,1152]{2,1,0:T(8,128)} async-done(((f32[8,192,1152]{2,1,0:T(8,128)}), f32[8,192,1152]{2,1,0:T(8,128)}) %all-reduce.12.cloned.1.call-update) | async-done | bytes 7077904 | tf_op jit(solution)/shard_map/psum | solution.py:130
  741.2 7.3 fusion.83
  771.3 8.2 multiply_reduce_fusion.2
  780.8 3.8 convolution_convert_fusion.4
  784.6 5.8 fusion.1
  791.1 9.1 multiply_reduce_fusion.1
  809.1 4.8 fusion.19
  813.9 73.5 %reduce-scatter.4.cloned.1.call-done = f32[864,8]{1,0:T(8,128)} async-done(((f32[6912,8]{1,0:T(8,128)}), f32[864,8]{1,0:T(8,128)}) %reduce-scatter.4.cloned.1.call-update) | async-done | bytes 27664
  887.4 4.0 convolution_convert_fusion.1
  892.8 11.2 all-reduce
  907.9 36.0 %psum.109 = f32[8,1152]{1,0:T(8,128)S(1)} all-reduce(f32[8,1152]{1,0:T(8,128)S(1)} %fusion.58), channel_id=1, replica_groups=mesh['dp'=4,'tensor'=8] {'tensor'}, use_global_device_ids=true, to_apply=%region_23.24 | all-reduce | flops 9216 | bytes 73728 | tf_op jit(solution)/shard_map/psum | solution.py:211
  944.6 61.4 %all-reduce.16.cloned.1.call-done = (bf16[1152,864]{0,1:T(8,128)(2,1)}, bf16[3,1152,144]{1,2,0:T(8,128)(2,1)}, bf16[144,1152]{1,0:T(8,128)(2,1)}, bf16[1152,576]{0,1:T(8,128)(2,1)}, bf16[576,1152]{1,0:T(8,128)(2,1)}) async-done(((bf16[1152,864]{0,1:T(8,128)(2,1)}, bf16[3,1152,144]{1,2,0:T(8,128)(2,1)}, bf16[144,1152]{1,0:T(8,128)(2,1)}, bf16[1152,576]{0,1:T(8,128)(2,1)}, bf16[576,1152]{1,0:T(8,128)(2,1)}), ...) | async-done | bytes 5971984 | tf_op jit(solution)/shard_map/psum | solution.py:215
  1008.0 3.9 convert_element_type.225
  1016.6 224.6 %all-reduce.14.cloned.1.call-done = f32[8,192,1152]{2,1,0:T(8,128)} async-done(((f32[8,192,1152]{2,1,0:T(8,128)}), f32[8,192,1152]{2,1,0:T(8,128)}) %all-reduce.14.cloned.1.call-update) | async-done | bytes 7077904 | tf_op jit(solution)/shard_map/psum | solution.py:187
  1241.2 7.4 multiply_convert_fusion
  1248.7 11.3 scatter_custom_fusion
  (201 shorter events, 80.2 us)
Async XLA Ops:
  7.2 40.4 %copy-start = (bf16[1152,864]{0,1:T(8,128)(2,1)S(1)}, bf16[1152,864]{0,1:T(8,128)(2,1)}, u32[]{:S(2)}) copy-start(bf16[1152,864]{0,1:T(8,128)(2,1)} %param.19) | copy-start | bytes 5971972
  7.2 325.1 %all-reduce.8.cloned.1.call-start = ((), (), s32[]{:S(2)}) async-start(), calls=%async_computation.1 | async-start | bytes 14155776 | tf_op jit(solution)/shard_map/psum | solution.py:91
  8.9 85.2 %copy-start.28 = (pred[8,192]{1,0:T(8,128)(4,1)}, pred[8,192]{1,0:T(8,128)(4,1)S(1)}, u32[]{:S(2)}) copy-start(pred[8,192]{1,0:T(8,128)(4,1)S(1)} %get-tuple-element.56) | copy-start | bytes 4612
  9.0 71.9 %copy-start.27 = (pred[1536]{0:T(1024)(128)(4,1)}, pred[1536]{0:T(1024)(128)(4,1)S(1)}, u32[]{:S(2)}) copy-start(pred[1536]{0:T(1024)(128)(4,1)S(1)} %broadcast_in_dim.78) | copy-start | bytes 4612
  41.3 6.2 copy-start.34
  41.3 6.2 copy-start.35
  41.3 6.2 copy-start.24
  81.0 4.5 copy-start.20
  90.2 2.9 copy-start.12
  99.7 393.3 %all-reduce.10.cloned.1.call-start = ((), (), s32[]{:S(2)}) async-start(), calls=%async_computation.2 | async-start | bytes 7077888 | tf_op jit(solution)/shard_map/psum | solution.py:106
  100.4 5.2 copy-start.41
  339.1 2.8 copy-start.1
  343.6 6.6 copy-start.10
  344.4 5.8 copy-start.42
  350.2 4.8 copy-start.46
  355.1 386.1 %all-reduce.12.cloned.1.call-start = ((), (), s32[]{:S(2)}) async-start(), calls=%async_computation.3 | async-start | bytes 14155776 | tf_op jit(solution)/shard_map/psum | solution.py:130
  360.8 6.4 copy-start.3
  510.5 376.9 %reduce-scatter.4.cloned.1.call-start = ((), (), s32[]{:S(2)}) async-start(), calls=%async_computation.5 | async-start | bytes 3981312
  512.1 6.2 copy-start.9
  512.2 6.2 copy-start.47
  524.1 226.1 %copy-start.23 = (bf16[144,1152]{1,0:T(8,128)(2,1)S(1)}, bf16[144,1152]{1,0:T(8,128)(2,1)}, u32[]{:S(2)}) copy-start(bf16[144,1152]{1,0:T(8,128)(2,1)} %param.23) | copy-start | bytes 995332
  748.5 5.4 copy-start.29
  752.3 5.2 copy-start.17
  753.8 3.6 copy-start.5
  759.1 2.7 copy-start.13
  780.1 4.4 copy-start.26
  780.8 3.8 copy-start.2
  808.8 197.2 %all-reduce.16.cloned.1.call-start = ((), (), s32[]{:S(2)}) async-start(), calls=%async_computation.6 | async-start | bytes 11943936 | tf_op jit(solution)/shard_map/psum | solution.py:215
  891.4 349.8 %all-reduce.14.cloned.1.call-start = ((), (), s32[]{:S(2)}) async-start(), calls=%async_computation.4 | async-start | bytes 14155776 | tf_op jit(solution)/shard_map/psum | solution.py:187
  1006.0 5.8 copy-start.21
  1008.0 5.3 copy-start.19
  1011.8 3.1 copy-start.18
  (22 other events, 29.8 us)
Sparse Core Ops, SparseCore 0:
  99.8 232.3 all-reduce.7
  355.2 137.7 all-reduce.9
  510.6 230.5 all-reduce.11
  808.9 78.4 reduce-scatter.3
  891.5 114.4 all-reduce.15
  1009.7 231.5 all-reduce.13
where the time goes:
time: 1280 us; the launch traced here: 1270 us
  waiting for transfers between devices  920 us (72%)
  other arithmetic  105 us (8%)
  blocking collectives  79.6 us (6%)
  local copies, waits for them, and re-layouts  74.9 us (6%)
  matrix products  71.1 us (6%)
  between operations  15.2 us (1%)
    psum x1, waiting for transfers between devices, on_device(): grad_tokens = (grad_middle + lax.psum(first_term, 'tensor')) * live_rows  225 us
    psum x1, waiting for transfers between devices, on_device(): branch = lax.psum(branch_part, 'tensor') + out_bias_float  222 us
    psum x1, waiting for transfers between devices, on_device(): grad_middle = grad_out + lax.psum(second_term, 'tensor')  217 us
    psum x1, waiting for transfers between devices, on_device(): lax.psum(mlp_part.astype(jnp.bfloat16), 'tensor').astype(jnp.float32)  120 us
    unnamed x7, waiting for transfers between devices  74 us
    psum x1, waiting for transfers between devices, on_device(): lax.psum(mod_weight_grad.astype(jnp.bfloat16), 'dp').astype(jnp.float32)  61.4 us
    psum x1, blocking collectives, on_device(): grad_silu = lax.psum(silu_term, 'tensor')  36 us
    all_gather x1, blocking collectives, on_device(): lax.all_gather(mod_local, 'tensor', axis=1, tiled=True).astype(jnp.float32)  32.4 us
  transfers between devices with their start and end apart: 6, of which 6 were waited for; matrix products, arithmetic and copies ran while one was open for 5% of the time, Pallas kernels for 0%

commit v1 on v0

v1 whole, which is shorter than its diff:
```python
import functools

import jax
import jax.numpy as jnp
from jax import lax
from jax.experimental import pallas as pl
from jax.experimental.pallas import tpu as pltpu
from jax.sharding import PartitionSpec as P

HD = 72
MESH = pl.DeviceIdType.MESH
F32 = jnp.float32
LOW = jnp.bfloat16
DMA = pltpu.SemaphoreType.DMA
VM = pl.BlockSpec(memory_space=pltpu.VMEM)
SM = pl.BlockSpec(memory_space=pltpu.SMEM)
HB = pl.BlockSpec(memory_space=pl.ANY)
PAIR = 2
GELU_ROOT = 0.7978845608028654
GELU_CUBE = 0.044715


def remote(source, target, send_sem, recv_sem, device):
    return pltpu.make_async_remote_copy(
        src_ref=source,
        dst_ref=target,
        send_sem=send_sem,
        recv_sem=recv_sem,
        device_id={"tensor": device},
        device_id_type=MESH,
    )


def place(depth):
    me = lax.axis_index("tensor")
    return me, me // PAIR, me % PAIR


def meet(peers):
    barrier = pltpu.get_barrier_semaphore()
    for peer in peers:
        pl.semaphore_signal(barrier, inc=1, device_id={"tensor": peer}, device_id_type=MESH)
    pl.semaphore_wait(barrier, len(peers))


def column_peers(depth):
    me, up, side = place(depth)
    return [((up + step) % depth) * PAIR + side for step in range(1, depth)]


def dot(left, right):
    return jnp.dot(left, right, preferred_element_type=F32)


def dot_nt(left, right):
    return lax.dot_general(left, right, (((1,), (1,)), ((), ())), preferred_element_type=F32)


def dot_tn(left, right):
    return lax.dot_general(left, right, (((0,), (0,)), ((), ())), preferred_element_type=F32)


def norm_parts(rows):
    width = rows.shape[-1]
    centred = rows - jnp.sum(rows, axis=-1, keepdims=True) * (1.0 / width)
    spread = lax.rsqrt(jnp.sum(centred * centred, axis=-1, keepdims=True) * (1.0 / width) + 1e-06)
    return centred * spread, spread


def norm_back(norm, spread, grad):
    width = norm.shape[-1]
    mean_grad = jnp.sum(grad, axis=-1, keepdims=True) * (1.0 / width)
    mean_both = jnp.sum(grad * norm, axis=-1, keepdims=True) * (1.0 / width)
    return (grad - mean_grad - norm * mean_both) * spread


class Gather:
    def __init__(self, buffer, share, depth, pieces, send, recv):
        self.buffer, self.share, self.depth, self.pieces = buffer, share, depth, pieces
        self.send, self.recv = send, recv
        self.me, self.up, self.side = place(depth)

    def piece(self, index, part):
        rows = self.share // self.pieces
        return self.buffer.at[pl.ds(pl.multiple_of(index * self.share + part * rows, rows), rows), :]

    def copy(self, way, step, part):
        source = self.up - (step - 1) * (1 - 2 * way)
        target = self.up + 1 - 2 * way
        view = self.piece(source, part)
        return remote(
            view,
            view,
            self.send.at[way, step, part],
            self.recv.at[way, step, part],
            target * PAIR + self.side,
        )

    def may_send(self, way, step):
        if way == 0:
            return (self.up + 1 < self.depth) & (self.up >= step - 1)
        return (self.up >= 1) & (self.up + step - 1 < self.depth)

    def open(self):
        for part in range(self.pieces):
            for way in range(2):

                @pl.when(self.may_send(way, 1))
                def _():
                    self.copy(way, 1, part).start()

    def arrival(self, turn):
        below = self.up
        above = self.depth - 1 - self.up
        both = jnp.minimum(below, above)
        mixed = turn <= 2 * both
        way = jnp.where(mixed, (turn + 1) % 2, jnp.where(below > above, 0, 1))
        step = jnp.where(mixed, (turn + 1) // 2, turn - both)
        step = jnp.where(turn == 0, 0, step)
        return way, step, self.up - step * (1 - 2 * way)

    def take(self, turn):
        way, step, source = self.arrival(turn)
        ahead = jnp.where(way == 0, self.up + 1 < self.depth, self.up >= 1)

        @pl.when(turn > 0)
        def _():
            for part in range(self.pieces):
                view = self.piece(source, part)
                remote(
                    view,
                    view,
                    self.send.at[way, step, part],
                    self.recv.at[way, step, part],
                    self.me,
                ).wait_recv()

                @pl.when(ahead)
                def _():
                    self.copy(way, step + 1, part).start()

        return source

    def close(self):
        for way in range(2):
            for step in range(1, self.depth):

                @pl.when(self.may_send(way, step))
                def _():
                    for part in range(self.pieces):
                        self.copy(way, step, part).wait_send()


class Reduce:
    def __init__(self, terms, landing, share, depth, pieces, send, recv):
        self.terms, self.landing, self.share, self.depth, self.pieces = (
            terms,
            landing,
            share,
            depth,
            pieces,
        )
        self.send, self.recv = send, recv
        self.me, self.up, self.side = place(depth)
        self.rows = share // pieces

    def span(self, index, part):
        return pl.ds(pl.multiple_of(index * self.share + part * self.rows, self.rows), self.rows)

    def copy(self, way, owner, part):
        target = self.up + 1 - 2 * way
        slot = owner if way == 0 else jnp.where(owner == target, self.depth, owner)
        return remote(
            self.terms.at[self.span(owner, part), :],
            self.landing.at[self.span(slot, part), :],
            self.send.at[owner, part],
            self.recv.at[slot, part],
            target * PAIR + self.side,
        )

    def landed(self, slot, part):
        view = self.landing.at[self.span(slot, part), :]
        remote(view, view, self.send.at[0, part], self.recv.at[slot, part], self.me).wait_recv()

    def ready(self, owner):
        @pl.when((self.up == 0) & (owner > 0))
        def _():
            for part in range(self.pieces):
                self.copy(0, owner, part).start()

        @pl.when((self.up == self.depth - 1) & (owner < self.depth - 1))
        def _():
            for part in range(self.pieces):
                self.copy(1, owner, part).start()

    def add(self, target, target_start, term_start, starts):
        def body(index, carry):
            offset = index * 16
            value = self.terms[
                pl.ds(pl.multiple_of(term_start + offset, 16), 16), :
            ].astype(F32)
            for start in starts:
                value = value + self.landing[
                    pl.ds(pl.multiple_of(start + offset, 16), 16), :
                ].astype(F32)
            target[pl.ds(pl.multiple_of(target_start + offset, 16), 16), :] = value.astype(
                target.dtype
            )
            return carry

        lax.fori_loop(0, self.rows // 16, body, 0)

    def relay(self, owner, part):
        start = owner * self.share + part * self.rows

        def pass_on(way):
            self.landed(owner, part)
            self.add(self.terms, start, start, [start])
            self.copy(way, owner, part).start()

        @pl.when((owner > self.up) & (self.up > 0))
        def _():
            pass_on(0)

        @pl.when((owner < self.up) & (self.up < self.depth - 1))
        def _():
            pass_on(1)

    def finish(self, total):
        start = self.up * self.share
        end = self.depth * self.share
        for part in range(self.pieces):
            skip = part * self.rows

            @pl.when(self.up == 0)
            def _():
                self.landed(self.depth, part)
                self.add(total, skip, start + skip, [end + skip])

            @pl.when(self.up == self.depth - 1)
            def _():
                self.landed(self.up, part)
                self.add(total, skip, start + skip, [start + skip])

            @pl.when((self.up > 0) & (self.up < self.depth - 1))
            def _():
                self.landed(self.up, part)
                self.landed(self.depth, part)
                self.add(total, skip, start + skip, [start + skip, end + skip])

    def close(self):
        for owner in range(self.depth):

            @pl.when(self.up != owner)
            def _():
                for part in range(self.pieces):
                    remote(
                        self.terms.at[self.span(owner, part), :],
                        self.landing.at[self.span(owner, part), :],
                        self.send.at[owner, part],
                        self.recv.at[owner, part],
                        self.me,
                    ).wait_send()


def far_first(turn, group, count):
    low = group < count // 2
    own = jnp.where(low, count - 1 - group, group)
    moved = jnp.where(turn >= own, turn + 1, turn)
    other = jnp.where(low, count - 1 - moved, moved)
    return jnp.where(turn == count - 1, group, other)


def near_first(turn, up, depth):
    low = up < depth // 2
    ahead = jnp.where(turn < depth - 1 - up, up + 1 + turn, depth - 2 - turn)
    behind = jnp.where(turn < up, up - 1 - turn, turn + 1)
    return jnp.where(low, ahead, behind)


def modulation_kernel(devices, cond, weight, bias, gathered, silu_out, mine, send, recv):
    me = lax.axis_index("tensor")
    meet([(me + step) % devices for step in range(1, devices)])
    value = cond[...].astype(F32)
    silu = (value / (1.0 + jnp.exp(-value))).astype(LOW)
    silu_out[...] = silu
    local = (dot(silu, weight[...]) + bias[...].astype(F32)).astype(LOW)
    mine[...] = local
    gathered[me] = local
    copies = []
    for step in range(1, devices):
        copy = remote(
            mine, gathered.at[me], send.at[step], recv.at[step], (me + step) % devices
        )
        copy.start()
        copies.append(copy)
    for step in range(1, devices):
        source = (me + devices - step) % devices
        remote(mine, gathered.at[source], send.at[step], recv.at[step], me).wait_recv()
    for copy in copies:
        copy.wait_send()


def modulation(cond, weight, bias, devices):
    images, width = cond.shape
    columns = weight.shape[1]
    return pl.pallas_call(
        functools.partial(modulation_kernel, devices),
        out_shape=(
            jax.ShapeDtypeStruct((devices, images, columns), LOW),
            jax.ShapeDtypeStruct((images, width), LOW),
        ),
        in_specs=[VM] * 3,
        out_specs=(VM, VM),
        scratch_shapes=[pltpu.VMEM((images, columns), LOW), DMA((devices,)), DMA((devices,))],
        compiler_params=pltpu.CompilerParams(collective_id=0, has_side_effects=True),
        name="modulation",
    )(cond, weight, bias)


def head_mask(head, width):
    lane = lax.broadcasted_iota(jnp.int32, (1, width), 1)
    return (lane >= head * HD) & (lane < (head + 1) * HD)


def softmax_rows(queries, keys, key_live, scale):
    scores = dot_nt(queries, keys) * scale
    scores = jnp.where(key_live, scores, -1e30)
    top = jnp.max(scores, axis=-1, keepdims=True)
    raised = jnp.exp(scores - top)
    return raised / jnp.sum(raised, axis=-1, keepdims=True)


def attend_kernel(
    sizes,
    count,
    index,
    patches,
    mod,
    qkv_own,
    qkv_other,
    qv_own,
    qv_other,
    out_own,
    out_other,
    out_bias,
    normed_out,
    proj_out,
    attended_out,
    tokens_own,
    mid_out,
    branch_out,
    normed_two_out,
    patch_rows,
    tokens,
    terms,
    landing,
    total,
    patch_sem,
    send,
    recv,
):
    depth, images, kept, share, pieces = sizes
    me, up, side = place(depth)
    width = patches.shape[2]
    local = out_own.shape[0]
    scale = HD ** (-0.5)
    fold = depth // images
    first = side * images

    def fetch(image):
        return pltpu.make_async_copy(
            patches.at[first + image], patch_rows.at[image], patch_sem.at[image]
        )

    for turn in range(images):
        fetch(far_first(turn, up // fold, images)).start()
    meet(column_peers(depth))
    reduce = Reduce(terms, landing, share, depth, pieces, send, recv)

    def one(turn, carry):
        image = far_first(turn, up // fold, images)
        fetch(image).wait()
        rows = pl.ds(pl.multiple_of(image * kept, kept), kept)
        kept_count = count[first + image]
        spots = lax.broadcasted_iota(jnp.int32, (patches.shape[1], kept), 0)
        slots = lax.broadcasted_iota(jnp.int32, (patches.shape[1], kept), 1)
        pick = jnp.where((spots == index[first + image]) & (slots < kept_count), 1.0, 0.0)
        rows_float = dot_tn(pick.astype(LOW), patch_rows[image])
        tokens[rows, :] = rows_float.astype(LOW)
        norm, _ = norm_parts(rows_float)
        normed = (
            norm * (1.0 + mod[first + image, 1:2, :]) + mod[first + image, 0:1, :]
        ).astype(LOW)
        normed_out[rows, :] = normed
        key_live = lax.broadcasted_iota(jnp.int32, (1, kept), 1) < kept_count
        branch = None
        for shard, (qkv, qv, out) in enumerate(
            ((qkv_own, qv_own, out_own), (qkv_other, qv_other, out_other))
        ):
            queries = (dot(normed, qkv[0]) + qv[0:1, :].astype(F32)).astype(LOW)
            keys = dot(normed, qkv[1]).astype(LOW)
            values = (dot(normed, qkv[2]) + qv[1:2, :].astype(F32)).astype(LOW)
            proj_out[shard, 0, rows, :] = queries
            proj_out[shard, 1, rows, :] = keys
            proj_out[shard, 2, rows, :] = values
            attended = jnp.zeros((kept, local), F32)
            for head in range(local // HD):
                mask = head_mask(head, local)
                weights = softmax_rows(
                    jnp.where(mask, queries, 0.0).astype(LOW), keys, key_live, scale
                )
                attended = attended + dot(
                    weights.astype(LOW), jnp.where(mask, values, 0.0).astype(LOW)
                )
            attended = attended.astype(LOW)
            attended_out[shard, rows, :] = attended
            part = dot(attended, out[...])
            branch = part if branch is None else branch + part
        terms[rows, :] = branch.astype(LOW)
        for part in range(fold):
            reduce.ready(image * fold + part)
        return carry

    lax.fori_loop(0, images, one, 0)
    for turn in range(depth - 1):
        for part in range(pieces):
            reduce.relay(far_first(turn, up, depth), part)
    reduce.finish(total)
    image = first + (up * share) // kept
    own = tokens[pl.ds(pl.multiple_of(up * share, share), share), :]
    tokens_own[...] = own
    branch = total[...] + out_bias[...].astype(F32)
    branch_out[...] = branch
    mid = own.astype(F32) + mod[image, 2:3, :] * branch
    mid_out[...] = mid
    norm, _ = norm_parts(mid)
    normed_two_out[...] = (norm * (1.0 + mod[image, 4:5, :]) + mod[image, 3:4, :]).astype(LOW)
    reduce.close()


def attend(sizes, args):
    depth, images, kept, share, pieces = sizes
    width = args[2].shape[2]
    spots = args[2].shape[1]
    local = args[8].shape[0]
    rows = images * kept
    return pl.pallas_call(
        functools.partial(attend_kernel, sizes),
        out_shape=(
            jax.ShapeDtypeStruct((rows, width), LOW),
            jax.ShapeDtypeStruct((PAIR, 3, rows, local), LOW),
            jax.ShapeDtypeStruct((PAIR, rows, local), LOW),
            jax.ShapeDtypeStruct((share, width), LOW),
            jax.ShapeDtypeStruct((share, width), F32),
            jax.ShapeDtypeStruct((share, width), F32),
            jax.ShapeDtypeStruct((share, width), LOW),
        ),
        in_specs=[SM, VM, HB] + [VM] * 8,
        out_specs=(VM,) * 7,
        scratch_shapes=[
            pltpu.VMEM((images, spots, width), LOW),
            pltpu.VMEM((rows, width), LOW),
            pltpu.VMEM((rows, width), LOW),
            pltpu.VMEM((rows + share, width), LOW),
            pltpu.VMEM((share, width), F32),
            DMA((images,)),
            DMA((depth, pieces)),
            DMA((depth + 1, pieces)),
        ],
        compiler_params=pltpu.CompilerParams(
            collective_id=1, has_side_effects=True, vmem_limit_bytes=60 << 20
        ),
        name="attend",
    )(*args)


def feed_kernel(
    sizes,
    count,
    normed_own,
    cotangent,
    mod,
    up_own,
    up_other,
    up_bias_own,
    up_bias_other,
    down_own,
    down_other,
    down_bias,
    mid,
    branch,
    up_grad,
    down_grad,
    up_bias_grad,
    down_bias_grad,
    block_own,
    grad_mid_out,
    grad_branch_out,
    sums_out,
    normed,
    cot,
    hidden,
    grad_pre,
    grad_mlp,
    terms,
    landing,
    mlp_terms,
    mlp_landing,
    total,
    mlp_total,
    cot_sem,
    own_sem,
    gather_send,
    gather_recv,
    send,
    recv,
    mlp_send,
    mlp_recv,
):
    depth, images, kept, share, pieces = sizes
    me, up, side = place(depth)
    width = normed_own.shape[1]
    fold = depth // images
    first = side * images
    own_rows = pl.ds(pl.multiple_of(up * share, share), share)
    own_copy = pltpu.make_async_copy(normed_own, normed.at[own_rows, :], own_sem)
    own_copy.start()

    def fetch(image):
        return pltpu.make_async_copy(
            cotangent.at[first + image],
            cot.at[pl.ds(pl.multiple_of(image * kept, kept), kept), :],
            cot_sem.at[image],
        )

    for image in range(images):
        fetch(image).start()
    meet(column_peers(depth))
    own_copy.wait()
    gather = Gather(normed, share, depth, pieces, gather_send, gather_recv)
    reduce = Reduce(terms, landing, share, depth, pieces, send, recv)
    mlp_reduce = Reduce(mlp_terms, mlp_landing, share, depth, pieces, mlp_send, mlp_recv)
    gather.open()
    up_bias_grad[...] = jnp.zeros_like(up_bias_grad)
    down_bias_grad[...] = jnp.zeros_like(down_bias_grad)

    def one(image):
        fetch(image).wait()
        rows = pl.ds(pl.multiple_of(image * kept, kept), kept)
        live = lax.broadcasted_iota(jnp.int32, (kept, 1), 0) < count[first + image]
        grad = jnp.where(live, cot[rows, :].astype(F32), 0.0)
        grad = (mod[first + image, 5:6, :] * grad).astype(LOW)
        grad_mlp[rows, :] = grad
        down_bias_grad[...] += jnp.sum(grad.astype(F32), axis=0, keepdims=True)
        source = normed[rows, :]
        mlp = None
        back = None
        for shard, (weight_up, bias, weight_down) in enumerate(
            ((up_own, up_bias_own, down_own), (up_other, up_bias_other, down_other))
        ):
            pre = dot(source, weight_up[...]) + bias[...].astype(F32)
            square = pre * pre
            bent = jnp.tanh(GELU_ROOT * pre * (1.0 + GELU_CUBE * square))
            half = 0.5 * (1.0 + bent)
            low_hidden = (pre * half).astype(LOW)
            hidden[shard, rows, :] = low_hidden
            slope = half + 0.5 * pre * (1.0 - bent * bent) * (
                GELU_ROOT * (1.0 + 3.0 * GELU_CUBE * square)
            )
            low_grad = (slope * dot_nt(grad, weight_down[...])).astype(LOW)
            grad_pre[shard, rows, :] = low_grad
            up_bias_grad[shard : shard + 1, :] += jnp.sum(
                low_grad.astype(F32), axis=0, keepdims=True
            )
            mlp_part = dot(low_hidden, weight_down[...])
            back_part = dot_nt(low_grad, weight_up[...])
            mlp = mlp_part if mlp is None else mlp + mlp_part
            back = back_part if back is None else back + back_part
        terms[rows, :] = back.astype(LOW)
        mlp_terms[rows, :] = mlp.astype(LOW)
        for part in range(fold):
            reduce.ready(image * fold + part)

    if fold == 1:

        def turn_of(turn, carry):
            one(gather.take(turn))
            return carry

        lax.fori_loop(0, depth, turn_of, 0)
    else:

        def take_of(turn, carry):
            gather.take(turn)
            return carry

        def image_of(image, carry):
            one(image)
            return carry

        lax.fori_loop(0, depth, take_of, 0)
        lax.fori_loop(0, images, image_of, 0)
    for owner in range(depth):
        mlp_reduce.ready(owner)
    for turn in range(depth - 1):
        for part in range(pieces):
            reduce.relay(near_first(turn, up, depth), part)
    for shard in range(PAIR):

        def tile(step, carry):
            columns = pl.ds(pl.multiple_of(step * 128, 128), 128)
            up_grad[shard, columns, :] = dot_tn(
                normed[:, columns], grad_pre[shard]
            ).astype(LOW)
            down_grad[shard, :, columns] = dot_tn(hidden[shard], grad_mlp[:, columns]).astype(LOW)
            return carry

        lax.fori_loop(0, width // 128, tile, 0)
    reduce.finish(total)
    for turn in range(depth - 1):
        for part in range(pieces):
            mlp_reduce.relay(far_first(turn, up, depth), part)
    image = first + (up * share) // kept
    place_in = (up * share) % kept
    live = (
        lax.broadcasted_iota(jnp.int32, (share, 1), 0) + place_in < count[image]
    )
    grad_out = jnp.where(live, cot[own_rows, :].astype(F32), 0.0)
    norm, spread = norm_parts(mid[...])
    back = total[...]
    grad_mid = grad_out + norm_back(norm, spread, back * (1.0 + mod[image, 4:5, :]))
    grad_mid_out[...] = grad_mid
    grad_branch_out[...] = (mod[image, 2:3, :] * grad_mid).astype(LOW)
    sums_out[0:1, :] = jnp.sum(grad_mid * branch[...], axis=0, keepdims=True)
    sums_out[1:2, :] = jnp.sum(back, axis=0, keepdims=True)
    sums_out[2:3, :] = jnp.sum(back * norm, axis=0, keepdims=True)
    mlp_reduce.finish(mlp_total)
    mlp = mlp_total[...] + down_bias[...].astype(F32)
    sums_out[3:4, :] = jnp.sum(grad_out * mlp, axis=0, keepdims=True)
    block_own[...] = jnp.where(live, mid[...] + mod[image, 5:6, :] * mlp, 0.0).astype(LOW)
    gather.close()
    reduce.close()
    mlp_reduce.close()


def feed(sizes, args):
    depth, images, kept, share, pieces = sizes
    width = args[1].shape[1]
    units = args[4].shape[1]
    rows = images * kept
    shape = jax.ShapeDtypeStruct
    return pl.pallas_call(
        functools.partial(feed_kernel, sizes),
        out_shape=(
            shape((PAIR, width, units), LOW),
            shape((PAIR, units, width), LOW),
            shape((PAIR, units), F32),
            shape((1, width), F32),
            shape((share, width), LOW),
            shape((share, width), F32),
            shape((share, width), LOW),
            shape((4, width), F32),
        ),
        in_specs=[SM, VM, HB] + [VM] * 10,
        out_specs=(VM,) * 8,
        scratch_shapes=[
            pltpu.VMEM((rows, width), LOW),
            pltpu.VMEM((rows, width), LOW),
            pltpu.VMEM((PAIR, rows, units), LOW),
            pltpu.VMEM((PAIR, rows, units), LOW),
            pltpu.VMEM((rows, width), LOW),
            pltpu.VMEM((rows, width), LOW),
            pltpu.VMEM((rows + share, width), LOW),
            pltpu.VMEM((rows, width), LOW),
            pltpu.VMEM((rows + share, width), LOW),
            pltpu.VMEM((share, width), F32),
            pltpu.VMEM((share, width), F32),
            DMA((images,)),
            DMA,
            DMA((2, depth, pieces)),
            DMA((2, depth, pieces)),
            DMA((depth, pieces)),
            DMA((depth + 1, pieces)),
            DMA((depth, pieces)),
            DMA((depth + 1, pieces)),
        ],
        compiler_params=pltpu.CompilerParams(
            collective_id=2, has_side_effects=True, vmem_limit_bytes=60 << 20
        ),
        name="feed",
    )(*args)


def attend_back_kernel(
    sizes,
    count,
    grad_own,
    normed,
    proj,
    attended,
    qkv_own,
    qkv_other,
    out_own,
    out_other,
    mod,
    tokens_own,
    grad_mid,
    qkv_grad,
    out_grad,
    qv_grad,
    out_bias_grad,
    grad_tokens,
    sums_out,
    grads,
    grad_proj,
    terms,
    landing,
    total,
    own_sem,
    gather_send,
    gather_recv,
    send,
    recv,
):
    depth, images, kept, share, pieces = sizes
    me, up, side = place(depth)
    width = grad_own.shape[1]
    local = out_own.shape[0]
    scale = HD ** (-0.5)
    fold = depth // images
    first = side * images
    own_rows = pl.ds(pl.multiple_of(up * share, share), share)
    own_copy = pltpu.make_async_copy(grad_own, grads.at[own_rows, :], own_sem)
    own_copy.start()
    meet(column_peers(depth))
    own_copy.wait()
    gather = Gather(grads, share, depth, pieces, gather_send, gather_recv)
    reduce = Reduce(terms, landing, share, depth, pieces, send, recv)
    gather.open()
    qv_grad[...] = jnp.zeros_like(qv_grad)
    out_bias_grad[...] = jnp.zeros_like(out_bias_grad)

    def one(image):
        rows = pl.ds(pl.multiple_of(image * kept, kept), kept)
        key_live = lax.broadcasted_iota(jnp.int32, (1, kept), 1) < count[first + image]
        grad = grads[rows, :]
        out_bias_grad[...] += jnp.sum(grad.astype(F32), axis=0, keepdims=True)
        back = None
        for shard, (qkv, out) in enumerate(((qkv_own, out_own), (qkv_other, out_other))):
            grad_att = dot_nt(grad, out[...]).astype(LOW)
            queries = proj[shard, 0, rows, :]
            keys = proj[shard, 1, rows, :]
            values = proj[shard, 2, rows, :]
            grad_q = jnp.zeros((kept, local), F32)
            grad_k = jnp.zeros((kept, local), F32)
            grad_v = jnp.zeros((kept, local), F32)
            for head in range(local // HD):
                mask = head_mask(head, local)
                head_q = jnp.where(mask, queries, 0.0).astype(LOW)
                head_grad = jnp.where(mask, grad_att, 0.0).astype(LOW)
                weights = softmax_rows(head_q, keys, key_live, scale)
                grad_weights = dot_nt(head_grad, values)
                inner = jnp.sum(weights * grad_weights, axis=-1, keepdims=True)
                grad_scores = (weights * (grad_weights - inner)).astype(LOW)
                grad_v = grad_v + dot_tn(weights.astype(LOW), head_grad)
                grad_q = grad_q + dot(grad_scores, jnp.where(mask, keys, 0.0).astype(LOW))
                grad_k = grad_k + dot_tn(grad_scores, head_q)
            for member, value in enumerate((grad_q * scale, grad_k * scale, grad_v)):
                low = value.astype(LOW)
                grad_proj[shard, member, rows, :] = low
                part = dot_nt(low, qkv[member])
                back = part if back is None else back + part
                if member != 1:
                    row = 2 * shard + member // 2
                    qv_grad[row : row + 1, :] += jnp.sum(low.astype(F32), axis=0, keepdims=True)
        terms[rows, :] = back.astype(LOW)
        for part in range(fold):
            reduce.ready(image * fold + part)

    if fold == 1:

        def turn_of(turn, carry):
            one(gather.take(turn))
            return carry

        lax.fori_loop(0, depth, turn_of, 0)
    else:

        def take_of(turn, carry):
            gather.take(turn)
            return carry

        def image_of(image, carry):
            one(image)
            return carry

        lax.fori_loop(0, depth, take_of, 0)
        lax.fori_loop(0, images, image_of, 0)
    for turn in range(depth - 1):
        for part in range(pieces):
            reduce.relay(near_first(turn, up, depth), part)
    for shard in range(PAIR):

        def tile(step, carry):
            columns = pl.ds(pl.multiple_of(step * 128, 128), 128)
            source = normed[:, columns]
            for member in range(3):
                qkv_grad[shard, member, columns, :] = dot_tn(
                    source, grad_proj[shard, member]
                ).astype(LOW)
            out_grad[shard, :, columns] = dot_tn(attended[shard], grads[:, columns]).astype(LOW)
            return carry

        lax.fori_loop(0, width // 128, tile, 0)
    reduce.finish(total)
    image = first + (up * share) // kept
    live = (
        lax.broadcasted_iota(jnp.int32, (share, 1), 0) + (up * share) % kept < count[image]
    )
    norm, spread = norm_parts(tokens_own[...].astype(F32))
    back = total[...]
    grad = grad_mid[...] + norm_back(norm, spread, back * (1.0 + mod[image, 1:2, :]))
    grad_tokens[...] = jnp.where(live, grad, 0.0).astype(LOW)
    sums_out[0:1, :] = jnp.sum(back, axis=0, keepdims=True)
    sums_out[1:2, :] = jnp.sum(back * norm, axis=0, keepdims=True)
    gather.close()
    reduce.close()


def attend_back(sizes, args):
    depth, images, kept, share, pieces = sizes
    width = args[1].shape[1]
    local = args[7].shape[0]
    rows = images * kept
    shape = jax.ShapeDtypeStruct
    return pl.pallas_call(
        functools.partial(attend_back_kernel, sizes),
        out_shape=(
            shape((PAIR, 3, width, local), LOW),
            shape((PAIR, local, width), LOW),
            shape((2 * PAIR, local), F32),
            shape((1, width), F32),
            shape((share, width), LOW),
            shape((2, width), F32),
        ),
        in_specs=[SM] + [VM] * 11,
        out_specs=(VM,) * 6,
        scratch_shapes=[
            pltpu.VMEM((rows, width), LOW),
            pltpu.VMEM((PAIR, 3, rows, local), LOW),
            pltpu.VMEM((rows, width), LOW),
            pltpu.VMEM((rows + share, width), LOW),
            pltpu.VMEM((share, width), F32),
            DMA,
            DMA((2, depth, pieces)),
            DMA((2, depth, pieces)),
            DMA((depth, pieces)),
            DMA((depth + 1, pieces)),
        ],
        compiler_params=pltpu.CompilerParams(
            collective_id=3, has_side_effects=True, vmem_limit_bytes=60 << 20
        ),
        name="attend_back",
    )(*args)


def spread_kernel(sizes, own, whole, own_sem, send, recv, side_send, side_recv):
    depth, share, pieces = sizes
    me, up, side = place(depth)
    half = depth * share
    rows = share // pieces

    def column(index):
        return side * half + index * share

    own_copy = pltpu.make_async_copy(
        own, whole.at[pl.ds(pl.multiple_of(column(up), share), share), :], own_sem
    )
    own_copy.start()
    meet(column_peers(depth) + [up * PAIR + 1 - side])
    own_copy.wait()
    here = whole.at[pl.ds(pl.multiple_of(side * half, share), half), :]
    gather = Gather(here, share, depth, pieces, send, recv)

    def across(index, part):
        view = whole.at[pl.ds(pl.multiple_of(column(index) + part * rows, rows), rows), :]
        return remote(
            view,
            view,
            side_send.at[index, part],
            side_recv.at[index, part],
            up * PAIR + 1 - side,
        )

    gather.open()
    for part in range(pieces):
        across(up, part).start()
    for turn in range(1, depth):
        source = gather.take(turn)
        for part in range(pieces):
            across(source, part).start()
    gather.close()
    for index in range(depth):
        for part in range(pieces):
            start = (1 - side) * half + index * share + part * rows
            view = whole.at[pl.ds(pl.multiple_of(start, rows), rows), :]
            remote(
                view, view, side_send.at[index, part], side_recv.at[index, part], me
            ).wait_recv()
            across(index, part).wait_send()


def spread(own, sizes, ident):
    depth, share, pieces = sizes
    width = own.shape[1]
    return pl.pallas_call(
        functools.partial(spread_kernel, sizes),
        out_shape=jax.ShapeDtypeStruct((PAIR * depth * share, width), own.dtype),
        in_specs=[VM],
        out_specs=VM,
        scratch_shapes=[
            DMA,
            DMA((2, depth, pieces)),
            DMA((2, depth, pieces)),
            DMA((depth, pieces)),
            DMA((depth, pieces)),
        ],
        compiler_params=pltpu.CompilerParams(collective_id=ident, has_side_effects=True),
        name="spread",
    )(own)


def scatter_kernel(index, grads, out):
    spots, kept = out.shape[0], grads.shape[0]
    rows = lax.broadcasted_iota(jnp.int32, (spots, kept), 0)
    pick = jnp.where(rows == index[...], 1.0, 0.0).astype(LOW)
    out[...] = dot(pick, grads[...]).astype(LOW)


def scatter(index, grads, spots):
    images, kept, width = grads.shape
    return pl.pallas_call(
        scatter_kernel,
        out_shape=jax.ShapeDtypeStruct((images, spots, width), LOW),
        grid=(images,),
        in_specs=[
            pl.BlockSpec((None, 1, kept), lambda image: (image, 0, 0)),
            pl.BlockSpec((None, kept, width), lambda image: (image, 0, 0)),
        ],
        out_specs=pl.BlockSpec((None, spots, width), lambda image: (image, 0, 0)),
        name="scatter",
    )(index, grads)


def on_device(
    patches,
    conditioning,
    keep_count,
    keep_index,
    mod_weight,
    mod_bias,
    qkv_weight,
    qv_bias,
    out_weight,
    out_bias,
    up_weight,
    up_bias,
    down_weight,
    down_bias,
    out_cotangent,
):
    devices = lax.axis_size("tensor")
    depth = devices // PAIR
    all_images, kept = keep_index.shape
    width = patches.shape[2]
    images = all_images // PAIR
    share = images * kept // depth
    pieces = 4 if share % 64 == 0 else 2
    sizes = (depth, images, kept, share, pieces)
    me = lax.axis_index("tensor")
    swap = [(member, member ^ 1) for member in range(devices)]

    def other(value):
        return lax.ppermute(value, "tensor", swap)

    qkv_other, qv_other, out_other = other(qkv_weight), other(qv_bias), other(out_weight)
    up_other, down_other = other(up_weight), other(down_weight)
    up_bias_row = up_bias[None, :]
    up_bias_other = other(up_bias_row)
    gathered, silu_low = modulation(conditioning, mod_weight, mod_bias[None, :], devices)
    mod = (
        gathered.transpose(1, 0, 2).reshape(all_images, 6, width).astype(F32)
    )
    index = keep_index[:, None, :]
    normed_one, proj, attended, tokens_own, mid, branch, normed_two = attend(
        sizes,
        (
            keep_count,
            index,
            patches,
            mod,
            qkv_weight,
            qkv_other,
            qv_bias,
            qv_other,
            out_weight,
            out_other,
            out_bias[None, :],
        ),
    )
    (
        up_grad,
        down_grad,
        up_bias_grad,
        down_bias_grad,
        block_own,
        grad_mid,
        grad_branch,
        sums_two,
    ) = feed(
        sizes,
        (
            keep_count,
            normed_two,
            out_cotangent,
            mod,
            up_weight,
            up_other,
            up_bias_row,
            up_bias_other,
            down_weight,
            down_other,
            down_bias[None, :],
            mid,
            branch,
        ),
    )
    qkv_grad, out_grad, qv_grad, out_bias_grad, grad_tokens, sums_one = attend_back(
        sizes,
        (
            keep_count,
            grad_branch,
            normed_one,
            proj,
            attended,
            qkv_weight,
            qkv_other,
            out_weight,
            out_other,
            mod,
            tokens_own,
            grad_mid,
        ),
    )
    block_out = spread(block_own, (depth, share, pieces), 4).reshape(all_images, kept, width)
    token_grads = spread(grad_tokens, (depth, share, pieces), 5).reshape(all_images, kept, width)
    grad_patches = scatter(index, token_grads, patches.shape[1])

    own_mod = jnp.concatenate(
        [sums_one[0], sums_one[1], sums_two[0], sums_two[1], sums_two[2], sums_two[3]]
    )
    columns = mod_weight.shape[1]
    every_mod = lax.all_gather(own_mod, ("dp", "tensor"))
    mine = lax.dynamic_slice_in_dim(every_mod, me * columns, columns, 1)
    groups = lax.axis_size("dp")
    holder = jnp.arange(devices)
    image_of = (holder % PAIR) * images + (holder // PAIR) * share // kept
    chosen = (image_of[None, :] == jnp.arange(all_images)[:, None]).astype(F32)
    per_image = jnp.einsum(
        "id,gdm->gim",
        chosen,
        mine.reshape(groups, devices, columns),
        precision=lax.Precision.HIGHEST,
    )
    silu_all = lax.all_gather(silu_low, "dp").astype(F32)
    mod_weight_grad = jnp.einsum(
        "gid,gim->dm", silu_all, per_image, precision=lax.Precision.HIGHEST
    )
    mod_bias_grad = jnp.sum(per_image, axis=(0, 1))
    here = lax.dynamic_index_in_dim(per_image, lax.axis_index("dp"), 0, keepdims=False)
    silu_term = jnp.einsum(
        "bm,dm->bd", here, mod_weight.astype(F32), precision=lax.Precision.HIGHEST
    )
    cond_float = conditioning.astype(F32)
    grad_silu = lax.psum(silu_term, "tensor")
    silu_pull = jax.vjp(jax.nn.silu, cond_float)[1]
    grad_conditioning = silu_pull(grad_silu)[0].astype(LOW)

    def total(both):
        pair = both[0].astype(F32) + other(both[1]).astype(F32)
        return lax.psum(pair.astype(LOW), "dp").astype(F32)

    qv_pair = qv_grad.reshape(PAIR, 2, qv_grad.shape[1])
    whole_bias = jnp.concatenate([down_bias_grad, out_bias_grad])
    return (
        block_out,
        grad_patches,
        grad_conditioning,
        mod_weight_grad,
        mod_bias_grad,
        total(qkv_grad),
        total(qv_pair.astype(LOW)),
        total(out_grad),
        total(jnp.stack([out_bias_grad[0], out_bias_grad[0]]).astype(LOW)),
        total(up_grad),
        total(up_bias_grad.astype(LOW)),
        total(down_grad),
        total(jnp.stack([down_bias_grad[0], down_bias_grad[0]]).astype(LOW)),
    )


def solution(mesh):
    placed = (
        P("dp", None, None),
        P("dp", None),
        P("dp"),
        P("dp", None),
        P(None, "tensor"),
        P("tensor"),
        P(None, None, "tensor"),
        P(None, "tensor"),
        P("tensor", None),
        P(),
        P(None, "tensor"),
        P("tensor"),
        P("tensor", None),
        P(),
        P("dp", None, None),
    )
    return jax.shard_map(
        on_device,
        mesh=mesh,
        in_specs=placed,
        out_specs=(
            P("dp", None, None),
            P("dp", None, None),
            P("dp", None),
            P(None, "tensor"),
            P("tensor"),
            P(None, None, "tensor"),
            P(None, "tensor"),
            P("tensor", None),
            P(),
            P(None, "tensor"),
            P("tensor"),
            P("tensor", None),
            P(),
        ),
        check_vma=False,
    )
```

time: 1280 us -> 653 us (0.51)
  waiting for transfers between devices: 920 us -> 57.9 us
  Pallas kernels: 0 us -> 368 us
  other arithmetic: 105 us -> 19.1 us
  matrix products: 71.1 us -> 6.67 us
  blocking collectives: 79.6 us -> 125 us
  local copies, waits for them, and re-layouts: 74.9 us -> 45.3 us
  starting transfers between devices: 1.29 us -> 15.9 us
    psum x5 -> x1, waiting for transfers between devices: 846 us -> 0.01 us  [total(): return lax.psum(pair.astype(LOW), 'dp').astype(F32)]
    pallas_call x0 -> x7, Pallas kernels: none -> 368 us  [the longest x1 93.6 us: feed(): pl.pallas_call(functools.partial(feed_kernel, sizes), out_shape=(shape((P...]
    unnamed x7 -> x1, waiting for transfers between devices: 74 us -> 0.02 us
    dot_general x20 -> x3, matrix products: 69.2 us -> 6.67 us  [the longest x1 3.71 us: on_device(): jnp.einsum('gid,gim->dm', silu_all, per_image, precision=lax.Precision.HI...]
    ppermute x0 -> x14, waiting for transfers between devices: none -> 57.8 us  [other(): return lax.ppermute(value, 'tensor', swap)]
    reduce_sum x14 -> x0, other arithmetic: 55.5 us -> none  [the longest x3 15.4 us: layer_norm(): centred = inputs - jnp.mean(inputs, axis=-1, keepdims=True)]
    all_gather x1 -> x2, blocking collectives: 32.4 us -> 81.3 us  [the longest x1 75.8 us: on_device(): every_mod = lax.all_gather(own_mod, ('dp', 'tensor'))]
    gather x3 -> x0, local copies, waits for them, and re-layouts: 32.3 us -> none  [on_device(): jnp.take_along_axis(patches, keep_index[:, :, None], axis=1)]
  transfers between devices with their start and end apart: 6 -> 15, of which waited for: 6 -> 2; matrix products, arithmetic and copies ran while one was open for 5% -> 9% of each run, Pallas kernels for 0% -> 32%
where the time goes in v1:
time: 653 us; the launch traced here: 652 us
  Pallas kernels  368 us (56%)
  blocking collectives  125 us (19%)
  waiting for transfers between devices  57.9 us (9%)
  local copies, waits for them, and re-layouts  45.3 us (7%)
  other arithmetic  19.1 us (3%)
  starting transfers between devices  15.9 us (2%)
  between operations  14.4 us (2%)
  matrix products  6.67 us (1%)
    pallas_call x1, Pallas kernels, feed(): pl.pallas_call(functools.partial(feed_kernel, sizes), out_shape=(shape((P...  93.6 us
    pallas_call x2, Pallas kernels, spread(): pl.pallas_call(functools.partial(spread_kernel, sizes), out_shape=jax.Sha...  81.2 us
    pallas_call x1, Pallas kernels, modulation(): pl.pallas_call(functools.partial(modulation_kernel, devices), out_shape=(...  76.2 us
    all_gather x1, blocking collectives, on_device(): every_mod = lax.all_gather(own_mod, ('dp', 'tensor'))  75.8 us
    pallas_call x1, Pallas kernels, attend_back(): pl.pallas_call(functools.partial(attend_back_kernel, sizes), out_shape=(s...  65.4 us
    ppermute x14, waiting for transfers between devices, other(): return lax.ppermute(value, 'tensor', swap)  57.8 us
    pallas_call x1, Pallas kernels, attend(): pl.pallas_call(functools.partial(attend_kernel, sizes), out_shape=(jax.Sh...  43.9 us
    psum x1, blocking collectives, on_device(): grad_silu = lax.psum(silu_term, 'tensor')  33.5 us
  transfers between devices with their start and end apart: 15, of which 2 were waited for; matrix products, arithmetic and copies ran while one was open for 9% of the time, Pallas kernels for 32%

profile of v1, /device:TPU:0, one launch (start us, length us, event | category | flops | bytes accessed | tf_op | source)
XLA Modules:
  0.0 651.9 jit_solution(4575991630963952443)
XLA Ops:
  7.2 3.0 collective-permute-start.3
  10.3 1.9 collective-permute-start
  13.1 1.9 collective-permute-start.2
  15.0 2.6 copy.50.up_own
  19.9 2.4 copy.46.weight
  22.3 76.2 %modulation.1 = (bf16[8,8,864]{2,1,0:T(8,128)(2,1)}, bf16[8,1152]{1,0:T(8,128)(2,1)}) custom-call(bf16[8,1152]{1,0:T(8,128)(2,1)} %cond.1, bf16[1152,864]{1,0:T(8,128)(2,1)} %copy.46.weight, bf16[1,864]{1,0:T(2,128)(2,1)} %broadcast_in_dim.18.bias), custom_call_target="tpu_custom_call" | custom-call | tf_op jit(solution)/shard_map/modulation/pallas_call | solution.py:307
  98.6 5.5 all-gather.1
  110.1 2.6 copy.49.qkv_other
  114.0 43.9 %attend.1 = (bf16[768,1152]{1,0:T(8,128)(2,1)}, bf16[2,3,768,144]{3,2,1,0:T(8,128)(2,1)}, bf16[2,768,144]{2,1,0:T(8,128)(2,1)}, bf16[192,1152]{1,0:T(8,128)(2,1)...) custom-call(s32[8]{0:T(128)} %count.5, s32[8,1,192]{2,1,0:T(1,128)} %broadcast_in_dim.17.index, ...), custom_call_target="tpu_custom_call" | custom-call | tf_op jit(solution)/shard_map/attend/pallas_call | solution.py:448
  157.9 2.6 copy.51.up_other
  161.1 93.6 %feed.1 = (bf16[2,1152,576]{2,1,0:T(8,128)(2,1)}, bf16[2,576,1152]{2,1,0:T(8,128)(2,1)}, f32[2,576]{1,0:T(2,128)}, f32[1,1152]{1,0:T(1,128)}, bf16[192,1152]{1,0...) custom-call(s32[8]{0:T(128)} %count.5, ...), custom_call_target="tpu_custom_call" | custom-call | tf_op jit(solution)/shard_map/feed/pallas_call | solution.py:653
  254.7 65.4 %attend_back.1 = (bf16[2,3,1152,144]{3,2,1,0:T(8,128)(2,1)}, bf16[2,144,1152]{2,1,0:T(8,128)(2,1)}, f32[4,144]{1,0:T(4,128)}, f32[1,1152]{1,0:T(1,128)}, bf16[192,1152]{1,0:T(8,128)(2,1)}, /*index=5*/f32[2,1152]{1,0:T(2,128)}) custom-call(s32[8]{0:T(128)} %count.5, bf16[192,1152]{1,0:T(8,128)(2,1)} %get-tuple-element.41.grad_own, ...), custom_call_target="tpu_custom_call" | custom-call | tf_op jit(solution)/shard_map/attend_back/pallas_call | solution.py:837
  325.8 75.8 %all-gather.2 = f32[32,1,6912]{2,1,0:T(1,128)} all-gather(f32[1,1,6912]{2,1,0:T(1,128)S(1)} %reshape.102), channel_id=2, replica_groups=mesh['dp'=4,'tensor'=8] {'dp','tensor'}, dimensions={0}, use_global_device_ids=true | all-gather | bytes 912384 | tf_op jit(solution)/shard_map/all_gather | solution.py:1064
  401.6 2.5 slice_bitcast_fusion.2
  406.2 2.6 copy.54
  415.3 2.1 fusion.26
  419.3 38.5 %collective-permute-done.6 = bf16[3,1152,144]{1,2,0:T(8,128)(2,1)} collective-permute-done((bf16[3,1152,144]{1,2,0:T(8,128)(2,1)}, bf16[3,1152,144]{1,2,0:T(8,128)(2,1)}, u32[]{:S(2)}, u32[]{:S(2)}) %collective-permute-start.6) | collective-permute-done | bytes 995360 | tf_op jit(solution)/shard_map/ppermute | solution.py:985
  457.7 2.6 copy.55
  460.3 3.6 fusion
  464.0 19.4 %collective-permute-done.10 = bf16[1152,576]{0,1:T(8,128)(2,1)} collective-permute-done((bf16[1152,576]{0,1:T(8,128)(2,1)}, bf16[1152,576]{0,1:T(8,128)(2,1)}, u32[]{:S(2)}, u32[]{:S(2)}) %collective-permute-start.10) | collective-permute-done | bytes 1327136 | tf_op jit(solution)/shard_map/ppermute | solution.py:985
  483.3 2.1 copy.57
  485.4 3.1 fusion.1
  488.5 2.7 fusion.2
  492.9 33.5 %psum.63 = f32[8,1152]{1,0:T(8,128)S(1)} all-reduce(f32[8,1152]{1,0:T(8,128)S(1)} %fusion.15), channel_id=1, replica_groups=mesh['dp'=4,'tensor'=8] {'tensor'}, use_global_device_ids=true, to_apply=%region_0.1 | all-reduce | flops 9216 | bytes 73728 | tf_op jit(solution)/shard_map/psum | solution.py:1086
  526.5 3.7 convolution_bitcast_fusion
  530.9 2.0 collective-permute-start.13
  532.9 39.8 %spread.3 = bf16[1536,1152]{1,0:T(8,128)(2,1)} custom-call(bf16[192,1152]{1,0:T(8,128)(2,1)} %get-tuple-element.47.own), custom_call_target="tpu_custom_call" | custom-call | tf_op jit(solution)/shard_map/spread/pallas_call | solution.py:917
  572.7 7.6 %scatter.1 = bf16[8,256,1152]{2,1,0:T(8,128)(2,1)} custom-call(s32[8,1,192]{2,1,0:T(1,128)} %broadcast_in_dim.17.index, bf16[8,192,1152]{2,1,0:T(8,128)(2,1)} %bitcast.49), custom_call_target="tpu_custom_call" | custom-call | tf_op jit(solution)/shard_map/scatter/pallas_call | solution.py:943
  580.3 41.4 %spread.2 = bf16[1536,1152]{1,0:T(8,128)(2,1)} custom-call(bf16[192,1152]{1,0:T(8,128)(2,1)} %get-tuple-element.40.own), custom_call_target="tpu_custom_call" | custom-call | tf_op jit(solution)/shard_map/spread/pallas_call | solution.py:917
  621.8 10.1 %all-reduce = (bf16[2,144]{1,0:T(2,128)(2,1)S(1)}, bf16[1152]{0:T(1024)(128)(2,1)S(1)}, bf16[576]{0:T(1024)(128)(2,1)S(1)}, bf16[1152]{0:T(1024)(128)(2,1)S(1)}) all-reduce(bf16[2,144]{1,0:T(2,128)(2,1)S(1)} %add_convert_fusion.3, bf16[1152]{0:T(1024)(128)(2,1)S(1)} %add_convert_fusion.1, ...), channel_id=1, replica_groups=mesh['dp'=4,'tensor'=8] {'dp'}, use_global_device_ids=true, to_apply=%region_3.4 | all-reduce | flops 3168 | bytes 12672 | tf_op jit(solution)/shard_map/psum | solution.py:1092
  634.3 2.9 copy.58
  638.2 2.1 copy.59
  (117 shorter events, 37.8 us)
Async XLA Ops:
  7.2 10.4 %copy-start.7 = (bf16[3,1152,144]{1,2,0:T(8,128)(2,1)S(1)}, bf16[3,1152,144]{1,2,0:T(8,128)(2,1)}, u32[]{:S(2)}) copy-start(bf16[3,1152,144]{1,2,0:T(8,128)(2,1)} %param.21) | copy-start | bytes 2985988
  7.2 627.2 %all-reduce.4.cloned.1.call-start = ((), (), s32[]{:S(2)}) async-start(), calls=%async_computation | async-start | bytes 9805824 | tf_op jit(solution)/shard_map/psum | solution.py:1092
  7.2 150.7 %collective-permute-start.3 = (bf16[1152,576]{0,1:T(8,128)(2,1)}, bf16[1152,576]{0,1:T(8,128)(2,1)}, u32[]{:S(2)}, u32[]{:S(2)}) collective-permute-start(bf16[1152,576]{0,1:T(8,128)(2,1)} %param.25), channel_id=1, source_target_pairs={{0,1},{1,0},{2,3},{3,2},{4,5},{5,4},{6,7},{7,6},{8,9},{9,8},{10,11... | collective-permute-start | bytes 3981320 | tf_op jit(solution)/shard_map/ppermute | solution.py:985
  10.3 150.3 %collective-permute-start.5 = (bf16[576,1152]{1,0:T(8,128)(2,1)}, bf16[576,1152]{1,0:T(8,128)(2,1)}, u32[]{:S(2)}, u32[]{:S(2)}) collective-permute-start(bf16[576,1152]{1,0:T(8,128)(2,1)} %down_own.1), channel_id=1, source_target_pairs={{0,1},{1,0},{2,3},{3,2},{4,5},{5,4},{6,7},{7,6},{8,9},{9,8},{10,11... | collective-permute-start | bytes 3981320 | tf_op jit(solution)/shard_map/ppermute | solution.py:985
  10.3 95.1 %collective-permute-start = (bf16[3,1152,144]{1,2,0:T(8,128)(2,1)}, bf16[3,1152,144]{1,2,0:T(8,128)(2,1)}, u32[]{:S(2)}, u32[]{:S(2)}) collective-permute-start(bf16[3,1152,144]{1,2,0:T(8,128)(2,1)} %param.21), channel_id=1, source_target_pairs={{0,1},{1,0},{2,3},{3,2},{4,5},{5,4},{6,7},{7,6},{8,9},{9,8},{10,11... | collective-permute-start | bytes 2985992 | tf_op jit(solution)/shard_map/ppermute | solution.py:985
  13.0 6.4 copy-start.12
  13.0 147.6 %collective-permute-start.4 = (bf16[1,576]{1,0:T(2,128)(2,1)S(1)}, bf16[1,576]{1,0:T(2,128)(2,1)S(1)}, u32[]{:S(2)}, u32[]{:S(2)}) collective-permute-start(bf16[1,576]{1,0:T(2,128)(2,1)S(1)} %broadcast_in_dim.20.up_bias_own), channel_id=1, source_target_pairs={{0,1},{1,0},{2,3},{3,2},{4,5},{5,4},{6,7},{7,6},{8,9},{9,8},{10,11... | collective-permute-start | bytes 3464 | tf_op jit(solution)/shard_map/ppermute | solution.py:985
  13.1 99.7 %collective-permute-start.2 = (bf16[144,1152]{1,0:T(8,128)(2,1)}, bf16[144,1152]{1,0:T(8,128)(2,1)S(1)}, u32[]{:S(2)}, u32[]{:S(2)}) collective-permute-start(bf16[144,1152]{1,0:T(8,128)(2,1)} %out_own.3), channel_id=1, source_target_pairs={{0,1},{1,0},{2,3},{3,2},{4,5},{5,4},{6,7},{7,6},{8,9},{9,8},{10,11... | collective-permute-start | bytes 995336 | tf_op jit(solution)/shard_map/ppermute | solution.py:985
  17.6 2.3 copy-start.1
  22.3 83.2 %copy-start.21 = (bf16[2,144]{1,0:T(2,128)(2,1)S(1)}, bf16[2,144]{1,0:T(2,128)(2,1)}, u32[]{:S(2)}) copy-start(bf16[2,144]{1,0:T(2,128)(2,1)} %qv_own.1) | copy-start | bytes 1732
  22.3 85.0 %copy-start.17 = (bf16[1152]{0:T(1024)(128)(2,1)S(1)}, bf16[1152]{0:T(1024)(128)(2,1)}, u32[]{:S(2)}) copy-start(bf16[1152]{0:T(1024)(128)(2,1)} %param.24) | copy-start | bytes 6916
  22.3 85.6 %copy-start.18 = (bf16[1152]{0:T(1024)(128)(2,1)S(1)}, bf16[1152]{0:T(1024)(128)(2,1)}, u32[]{:S(2)}) copy-start(bf16[1152]{0:T(1024)(128)(2,1)} %param.28) | copy-start | bytes 6916
  22.3 86.2 %copy-start.13 = (s32[8,192]{1,0:T(8,128)S(1)}, s32[8,192]{1,0:T(8,128)}, u32[]{:S(2)}) copy-start(s32[8,192]{1,0:T(8,128)} %param.18) | copy-start | bytes 18436
  105.5 7.2 %collective-permute-start.1 = (bf16[2,144]{1,0:T(2,128)(2,1)S(1)}, bf16[2,144]{1,0:T(2,128)(2,1)S(1)}, u32[]{:S(2)}, u32[]{:S(2)}) collective-permute-start(bf16[2,144]{1,0:T(2,128)(2,1)S(1)} %copy-done.21), channel_id=1, source_target_pairs={{0,1},{1,0},{2,3},{3,2},{4,5},{5,4},{6,7},{7,6},{8,9},{9,8},{10,11... | collective-permute-start | bytes 1736 | tf_op jit(solution)/shard_map/ppermute | solution.py:985
  254.7 66.1 %copy-start.14 = (f32[2,576]{1,0:T(2,128)S(1)}, f32[2,576]{1,0:T(2,128)}, u32[]{:S(2)}) copy-start(f32[2,576]{1,0:T(2,128)} %get-tuple-element.56) | copy-start | bytes 13828
  254.7 67.5 %copy-start.11 = (f32[4,1152]{1,0:T(4,128)S(1)}, f32[4,1152]{1,0:T(4,128)}, u32[]{:S(2)}) copy-start(f32[4,1152]{1,0:T(4,128)} %get-tuple-element.49) | copy-start | bytes 55300
  320.8 300.9 %collective-permute-start.7 = (bf16[2,144]{1,0:T(2,128)(2,1)S(1)}, bf16[2,144]{1,0:T(2,128)(2,1)S(1)}, u32[]{:S(2)}, u32[]{:S(2)}) collective-permute-start(bf16[2,144]{1,0:T(2,128)(2,1)S(1)} %slice.85), channel_id=1, source_target_pairs={{0,1},{1,0},{2,3},{3,2},{4,5},{5,4},{6,7},{7,6},{8,9},{9,8},{10,11... | collective-permute-start | bytes 1736 | tf_op jit(solution)/shard_map/ppermute | solution.py:985
  322.4 82.5 %copy-start.2 = (bf16[2,3,1152,144]{3,2,1,0:T(8,128)(2,1)S(1)}, bf16[2,3,1152,144]{3,2,1,0:T(8,128)(2,1)}, u32[]{:S(2)}) copy-start(bf16[2,3,1152,144]{3,2,1,0:T(8,128)(2,1)} %get-tuple-element.51) | copy-start | bytes 5971972
  324.3 93.1 %collective-permute-start.8 = (bf16[144,1152]{1,0:T(8,128)(2,1)}, bf16[144,1152]{1,0:T(8,128)(2,1)}, u32[]{:S(2)}, u32[]{:S(2)}) collective-permute-start(bf16[144,1152]{1,0:T(8,128)(2,1)} %slice_bitcast_fusion.3), channel_id=1, source_target_pairs={{0,1},{1,0},{2,3},{3,2},{4,5},{5,4},{6,7},{7,6},{8,9},{9,8},{10,11... | collective-permute-start | bytes 995336 | tf_op jit(solution)/shard_map/ppermute | solution.py:985
  404.1 84.4 %collective-permute-start.12 = (bf16[576,1152]{1,0:T(8,128)(2,1)}, bf16[576,1152]{1,0:T(8,128)(2,1)}, u32[]{:S(2)}, u32[]{:S(2)}) collective-permute-start(bf16[576,1152]{1,0:T(8,128)(2,1)} %slice_bitcast_fusion.2), channel_id=1, source_target_pairs={{0,1},{1,0},{2,3},{3,2},{4,5},{5,4},{6,7},{7,6},{8,9},{9,8},{10,11... | collective-permute-start | bytes 3981320 | tf_op jit(solution)/shard_map/ppermute | solution.py:985
  408.8 48.9 %collective-permute-start.6 = (bf16[3,1152,144]{1,2,0:T(8,128)(2,1)}, bf16[3,1152,144]{1,2,0:T(8,128)(2,1)}, u32[]{:S(2)}, u32[]{:S(2)}) collective-permute-start(bf16[3,1152,144]{1,2,0:T(8,128)(2,1)} %copy.54), channel_id=1, source_target_pairs={{0,1},{1,0},{2,3},{3,2},{4,5},{5,4},{6,7},{7,6},{8,9},{9,8},{10,11... | collective-permute-start | bytes 2985992 | tf_op jit(solution)/shard_map/ppermute | solution.py:985
  413.3 70.0 %collective-permute-start.10 = (bf16[1152,576]{0,1:T(8,128)(2,1)}, bf16[1152,576]{0,1:T(8,128)(2,1)}, u32[]{:S(2)}, u32[]{:S(2)}) collective-permute-start(bf16[1152,576]{0,1:T(8,128)(2,1)} %copy.56), channel_id=1, source_target_pairs={{0,1},{1,0},{2,3},{3,2},{4,5},{5,4},{6,7},{7,6},{8,9},{9,8},{10,11... | collective-permute-start | bytes 3981320 | tf_op jit(solution)/shard_map/ppermute | solution.py:985
  485.4 3.1 copy-start.3
  491.2 35.3 %copy-start.16 = (f32[1,1152]{1,0:T(1,128)S(1)}, f32[1,1152]{1,0:T(1,128)}, u32[]{:S(2)}) copy-start(f32[1,1152]{1,0:T(1,128)} %get-tuple-element.54) | copy-start | bytes 13828
  491.2 35.3 %copy-start.15 = (f32[1,1152]{1,0:T(1,128)S(1)}, f32[1,1152]{1,0:T(1,128)}, u32[]{:S(2)}) copy-start(f32[1,1152]{1,0:T(1,128)} %get-tuple-element.58) | copy-start | bytes 13828
  526.5 3.7 copy-start.10
  530.9 90.9 %collective-permute-start.11 = (bf16[576]{0:T(1024)(128)(2,1)S(1)}, bf16[576]{0:T(1024)(128)(2,1)S(1)}, u32[]{:S(2)}, u32[]{:S(2)}) collective-permute-start(bf16[576]{0:T(1024)(128)(2,1)S(1)} %slice_reduce_fusion.6), channel_id=1, source_target_pairs={{0,1},{1,0},{2,3},{3,2},{4,5},{5,4},{6,7},{7,6},{8,9},{9,8},{10,11... | collective-permute-start | bytes 3464 | tf_op jit(solution)/shard_map/ppermute | solution.py:985
  530.9 90.9 %collective-permute-start.13 = (bf16[1152]{0:T(1024)(128)(2,1)S(1)}, bf16[1152]{0:T(1024)(128)(2,1)S(1)}, u32[]{:S(2)}, u32[]{:S(2)}) collective-permute-start(bf16[1152]{0:T(1024)(128)(2,1)S(1)} %convert_reduce_fusion), channel_id=1, source_target_pairs={{0,1},{1,0},{2,3},{3,2},{4,5},{5,4},{6,7},{7,6},{8,9},{9,8},{10,11... | collective-permute-start | bytes 6920 | tf_op jit(solution)/shard_map/ppermute | solution.py:985
  532.9 88.9 %collective-permute-start.9 = (bf16[1152]{0:T(1024)(128)(2,1)S(1)}, bf16[1152]{0:T(1024)(128)(2,1)S(1)}, u32[]{:S(2)}, u32[]{:S(2)}) collective-permute-start(bf16[1152]{0:T(1024)(128)(2,1)S(1)} %convert_reduce_fusion.1), channel_id=1, source_target_pairs={{0,1},{1,0},{2,3},{3,2},{4,5},{5,4},{6,7},{7,6},{8,9},{9,8},{10,11... | collective-permute-start | bytes 6920 | tf_op jit(solution)/shard_map/ppermute | solution.py:985
  634.3 2.9 copy-start.9
  634.3 3.8 copy-start.4
  640.3 3.0 copy-start
  (6 other events, 6.7 us)
Sparse Core Ops, SparseCore 0:
  491.3 94.6 all-reduce.3

commit v2 on v1

--- a/solution.py
+++ b/solution.py
@@ -20,13 +20,14 @@
 GELU_CUBE = 0.044715
 
 
-def remote(source, target, send_sem, recv_sem, device):
+def remote(source, target, send_sem, recv_sem, device, group=None):
+    there = {"tensor": device} if group is None else {"dp": group, "tensor": device}
     return pltpu.make_async_remote_copy(
         src_ref=source,
         dst_ref=target,
         send_sem=send_sem,
         recv_sem=recv_sem,
-        device_id={"tensor": device},
+        device_id=there,
         device_id_type=MESH,
     )
 
@@ -38,14 +39,24 @@
 
 def meet(peers):
     barrier = pltpu.get_barrier_semaphore()
-    for peer in peers:
-        pl.semaphore_signal(barrier, inc=1, device_id={"tensor": peer}, device_id_type=MESH)
+    for group, peer in peers:
+        pl.semaphore_signal(
+            barrier, inc=1, device_id={"dp": group, "tensor": peer}, device_id_type=MESH
+        )
     pl.semaphore_wait(barrier, len(peers))
 
 
 def column_peers(depth):
     me, up, side = place(depth)
-    return [((up + step) % depth) * PAIR + side for step in range(1, depth)]
+    group = lax.axis_index("dp")
+    return [(group, ((up + step) % depth) * PAIR + side) for step in range(1, depth)]
+
+
+def cube_peers(groups):
+    me = lax.axis_index("tensor")
+    group = lax.axis_index("dp")
+    peers = [((group + step) % groups, me) for step in range(1, groups)]
+    return peers + [((group + step) % groups, me + 1 - 2 * (me % PAIR)) for step in range(groups)]
 
 
 def dot(left, right):
@@ -263,6 +274,211 @@
                     ).wait_send()
 
 
+class Fold:
+    def __init__(self, source, scratch, out, groups, split):
+        self.source, self.out, self.groups, self.split = source, out, groups, split
+        self.stage, self.near, self.side_land, self.far, self.low, self.send, self.recv = scratch
+        self.me = lax.axis_index("tensor")
+        self.group = lax.axis_index("dp")
+        self.core = self.group % PAIR
+        self.line = self.group // PAIR
+        self.mate = self.group + 1 - 2 * self.core
+        self.partner = self.me + 1 - 2 * (self.me % PAIR)
+        self.lines = groups // PAIR
+        self.rows = self.stage.shape[1]
+        self.start = self.core * self.rows if split else 0
+
+    @staticmethod
+    def scratch(shape, groups, split):
+        _, rows, width = shape
+        half = rows // 2 if split else rows
+        lines = groups // PAIR
+        return [
+            pltpu.VMEM((PAIR, half, width), LOW),
+            pltpu.VMEM((PAIR, half, width), LOW),
+            pltpu.VMEM((half, width), LOW),
+            pltpu.VMEM((lines, half, width), LOW),
+            pltpu.VMEM((rows, width), LOW),
+            DMA((3 + lines,)),
+            DMA((3 + lines,)),
+        ]
+
+    def each(self, body):
+        step = 48 if self.rows % 48 == 0 else self.rows
+
+        def run(index, carry):
+            body(pl.multiple_of(index * step, step), step)
+            return carry
+
+        lax.fori_loop(0, self.rows // step, run, 0)
+
+    def window(self, start, size):
+        return pl.ds(pl.multiple_of(start, 16) if self.split else start, size)
+
+    def near_copy(self):
+        if self.split:
+            away = self.window((1 - self.core) * self.rows, self.rows)
+            source = self.source.at[:, away, :]
+        else:
+            source = self.source
+        return remote(
+            source, self.near, self.send.at[0], self.recv.at[0], self.me, self.mate
+        )
+
+    def side_copy(self):
+        return remote(
+            self.stage.at[1],
+            self.side_land,
+            self.send.at[1],
+            self.recv.at[1],
+            self.partner,
+            self.group,
+        )
+
+    def far_copy(self, step):
+        line = (self.line + step) % self.lines
+        return remote(
+            self.far.at[self.line],
+            self.far.at[self.line],
+            self.send.at[2 + step],
+            self.recv.at[2 + step],
+            self.me,
+            line * PAIR + self.core,
+        )
+
+    def mate_copy(self, core):
+        view = self.low.at[self.window(core * self.rows, self.rows), :]
+        return remote(view, view, self.send.at[2], self.recv.at[2], self.me, self.mate)
+
+    def one(self):
+        self.near_copy().start()
+
+    def two(self):
+        self.near_copy().wait_recv()
+
+        def add(at, size):
+            for shard in range(PAIR):
+                mine = self.source[shard, self.window(self.start + at, size), :].astype(F32)
+                rows = self.window(at, size)
+                self.stage[shard, rows, :] = (
+                    mine + self.near[shard, rows, :].astype(F32)
+                ).astype(LOW)
+
+        self.each(add)
+        self.side_copy().start()
+
+    def three(self):
+        self.side_copy().wait_recv()
+
+        def add(at, size):
+            rows = self.window(at, size)
+            self.far[self.line, rows, :] = (
+                self.stage[0, rows, :].astype(F32) + self.side_land[rows, :].astype(F32)
+            ).astype(LOW)
+
+        self.each(add)
+        for step in range(1, self.lines):
+            self.far_copy(step).start()
+
+    def four(self):
+        for step in range(1, self.lines):
+            line = (self.line + self.lines - step) % self.lines
+            view = self.far.at[line]
+            remote(
+                view, view, self.send.at[2 + step], self.recv.at[2 + step], self.me, self.mate
+            ).wait_recv()
+
+        def add(at, size):
+            rows = self.window(at, size)
+            value = self.far[0, rows, :].astype(F32)
+            for line in range(1, self.lines):
+                value = value + self.far[line, rows, :].astype(F32)
+            low = value.astype(LOW)
+            spot = self.window(self.start + at, size)
+            self.low[spot, :] = low
+            self.out[spot, :] = low.astype(F32)
+
+        self.each(add)
+        if self.split:
+            self.mate_copy(self.core).start()
+
+    def five(self):
+        if self.split:
+            self.mate_copy(1 - self.core).wait_recv()
+
+            def put(at, size):
+                spot = self.window((1 - self.core) * self.rows + at, size)
+                self.out[spot, :] = self.low[spot, :].astype(F32)
+
+            self.each(put)
+            self.mate_copy(self.core).wait_send()
+        self.near_copy().wait_send()
+        self.side_copy().wait_send()
+        for step in range(1, self.lines):
+            self.far_copy(step).wait_send()
+
+
+class Spread:
+    def __init__(self, whole, share, depth, pieces, scratch):
+        self.whole, self.share, self.depth, self.pieces = whole, share, depth, pieces
+        send, recv, self.side_send, self.side_recv = scratch
+        self.me, self.up, self.side = place(depth)
+        self.half = depth * share
+        here = whole.at[pl.ds(pl.multiple_of(self.side * self.half, share), self.half), :]
+        self.gather = Gather(here, share, depth, pieces, send, recv)
+
+    @staticmethod
+    def scratch(depth, pieces):
+        return [
+            DMA((2, depth, pieces)),
+            DMA((2, depth, pieces)),
+            DMA((depth, pieces)),
+            DMA((depth, pieces)),
+        ]
+
+    def view(self, side, index, part):
+        rows = self.share // self.pieces
+        start = side * self.half + index * self.share + part * rows
+        return self.whole.at[pl.ds(pl.multiple_of(start, rows), rows), :]
+
+    def own(self):
+        start = self.side * self.half + self.up * self.share
+        return self.whole.at[pl.ds(pl.multiple_of(start, self.share), self.share), :]
+
+    def across(self, index, part):
+        view = self.view(self.side, index, part)
+        return remote(
+            view,
+            view,
+            self.side_send.at[index, part],
+            self.side_recv.at[index, part],
+            self.me + 1 - 2 * self.side,
+        )
+
+    def open(self):
+        self.gather.open()
+        for part in range(self.pieces):
+            self.across(self.up, part).start()
+
+    def take(self, turn):
+        source = self.gather.take(turn)
+        for part in range(self.pieces):
+            self.across(source, part).start()
+
+    def crossed(self, index):
+        for part in range(self.pieces):
+            view = self.view(1 - self.side, index, part)
+            remote(
+                view, view, self.side_send.at[index, part], self.side_recv.at[index, part], self.me
+            ).wait_recv()
+
+    def close(self):
+        self.gather.close()
+        for index in range(self.depth):
+            for part in range(self.pieces):
+                self.across(index, part).wait_send()
+
+
 def far_first(turn, group, count):
     low = group < count // 2
     own = jnp.where(low, count - 1 - group, group)
@@ -278,46 +494,6 @@
     return jnp.where(low, ahead, behind)
 
 
-def modulation_kernel(devices, cond, weight, bias, gathered, silu_out, mine, send, recv):
-    me = lax.axis_index("tensor")
-    meet([(me + step) % devices for step in range(1, devices)])
-    value = cond[...].astype(F32)
-    silu = (value / (1.0 + jnp.exp(-value))).astype(LOW)
-    silu_out[...] = silu
-    local = (dot(silu, weight[...]) + bias[...].astype(F32)).astype(LOW)
-    mine[...] = local
-    gathered[me] = local
-    copies = []
-    for step in range(1, devices):
-        copy = remote(
-            mine, gathered.at[me], send.at[step], recv.at[step], (me + step) % devices
-        )
-        copy.start()
-        copies.append(copy)
-    for step in range(1, devices):
-        source = (me + devices - step) % devices
-        remote(mine, gathered.at[source], send.at[step], recv.at[step], me).wait_recv()
-    for copy in copies:
-        copy.wait_send()
-
-
-def modulation(cond, weight, bias, devices):
-    images, width = cond.shape
-    columns = weight.shape[1]
-    return pl.pallas_call(
-        functools.partial(modulation_kernel, devices),
-        out_shape=(
-            jax.ShapeDtypeStruct((devices, images, columns), LOW),
-            jax.ShapeDtypeStruct((images, width), LOW),
-        ),
-        in_specs=[VM] * 3,
-        out_specs=(VM, VM),
-        scratch_shapes=[pltpu.VMEM((images, columns), LOW), DMA((devices,)), DMA((devices,))],
-        compiler_params=pltpu.CompilerParams(collective_id=0, has_side_effects=True),
-        name="modulation",
-    )(cond, weight, bias)
-
-
 def head_mask(head, width):
     lane = lax.broadcasted_iota(jnp.int32, (1, width), 1)
     return (lane >= head * HD) & (lane < (head + 1) * HD)
@@ -331,19 +507,38 @@
     return raised / jnp.sum(raised, axis=-1, keepdims=True)
 
 
+def attend_shard(normed, qkv, qv, proj_out, shard, rows, key_live, scale):
+    local = qkv.shape[2]
+    queries = (dot(normed, qkv[0]) + qv[0:1, :].astype(F32)).astype(LOW)
+    keys = dot(normed, qkv[1]).astype(LOW)
+    values = (dot(normed, qkv[2]) + qv[1:2, :].astype(F32)).astype(LOW)
+    proj_out[shard, 0, rows, :] = queries
+    proj_out[shard, 1, rows, :] = keys
+    proj_out[shard, 2, rows, :] = values
+    attended = jnp.zeros((normed.shape[0], local), F32)
+    for head in range(local // HD):
+        mask = head_mask(head, local)
+        weights = softmax_rows(jnp.where(mask, queries, 0.0).astype(LOW), keys, key_live, scale)
+        attended = attended + dot(weights.astype(LOW), jnp.where(mask, values, 0.0).astype(LOW))
+    return attended.astype(LOW)
+
+
 def attend_kernel(
     sizes,
+    groups,
     count,
     index,
     patches,
-    mod,
+    cond,
+    mod_weight,
+    mod_bias,
     qkv_own,
-    qkv_other,
     qv_own,
-    qv_other,
     out_own,
-    out_other,
     out_bias,
+    up_own,
+    down_own,
+    up_bias_own,
     normed_out,
     proj_out,
     attended_out,
@@ -351,19 +546,41 @@
     mid_out,
     branch_out,
     normed_two_out,
+    mod,
+    silu_all,
+    qkv_other,
+    qv_other,
+    out_other,
+    up_other,
+    down_other,
+    up_bias_other,
     patch_rows,
     tokens,
     terms,
     landing,
     total,
+    mod_mine,
+    mod_gathered,
     patch_sem,
     send,
     recv,
+    mod_send,
+    mod_recv,
+    silu_send,
+    silu_recv,
+    weight_send,
+    weight_recv,
+    mate_send,
+    mate_recv,
 ):
     depth, images, kept, share, pieces = sizes
+    devices = depth * PAIR
     me, up, side = place(depth)
+    group = lax.axis_index("dp")
+    core = group % PAIR
+    mate = group + 1 - 2 * core
+    partner = me + 1 - 2 * side
     width = patches.shape[2]
-    local = out_own.shape[0]
     scale = HD ** (-0.5)
     fold = depth // images
     first = side * images
@@ -375,98 +592,228 @@
 
     for turn in range(images):
         fetch(far_first(turn, up // fold, images)).start()
-    meet(column_peers(depth))
+    meet(
+        [(group, (me + step) % devices) for step in range(1, devices)]
+        + [((group + step) % groups, me) for step in range(1, groups)]
+    )
+    value = cond[...].astype(F32)
+    silu = (value / (1.0 + jnp.exp(-value))).astype(LOW)
+    silu_all[group] = silu
+    local_mod = (dot(silu, mod_weight[...]) + mod_bias[...].astype(F32)).astype(LOW)
+    mod_mine[...] = local_mod
+    mod_gathered[me] = local_mod
+    mod_copies = [
+        remote(
+            mod_mine,
+            mod_gathered.at[me],
+            mod_send.at[step],
+            mod_recv.at[step],
+            (me + step) % devices,
+        )
+        for step in range(1, devices)
+    ]
+    silu_copies = [
+        remote(
+            silu_all.at[group],
+            silu_all.at[group],
+            silu_send.at[step],
+            silu_recv.at[step],
+            me,
+            (group + step) % groups,
+        )
+        for step in range(1, groups)
+    ]
+    for copy in mod_copies + silu_copies:
+        copy.start()
+
+    def part_of(array, which):
+        if len(array.shape) == 3:
+            rows = array.shape[1] // 2
+            return array.at[:, pl.ds(pl.multiple_of(which * rows, 16), rows), :]
+        rows = array.shape[0] // 2
+        return array.at[pl.ds(pl.multiple_of(which * rows, 16), rows), :]
+
+    halved = [(qkv_own, qkv_other), (up_own, up_other), (down_own, down_other)]
+    full = [(qv_own, qv_other), (out_own, out_other), (up_bias_own, up_bias_other)]
+
+    def half_copy(which):
+        source, target = halved[which]
+        return remote(
+            part_of(source, core),
+            part_of(target, core),
+            weight_send.at[which],
+            weight_recv.at[which],
+            partner,
+        )
+
+    def full_copy(which):
+        source, target = full[which]
+        return remote(
+            source,
+            target,
+            weight_send.at[3 + which],
+            weight_recv.at[3 + which],
+            partner,
+        )
+
+    def mate_copy(which, half):
+        view = part_of(halved[which][1], half)
+        return remote(view, view, mate_send.at[which], mate_recv.at[which], me, mate)
+
+    full_copy(0).start()
+    half_copy(0).start()
+    full_copy(1).start()
+    full_copy(2).start()
+    half_copy(1).start()
+    half_copy(2).start()
     reduce = Reduce(terms, landing, share, depth, pieces, send, recv)
 
-    def one(turn, carry):
+    def pick_rows(turn, carry):
         image = far_first(turn, up // fold, images)
         fetch(image).wait()
         rows = pl.ds(pl.multiple_of(image * kept, kept), kept)
-        kept_count = count[first + image]
         spots = lax.broadcasted_iota(jnp.int32, (patches.shape[1], kept), 0)
         slots = lax.broadcasted_iota(jnp.int32, (patches.shape[1], kept), 1)
-        pick = jnp.where((spots == index[first + image]) & (slots < kept_count), 1.0, 0.0)
-        rows_float = dot_tn(pick.astype(LOW), patch_rows[image])
-        tokens[rows, :] = rows_float.astype(LOW)
-        norm, _ = norm_parts(rows_float)
-        normed = (
-            norm * (1.0 + mod[first + image, 1:2, :]) + mod[first + image, 0:1, :]
-        ).astype(LOW)
+        pick = jnp.where(
+            (spots == index[first + image]) & (slots < count[first + image]), 1.0, 0.0
+        )
+        tokens[rows, :] = dot_tn(pick.astype(LOW), patch_rows[image]).astype(LOW)
+        return carry
+
+    lax.fori_loop(0, images, pick_rows, 0)
+    for step in range(1, devices):
+        source = (me + devices - step) % devices
+        remote(
+            mod_mine, mod_gathered.at[source], mod_send.at[step], mod_recv.at[step], me
+        ).wait_recv()
+    mod[...] = jnp.concatenate(
+        [mod_gathered[device].astype(F32) for device in range(devices)], axis=-1
+    )
+
+    def block(image, member):
+        return mod[pl.ds(first + image, 1), member * width : (member + 1) * width]
+
+    def one(turn, carry):
+        image = far_first(turn, up // fold, images)
+        rows = pl.ds(pl.multiple_of(image * kept, kept), kept)
+
+        @pl.when(turn == images - 1)
+        def _():
+            half_copy(0).wait_recv()
+            mate_copy(0, core).start()
+
+        norm, _ = norm_parts(tokens[rows, :].astype(F32))
+        normed = (norm * (1.0 + block(image, 1)) + block(image, 0)).astype(LOW)
         normed_out[rows, :] = normed
-        key_live = lax.broadcasted_iota(jnp.int32, (1, kept), 1) < kept_count
-        branch = None
-        for shard, (qkv, qv, out) in enumerate(
-            ((qkv_own, qv_own, out_own), (qkv_other, qv_other, out_other))
-        ):
-            queries = (dot(normed, qkv[0]) + qv[0:1, :].astype(F32)).astype(LOW)
-            keys = dot(normed, qkv[1]).astype(LOW)
-            values = (dot(normed, qkv[2]) + qv[1:2, :].astype(F32)).astype(LOW)
-            proj_out[shard, 0, rows, :] = queries
-            proj_out[shard, 1, rows, :] = keys
-            proj_out[shard, 2, rows, :] = values
-            attended = jnp.zeros((kept, local), F32)
-            for head in range(local // HD):
-                mask = head_mask(head, local)
-                weights = softmax_rows(
-                    jnp.where(mask, queries, 0.0).astype(LOW), keys, key_live, scale
-                )
-                attended = attended + dot(
-                    weights.astype(LOW), jnp.where(mask, values, 0.0).astype(LOW)
-                )
-            attended = attended.astype(LOW)
-            attended_out[shard, rows, :] = attended
-            part = dot(attended, out[...])
-            branch = part if branch is None else branch + part
+        key_live = lax.broadcasted_iota(jnp.int32, (1, kept), 1) < count[first + image]
+        attended_out[0, rows, :] = attend_shard(
+            normed, qkv_own, qv_own, proj_out, 0, rows, key_live, scale
+        )
+        return carry
+
+    def two(turn, carry):
+        image = far_first(turn, up // fold, images)
+        rows = pl.ds(pl.multiple_of(image * kept, kept), kept)
+        key_live = lax.broadcasted_iota(jnp.int32, (1, kept), 1) < count[first + image]
+        attended = attend_shard(
+            normed_out[rows, :], qkv_other, qv_other, proj_out, 1, rows, key_live, scale
+        )
+        attended_out[1, rows, :] = attended
+        branch = dot(attended_out[0, rows, :], out_own[...]) + dot(attended, out_other[...])
         terms[rows, :] = branch.astype(LOW)
         for part in range(fold):
             reduce.ready(image * fold + part)
         return carry
 
     lax.fori_loop(0, images, one, 0)
+    full_copy(0).wait_recv()
+    full_copy(1).wait_recv()
+    mate_copy(0, 1 - core).wait_recv()
+    lax.fori_loop(0, images, two, 0)
     for turn in range(depth - 1):
         for part in range(pieces):
             reduce.relay(far_first(turn, up, depth), part)
+        if turn == 0:
+            half_copy(1).wait_recv()
+            mate_copy(1, core).start()
+    half_copy(2).wait_recv()
+    mate_copy(2, core).start()
     reduce.finish(total)
-    image = first + (up * share) // kept
+    image = (up * share) // kept
     own = tokens[pl.ds(pl.multiple_of(up * share, share), share), :]
     tokens_own[...] = own
     branch = total[...] + out_bias[...].astype(F32)
     branch_out[...] = branch
-    mid = own.astype(F32) + mod[image, 2:3, :] * branch
+    mid = own.astype(F32) + block(image, 2) * branch
     mid_out[...] = mid
     norm, _ = norm_parts(mid)
-    normed_two_out[...] = (norm * (1.0 + mod[image, 4:5, :]) + mod[image, 3:4, :]).astype(LOW)
+    normed_two_out[...] = (norm * (1.0 + block(image, 4)) + block(image, 3)).astype(LOW)
     reduce.close()
-
-
-def attend(sizes, args):
+    full_copy(2).wait_recv()
+    mate_copy(1, 1 - core).wait_recv()
+    mate_copy(2, 1 - core).wait_recv()
+    for step in range(1, groups):
+        source = (group + groups - step) % groups
+        view = silu_all.at[source]
+        remote(
+            view, view, silu_send.at[step], silu_recv.at[step], me, mate
+        ).wait_recv()
+    for which in range(3):
+        half_copy(which).wait_send()
+        full_copy(which).wait_send()
+        mate_copy(which, core).wait_send()
+    for copy in mod_copies + silu_copies:
+        copy.wait_send()
+
+
+def attend(sizes, groups, args):
     depth, images, kept, share, pieces = sizes
-    width = args[2].shape[2]
-    spots = args[2].shape[1]
-    local = args[8].shape[0]
+    (count, index, patches, cond, mod_weight, mod_bias, qkv, qv, out, out_bias, up, down, up_bias) = args
+    spots, width = patches.shape[1:]
+    local = out.shape[0]
     rows = images * kept
+    shape = jax.ShapeDtypeStruct
+    devices = depth * PAIR
     return pl.pallas_call(
-        functools.partial(attend_kernel, sizes),
+        functools.partial(attend_kernel, sizes, groups),
         out_shape=(
-            jax.ShapeDtypeStruct((rows, width), LOW),
-            jax.ShapeDtypeStruct((PAIR, 3, rows, local), LOW),
-            jax.ShapeDtypeStruct((PAIR, rows, local), LOW),
-            jax.ShapeDtypeStruct((share, width), LOW),
-            jax.ShapeDtypeStruct((share, width), F32),
-            jax.ShapeDtypeStruct((share, width), F32),
-            jax.ShapeDtypeStruct((share, width), LOW),
+            shape((rows, width), LOW),
+            shape((PAIR, 3, rows, local), LOW),
+            shape((PAIR, rows, local), LOW),
+            shape((share, width), LOW),
+            shape((share, width), F32),
+            shape((share, width), F32),
+            shape((share, width), LOW),
+            shape((cond.shape[0], devices * mod_weight.shape[1]), F32),
+            shape((groups,) + cond.shape, LOW),
+            shape(qkv.shape, LOW),
+            shape(qv.shape, LOW),
+            shape(out.shape, LOW),
+            shape(up.shape, LOW),
+            shape(down.shape, LOW),
+            shape(up_bias.shape, LOW),
         ),
-        in_specs=[SM, VM, HB] + [VM] * 8,
-        out_specs=(VM,) * 7,
+        in_specs=[SM, VM, HB] + [VM] * 10,
+        out_specs=(VM,) * 15,
         scratch_shapes=[
             pltpu.VMEM((images, spots, width), LOW),
             pltpu.VMEM((rows, width), LOW),
             pltpu.VMEM((rows, width), LOW),
             pltpu.VMEM((rows + share, width), LOW),
             pltpu.VMEM((share, width), F32),
+            pltpu.VMEM((cond.shape[0], mod_weight.shape[1]), LOW),
+            pltpu.VMEM((devices, cond.shape[0], mod_weight.shape[1]), LOW),
             DMA((images,)),
             DMA((depth, pieces)),
             DMA((depth + 1, pieces)),
+            DMA((devices,)),
+            DMA((devices,)),
+            DMA((groups,)),
+            DMA((groups,)),
+            DMA((6,)),
+            DMA((6,)),
+            DMA((3,)),
+            DMA((3,)),
         ],
         compiler_params=pltpu.CompilerParams(
             collective_id=1, has_side_effects=True, vmem_limit_bytes=60 << 20
@@ -509,6 +856,8 @@
     mlp_landing,
     total,
     mlp_total,
+    up_sums,
+    down_sums,
     cot_sem,
     own_sem,
     gather_send,
@@ -542,17 +891,18 @@
     reduce = Reduce(terms, landing, share, depth, pieces, send, recv)
     mlp_reduce = Reduce(mlp_terms, mlp_landing, share, depth, pieces, mlp_send, mlp_recv)
     gather.open()
-    up_bias_grad[...] = jnp.zeros_like(up_bias_grad)
-    down_bias_grad[...] = jnp.zeros_like(down_bias_grad)
+
+    def block(image, member):
+        return mod[pl.ds(image, 1), member * width : (member + 1) * width]
 
     def one(image):
         fetch(image).wait()
         rows = pl.ds(pl.multiple_of(image * kept, kept), kept)
         live = lax.broadcasted_iota(jnp.int32, (kept, 1), 0) < count[first + image]
         grad = jnp.where(live, cot[rows, :].astype(F32), 0.0)
-        grad = (mod[first + image, 5:6, :] * grad).astype(LOW)
+        grad = (block(first + image, 5) * grad).astype(LOW)
         grad_mlp[rows, :] = grad
-        down_bias_grad[...] += jnp.sum(grad.astype(F32), axis=0, keepdims=True)
+        down_sums[image] = jnp.sum(grad.astype(F32), axis=0, keepdims=True)
         source = normed[rows, :]
         mlp = None
         back = None
@@ -570,9 +920,7 @@
             )
             low_grad = (slope * dot_nt(grad, weight_down[...])).astype(LOW)
             grad_pre[shard, rows, :] = low_grad
-            up_bias_grad[shard : shard + 1, :] += jnp.sum(
-                low_grad.astype(F32), axis=0, keepdims=True
-            )
+            up_sums[shard, image] = jnp.sum(low_grad.astype(F32), axis=0, keepdims=True)
             mlp_part = dot(low_hidden, weight_down[...])
             back_part = dot_nt(low_grad, weight_up[...])
             mlp = mlp_part if mlp is None else mlp + mlp_part
@@ -621,6 +969,9 @@
     for turn in range(depth - 1):
         for part in range(pieces):
             mlp_reduce.relay(far_first(turn, up, depth), part)
+    for shard in range(PAIR):
+        up_bias_grad[shard : shard + 1, :] = sum(up_sums[shard, image] for image in range(images))
+    down_bias_grad[...] = sum(down_sums[image] for image in range(images))
     image = first + (up * share) // kept
     place_in = (up * share) % kept
     live = (
@@ -629,16 +980,16 @@
     grad_out = jnp.where(live, cot[own_rows, :].astype(F32), 0.0)
     norm, spread = norm_parts(mid[...])
     back = total[...]
-    grad_mid = grad_out + norm_back(norm, spread, back * (1.0 + mod[image, 4:5, :]))
+    grad_mid = grad_out + norm_back(norm, spread, back * (1.0 + block(image, 4)))
     grad_mid_out[...] = grad_mid
-    grad_branch_out[...] = (mod[image, 2:3, :] * grad_mid).astype(LOW)
+    grad_branch_out[...] = (block(image, 2) * grad_mid).astype(LOW)
     sums_out[0:1, :] = jnp.sum(grad_mid * branch[...], axis=0, keepdims=True)
     sums_out[1:2, :] = jnp.sum(back, axis=0, keepdims=True)
     sums_out[2:3, :] = jnp.sum(back * norm, axis=0, keepdims=True)
     mlp_reduce.finish(mlp_total)
     mlp = mlp_total[...] + down_bias[...].astype(F32)
     sums_out[3:4, :] = jnp.sum(grad_out * mlp, axis=0, keepdims=True)
-    block_own[...] = jnp.where(live, mid[...] + mod[image, 5:6, :] * mlp, 0.0).astype(LOW)
+    block_own[...] = jnp.where(live, mid[...] + block(image, 5) * mlp, 0.0).astype(LOW)
     gather.close()
     reduce.close()
     mlp_reduce.close()
@@ -676,6 +1027,8 @@
             pltpu.VMEM((rows + share, width), LOW),
             pltpu.VMEM((share, width), F32),
             pltpu.VMEM((share, width), F32),
+            pltpu.VMEM((PAIR, images, 1, units), F32),
+            pltpu.VMEM((images, 1, width), F32),
             DMA((images,)),
             DMA,
             DMA((2, depth, pieces)),
@@ -694,6 +1047,7 @@
 
 def attend_back_kernel(
     sizes,
+    groups,
     count,
     grad_own,
     normed,
@@ -706,22 +1060,31 @@
     mod,
     tokens_own,
     grad_mid,
+    block_own,
+    up_grad,
+    down_grad,
     qkv_grad,
     out_grad,
     qv_grad,
     out_bias_grad,
     grad_tokens,
     sums_out,
+    block_out,
+    up_total,
+    down_total,
     grads,
     grad_proj,
     terms,
     landing,
     total,
+    qv_sums,
+    out_sums,
     own_sem,
     gather_send,
     gather_recv,
     send,
     recv,
+    *rest,
 ):
     depth, images, kept, share, pieces = sizes
     me, up, side = place(depth)
@@ -730,22 +1093,28 @@
     scale = HD ** (-0.5)
     fold = depth // images
     first = side * images
+    up_fold = Fold(up_grad, rest[:7], up_total, groups, True)
+    down_fold = Fold(down_grad, rest[7:14], down_total, groups, True)
+    spread = Spread(block_out, share, depth, pieces, rest[14:18])
     own_rows = pl.ds(pl.multiple_of(up * share, share), share)
-    own_copy = pltpu.make_async_copy(grad_own, grads.at[own_rows, :], own_sem)
+    own_copy = pltpu.make_async_copy(grad_own, grads.at[own_rows, :], own_sem.at[0])
     own_copy.start()
-    meet(column_peers(depth))
+    block_copy = pltpu.make_async_copy(block_own, spread.own(), own_sem.at[1])
+    block_copy.start()
+    meet(column_peers(depth) + cube_peers(groups))
     own_copy.wait()
     gather = Gather(grads, share, depth, pieces, gather_send, gather_recv)
     reduce = Reduce(terms, landing, share, depth, pieces, send, recv)
     gather.open()
-    qv_grad[...] = jnp.zeros_like(qv_grad)
-    out_bias_grad[...] = jnp.zeros_like(out_bias_grad)
+    up_fold.one()
+    down_fold.one()
+    block_copy.wait()
 
     def one(image):
         rows = pl.ds(pl.multiple_of(image * kept, kept), kept)
         key_live = lax.broadcasted_iota(jnp.int32, (1, kept), 1) < count[first + image]
         grad = grads[rows, :]
-        out_bias_grad[...] += jnp.sum(grad.astype(F32), axis=0, keepdims=True)
+        out_sums[image] = jnp.sum(grad.astype(F32), axis=0, keepdims=True)
         back = None
         for shard, (qkv, out) in enumerate(((qkv_own, out_own), (qkv_other, out_other))):
             grad_att = dot_nt(grad, out[...]).astype(LOW)
@@ -773,7 +1142,7 @@
                 back = part if back is None else back + part
                 if member != 1:
                     row = 2 * shard + member // 2
-                    qv_grad[row : row + 1, :] += jnp.sum(low.astype(F32), axis=0, keepdims=True)
+                    qv_sums[row, image] = jnp.sum(low.astype(F32), axis=0, keepdims=True)
         terms[rows, :] = back.astype(LOW)
         for part in range(fold):
             reduce.ready(image * fold + part)
@@ -782,6 +1151,21 @@
 
         def turn_of(turn, carry):
             one(gather.take(turn))
+
+            @pl.when(turn == 0)
+            def _():
+                up_fold.two()
+                down_fold.two()
+                spread.open()
+
+            @pl.when(turn == 2)
+            def _():
+                up_fold.three()
+
+            @pl.when(turn >= 2)
+            def _():
+                spread.take(turn - 1)
+
             return carry
 
         lax.fori_loop(0, depth, turn_of, 0)
@@ -795,162 +1179,391 @@
             one(image)
             return carry
 
+        def spread_of(turn, carry):
+            spread.take(turn)
+            return carry
+
         lax.fori_loop(0, depth, take_of, 0)
+        up_fold.two()
+        down_fold.two()
+        spread.open()
         lax.fori_loop(0, images, image_of, 0)
+        up_fold.three()
+        lax.fori_loop(1, depth - 1, spread_of, 0)
+    down_fold.three()
     for turn in range(depth - 1):
         for part in range(pieces):
             reduce.relay(near_first(turn, up, depth), part)
+    spread.take(depth - 1)
+    up_fold.four()
     for shard in range(PAIR):
 
         def tile(step, carry):
             columns = pl.ds(pl.multiple_of(step * 128, 128), 128)
             source = normed[:, columns]
             for member in range(3):
-                qkv_grad[shard, member, columns, :] = dot_tn(
+                start = member * width + step * 128
+                qkv_grad[shard, pl.ds(pl.multiple_of(start, 128), 128), :] = dot_tn(
                     source, grad_proj[shard, member]
                 ).astype(LOW)
             out_grad[shard, :, columns] = dot_tn(attended[shard], grads[:, columns]).astype(LOW)
             return carry
 
         lax.fori_loop(0, width // 128, tile, 0)
+    down_fold.four()
     reduce.finish(total)
+    for row in range(2 * PAIR):
+        qv_grad[row : row + 1, :] = sum(qv_sums[row, image] for image in range(images))
+    out_bias_grad[...] = sum(out_sums[image] for image in range(images))
     image = first + (up * share) // kept
     live = (
         lax.broadcasted_iota(jnp.int32, (share, 1), 0) + (up * share) % kept < count[image]
     )
-    norm, spread = norm_parts(tokens_own[...].astype(F32))
+    norm, spread_rows = norm_parts(tokens_own[...].astype(F32))
     back = total[...]
-    grad = grad_mid[...] + norm_back(norm, spread, back * (1.0 + mod[image, 1:2, :]))
+    scale_one = mod[pl.ds(image, 1), width : 2 * width]
+    grad = grad_mid[...] + norm_back(norm, spread_rows, back * (1.0 + scale_one))
     grad_tokens[...] = jnp.where(live, grad, 0.0).astype(LOW)
     sums_out[0:1, :] = jnp.sum(back, axis=0, keepdims=True)
     sums_out[1:2, :] = jnp.sum(back * norm, axis=0, keepdims=True)
+    up_fold.five()
+    down_fold.five()
+    for index in range(depth):
+        spread.crossed(index)
+    spread.close()
     gather.close()
     reduce.close()
 
 
-def attend_back(sizes, args):
+def attend_back(sizes, groups, args):
     depth, images, kept, share, pieces = sizes
     width = args[1].shape[1]
     local = args[7].shape[0]
+    up_grad, down_grad = args[-2:]
     rows = images * kept
     shape = jax.ShapeDtypeStruct
     return pl.pallas_call(
-        functools.partial(attend_back_kernel, sizes),
+        functools.partial(attend_back_kernel, sizes, groups),
         out_shape=(
-            shape((PAIR, 3, width, local), LOW),
+            shape((PAIR, 3 * width, local), LOW),
             shape((PAIR, local, width), LOW),
             shape((2 * PAIR, local), F32),
             shape((1, width), F32),
             shape((share, width), LOW),
             shape((2, width), F32),
+            shape((PAIR * rows, width), LOW),
+            shape(up_grad.shape[1:], F32),
+            shape(down_grad.shape[1:], F32),
         ),
-        in_specs=[SM] + [VM] * 11,
-        out_specs=(VM,) * 6,
+        in_specs=[SM] + [VM] * 14,
+        out_specs=(VM,) * 9,
         scratch_shapes=[
             pltpu.VMEM((rows, width), LOW),
             pltpu.VMEM((PAIR, 3, rows, local), LOW),
             pltpu.VMEM((rows, width), LOW),
             pltpu.VMEM((rows + share, width), LOW),
             pltpu.VMEM((share, width), F32),
-            DMA,
+            pltpu.VMEM((2 * PAIR, images, 1, local), F32),
+            pltpu.VMEM((images, 1, width), F32),
+            DMA((2,)),
             DMA((2, depth, pieces)),
             DMA((2, depth, pieces)),
             DMA((depth, pieces)),
             DMA((depth + 1, pieces)),
-        ],
+        ]
+        + Fold.scratch(up_grad.shape, groups, True)
+        + Fold.scratch(down_grad.shape, groups, True)
+        + Spread.scratch(depth, pieces),
         compiler_params=pltpu.CompilerParams(
-            collective_id=3, has_side_effects=True, vmem_limit_bytes=60 << 20
+            collective_id=3, has_side_effects=True, vmem_limit_bytes=62 << 20
         ),
         name="attend_back",
     )(*args)
 
 
-def spread_kernel(sizes, own, whole, own_sem, send, recv, side_send, side_recv):
-    depth, share, pieces = sizes
+def split_low(value):
+    high = value.astype(LOW)
+    rest = value - high.astype(F32)
+    low = rest.astype(LOW)
+    return high, low, (rest - low.astype(F32)).astype(LOW)
+
+
+def close_kernel(
+    sizes,
+    groups,
+    index,
+    grad_tokens,
+    sums,
+    biases,
+    qkv_grad,
+    out_grad,
+    silu_all,
+    mod_weight,
+    cond,
+    grad_patches,
+    qkv_total,
+    out_total,
+    bias_total,
+    mod_weight_grad,
+    mod_bias_grad,
+    grad_cond,
+    whole,
+    sum_row,
+    sum_land,
+    bias_land,
+    cond_land,
+    own_sem,
+    sum_send,
+    sum_recv,
+    bias_send,
+    bias_recv,
+    cond_send,
+    cond_recv,
+    *rest,
+):
+    depth, images, kept, share, pieces = sizes
+    devices = depth * PAIR
+    everyone = devices * groups
     me, up, side = place(depth)
-    half = depth * share
-    rows = share // pieces
-
-    def column(index):
-        return side * half + index * share
-
-    own_copy = pltpu.make_async_copy(
-        own, whole.at[pl.ds(pl.multiple_of(column(up), share), share), :], own_sem
+    group = lax.axis_index("dp")
+    flat = group * devices + me
+    width = grad_tokens.shape[1]
+    columns = mod_weight.shape[1]
+    span = sum_land.shape[2]
+    spread = Spread(whole, share, depth, pieces, rest[:4])
+    qkv_fold = Fold(qkv_grad, rest[4:11], qkv_total, groups, True)
+    out_fold = Fold(out_grad, rest[11:18], out_total, groups, False)
+    own_copy = pltpu.make_async_copy(grad_tokens, spread.own(), own_sem)
+    own_copy.start()
+    barrier = pltpu.get_barrier_semaphore()
+
+    def greet(step, carry):
+        there = (flat + step) % everyone
+        pl.semaphore_signal(
+            barrier,
+            inc=1,
+            device_id={"dp": there // devices, "tensor": there % devices},
+            device_id_type=MESH,
+        )
+        return carry
+
+    lax.fori_loop(1, everyone, greet, 0)
+    pl.semaphore_wait(barrier, everyone - 1)
+    own_copy.wait()
+    spread.open()
+    qkv_fold.one()
+    out_fold.one()
+
+    def aligned(device):
+        return pl.multiple_of((device * columns) // 128 * 128, 128)
+
+    for member in range(6):
+        sum_row[:, member * width : (member + 1) * width] = sums[member : member + 1, :]
+    sum_row[:, 6 * width :] = jnp.zeros((1, sum_row.shape[1] - 6 * width), F32)
+
+    def sum_copy(step):
+        there = (flat + step) % everyone
+        device = there % devices
+        return remote(
+            sum_row.at[:, pl.ds(aligned(device), span)],
+            sum_land.at[flat],
+            sum_send.at[step],
+            sum_recv.at[step],
+            device,
+            there // devices,
+        )
+
+    def send_sum(step, carry):
+        sum_copy(step).start()
+        return carry
+
+    lax.fori_loop(1, everyone, send_sum, 0)
+    sum_land[flat] = sum_row[:, pl.ds(aligned(me), span)]
+    slot = side * groups + group
+    bias_land[slot] = biases[...]
+    partner = me + 1 - 2 * side
+
+    def bias_copy(step):
+        crossed = step // groups
+        there = (group + step) % groups
+        device = jnp.where(crossed == 1, partner, me)
+        return remote(
+            biases, bias_land.at[slot], bias_send.at[step], bias_recv.at[step], device, there
+        )
+
+    for step in range(1, PAIR * groups):
+        bias_copy(step).start()
+    qkv_fold.two()
+    out_fold.two()
+
+    def wait_sum(step, carry):
+        source = (flat + everyone - step) % everyone
+        view = sum_land.at[source]
+        remote(view, view, sum_send.at[step], sum_recv.at[step], me).wait_recv()
+        return carry
+
+    lax.fori_loop(1, everyone, wait_sum, 0)
+    offset = (me * columns) % 128
+    grads = jnp.concatenate([sum_land[device] for device in range(everyone)], axis=0)
+    grads = pltpu.roll(grads, lax.rem(span - offset, span), 1)[:, :columns]
+    mod_bias_grad[...] = jnp.sum(grads, axis=0, keepdims=True)
+    total_images = images * PAIR
+
+    def image_of(device):
+        return (device % PAIR) * images + (device // PAIR) * share // kept
+
+    source = lax.broadcasted_iota(jnp.int32, (everyone, groups * total_images), 0)
+    target = lax.broadcasted_iota(jnp.int32, (everyone, groups * total_images), 1)
+    row_image = source // devices * total_images + image_of(source % devices)
+    chosen = jnp.where(row_image == target, 1.0, 0.0).astype(LOW)
+    silu_rows = dot(
+        chosen,
+        jnp.concatenate([silu_all[member].astype(F32) for member in range(groups)], axis=0).astype(
+            LOW
+        ),
+    ).astype(LOW)
+    parts = split_low(grads)
+    spread.take(1)
+    mod_weight_grad[...] = (
+        dot_tn(silu_rows, parts[0]) + dot_tn(silu_rows, parts[1]) + dot_tn(silu_rows, parts[2])
     )
-    own_copy.start()
-    meet(column_peers(depth) + [up * PAIR + 1 - side])
-    own_copy.wait()
-    here = whole.at[pl.ds(pl.multiple_of(side * half, share), half), :]
-    gather = Gather(here, share, depth, pieces, send, recv)
-
-    def across(index, part):
-        view = whole.at[pl.ds(pl.multiple_of(column(index) + part * rows, rows), rows), :]
+    source = lax.broadcasted_iota(jnp.int32, (total_images, everyone), 1)
+    target = lax.broadcasted_iota(jnp.int32, (total_images, everyone), 0)
+    chosen = jnp.where(
+        (source // devices == group) & (image_of(source % devices) == target), 1.0, 0.0
+    ).astype(LOW)
+    mine = dot(chosen, parts[0]) + dot(chosen, parts[1]) + dot(chosen, parts[2])
+    parts = split_low(mine)
+    term = (
+        dot_nt(parts[0], mod_weight[...])
+        + dot_nt(parts[1], mod_weight[...])
+        + dot_nt(parts[2], mod_weight[...])
+    )
+    cond_land[me] = term
+
+    def cond_copy(step):
         return remote(
-            view,
-            view,
-            side_send.at[index, part],
-            side_recv.at[index, part],
-            up * PAIR + 1 - side,
-        )
-
-    gather.open()
-    for part in range(pieces):
-        across(up, part).start()
-    for turn in range(1, depth):
-        source = gather.take(turn)
-        for part in range(pieces):
-            across(source, part).start()
-    gather.close()
-    for index in range(depth):
-        for part in range(pieces):
-            start = (1 - side) * half + index * share + part * rows
-            view = whole.at[pl.ds(pl.multiple_of(start, rows), rows), :]
-            remote(
-                view, view, side_send.at[index, part], side_recv.at[index, part], me
-            ).wait_recv()
-            across(index, part).wait_send()
-
-
-def spread(own, sizes, ident):
-    depth, share, pieces = sizes
-    width = own.shape[1]
+            cond_land.at[me],
+            cond_land.at[me],
+            cond_send.at[step],
+            cond_recv.at[step],
+            (me + step) % devices,
+        )
+
+    for step in range(1, devices):
+        cond_copy(step).start()
+    qkv_fold.three()
+    out_fold.three()
+    for turn in range(2, depth):
+        spread.take(turn)
+    for step in range(1, PAIR * groups):
+        crossed = step // groups
+        source_group = (group + groups - step % groups) % groups
+        source_side = jnp.where(crossed == 1, 1 - side, side)
+        view = bias_land.at[source_side * groups + source_group]
+        remote(view, view, bias_send.at[step], bias_recv.at[step], me).wait_recv()
+    rows = biases.shape[0]
+    result = jnp.zeros((rows, width), F32)
+    swapped = lax.broadcasted_iota(jnp.int32, (rows, 1), 0) < 6
+    for member in range(PAIR * groups):
+        value = bias_land[member]
+        turned = jnp.concatenate([value[3:6, :], value[0:3, :], value[6:, :]], axis=0)
+        same = side == member // groups
+        result = result + jnp.where(same, value, turned)
+    bias_total[...] = result
+    for step in range(1, devices):
+        source = (me + devices - step) % devices
+        view = cond_land.at[source]
+        remote(view, view, cond_send.at[step], cond_recv.at[step], me).wait_recv()
+    back = cond_land[0]
+    for device in range(1, devices):
+        back = back + cond_land[device]
+    value = cond[...].astype(F32)
+    gate = 1.0 / (1.0 + jnp.exp(-value))
+    grad_cond[...] = (back * (gate + value * gate * (1.0 - gate))).astype(LOW)
+    qkv_fold.four()
+    out_fold.four()
+
+    def place_image(image):
+        rows = pl.ds(pl.multiple_of(image * kept, kept), kept)
+        spots = lax.broadcasted_iota(jnp.int32, (grad_patches.shape[1], kept), 0)
+        pick = jnp.where(spots == index[image], 1.0, 0.0).astype(LOW)
+        grad_patches[image] = dot(pick, whole[rows, :]).astype(LOW)
+
+    def own_side(image, carry):
+        place_image(side * images + image)
+        return carry
+
+    def other_side(image, carry):
+        for part in range(depth // images):
+            spread.crossed(image * (depth // images) + part)
+        place_image((1 - side) * images + image)
+        return carry
+
+    lax.fori_loop(0, images, own_side, 0)
+    lax.fori_loop(0, images, other_side, 0)
+    qkv_fold.five()
+    out_fold.five()
+    spread.close()
+
+    def done_sum(step, carry):
+        sum_copy(step).wait_send()
+        return carry
+
+    lax.fori_loop(1, everyone, done_sum, 0)
+    for step in range(1, PAIR * groups):
+        bias_copy(step).wait_send()
+    for step in range(1, devices):
+        cond_copy(step).wait_send()
+
+
+def close(sizes, groups, args):
+    depth, images, kept, share, pieces = sizes
+    index, grad_tokens, sums, biases, qkv_grad, out_grad, silu_all, mod_weight, cond, spots = args
+    devices = depth * PAIR
+    width = grad_tokens.shape[1]
+    columns = mod_weight.shape[1]
+    span = max(-(-((device * columns) % 128 + columns) // 128) * 128 for device in range(devices))
+    long = max((device * columns) // 128 * 128 + span for device in range(devices))
+    long = max(long, 6 * width + 128)
+    shape = jax.ShapeDtypeStruct
+    rows = PAIR * images * kept
+    everyone = devices * groups
     return pl.pallas_call(
-        functools.partial(spread_kernel, sizes),
-        out_shape=jax.ShapeDtypeStruct((PAIR * depth * share, width), own.dtype),
-        in_specs=[VM],
-        out_specs=VM,
+        functools.partial(close_kernel, sizes, groups),
+        out_shape=(
+            shape((PAIR * images, spots, width), LOW),
+            shape(qkv_grad.shape[1:], F32),
+            shape(out_grad.shape[1:], F32),
+            shape(biases.shape, F32),
+            shape(mod_weight.shape, F32),
+            shape((1, columns), F32),
+            shape(cond.shape, LOW),
+        ),
+        in_specs=[VM] * 9,
+        out_specs=(VM,) * 7,
         scratch_shapes=[
+            pltpu.VMEM((rows, width), LOW),
+            pltpu.VMEM((1, long), F32),
+            pltpu.VMEM((everyone, 1, span), F32),
+            pltpu.VMEM((PAIR * groups,) + biases.shape, F32),
+            pltpu.VMEM((devices,) + cond.shape, F32),
             DMA,
-            DMA((2, depth, pieces)),
-            DMA((2, depth, pieces)),
-            DMA((depth, pieces)),
-            DMA((depth, pieces)),
-        ],
-        compiler_params=pltpu.CompilerParams(collective_id=ident, has_side_effects=True),
-        name="spread",
-    )(own)
-
-
-def scatter_kernel(index, grads, out):
-    spots, kept = out.shape[0], grads.shape[0]
-    rows = lax.broadcasted_iota(jnp.int32, (spots, kept), 0)
-    pick = jnp.where(rows == index[...], 1.0, 0.0).astype(LOW)
-    out[...] = dot(pick, grads[...]).astype(LOW)
-
-
-def scatter(index, grads, spots):
-    images, kept, width = grads.shape
-    return pl.pallas_call(
-        scatter_kernel,
-        out_shape=jax.ShapeDtypeStruct((images, spots, width), LOW),
-        grid=(images,),
-        in_specs=[
-            pl.BlockSpec((None, 1, kept), lambda image: (image, 0, 0)),
-            pl.BlockSpec((None, kept, width), lambda image: (image, 0, 0)),
-        ],
-        out_specs=pl.BlockSpec((None, spots, width), lambda image: (image, 0, 0)),
-        name="scatter",
-    )(index, grads)
+            DMA((everyone,)),
+            DMA((everyone,)),
+            DMA((PAIR * groups,)),
+            DMA((PAIR * groups,)),
+            DMA((devices,)),
+            DMA((devices,)),
+        ]
+        + Spread.scratch(depth, pieces)
+        + Fold.scratch(qkv_grad.shape, groups, True)
+        + Fold.scratch(out_grad.shape, groups, False),
+        compiler_params=pltpu.CompilerParams(
+            collective_id=4, has_side_effects=True, vmem_limit_bytes=62 << 20
+        ),
+        name="close",
+    )(*args[:-1])
 
 
 def on_device(
@@ -978,35 +1591,43 @@
     share = images * kept // depth
     pieces = 4 if share % 64 == 0 else 2
     sizes = (depth, images, kept, share, pieces)
-    me = lax.axis_index("tensor")
-    swap = [(member, member ^ 1) for member in range(devices)]
-
-    def other(value):
-        return lax.ppermute(value, "tensor", swap)
-
-    qkv_other, qv_other, out_other = other(qkv_weight), other(qv_bias), other(out_weight)
-    up_other, down_other = other(up_weight), other(down_weight)
+    groups = lax.axis_size("dp")
+    index = keep_index[:, None, :]
+    qkv_local, units = qkv_weight.shape[2], up_weight.shape[1]
     up_bias_row = up_bias[None, :]
-    up_bias_other = other(up_bias_row)
-    gathered, silu_low = modulation(conditioning, mod_weight, mod_bias[None, :], devices)
-    mod = (
-        gathered.transpose(1, 0, 2).reshape(all_images, 6, width).astype(F32)
-    )
-    index = keep_index[:, None, :]
-    normed_one, proj, attended, tokens_own, mid, branch, normed_two = attend(
+    (
+        normed_one,
+        proj,
+        attended,
+        tokens_own,
+        mid,
+        branch,
+        normed_two,
+        mod,
+        silu_all,
+        qkv_other,
+        qv_other,
+        out_other,
+        up_other,
+        down_other,
+        up_bias_other,
+    ) = attend(
         sizes,
+        groups,
         (
             keep_count,
             index,
             patches,
-            mod,
+            conditioning,
+            mod_weight,
+            mod_bias[None, :],
             qkv_weight,
-            qkv_other,
             qv_bias,
-            qv_other,
             out_weight,
-            out_other,
             out_bias[None, :],
+            up_weight,
+            down_weight,
+            up_bias_row,
         ),
     )
     (
@@ -1036,8 +1657,19 @@
             branch,
         ),
     )
-    qkv_grad, out_grad, qv_grad, out_bias_grad, grad_tokens, sums_one = attend_back(
+    (
+        qkv_grad,
+        out_grad,
+        qv_grad,
+        out_bias_grad,
+        grad_tokens,
+        sums_one,
+        block_out,
+        up_total,
+        down_total,
+    ) = attend_back(
         sizes,
+        groups,
         (
             keep_count,
             grad_branch,
@@ -1051,62 +1683,64 @@
             mod,
             tokens_own,
             grad_mid,
+            block_own,
+            up_grad,
+            down_grad,
         ),
     )
-    block_out = spread(block_own, (depth, share, pieces), 4).reshape(all_images, kept, width)
-    token_grads = spread(grad_tokens, (depth, share, pieces), 5).reshape(all_images, kept, width)
-    grad_patches = scatter(index, token_grads, patches.shape[1])
-
-    own_mod = jnp.concatenate(
-        [sums_one[0], sums_one[1], sums_two[0], sums_two[1], sums_two[2], sums_two[3]]
+
+    def row(value):
+        return jnp.pad(value, ((0, 0), (0, width - value.shape[1])))
+
+    biases = jnp.concatenate(
+        [
+            row(up_bias_grad[0:1]),
+            row(qv_grad[0:2]),
+            row(up_bias_grad[1:2]),
+            row(qv_grad[2:4]),
+            down_bias_grad,
+            out_bias_grad,
+        ]
     )
-    columns = mod_weight.shape[1]
-    every_mod = lax.all_gather(own_mod, ("dp", "tensor"))
-    mine = lax.dynamic_slice_in_dim(every_mod, me * columns, columns, 1)
-    groups = lax.axis_size("dp")
-    holder = jnp.arange(devices)
-    image_of = (holder % PAIR) * images + (holder // PAIR) * share // kept
-    chosen = (image_of[None, :] == jnp.arange(all_images)[:, None]).astype(F32)
-    per_image = jnp.einsum(
-        "id,gdm->gim",
-        chosen,
-        mine.reshape(groups, devices, columns),
-        precision=lax.Precision.HIGHEST,
+    sums = jnp.concatenate([sums_one, sums_two])
+    (
+        grad_patches,
+        qkv_total,
+        out_total,
+        bias_total,
+        mod_weight_grad,
+        mod_bias_grad,
+        grad_conditioning,
+    ) = close(
+        sizes,
+        groups,
+        (
+            index,
+            grad_tokens,
+            sums,
+            biases,
+            qkv_grad,
+            out_grad,
+            silu_all,
+            mod_weight,
+            conditioning,
+            patches.shape[1],
+        ),
     )
-    silu_all = lax.all_gather(silu_low, "dp").astype(F32)
-    mod_weight_grad = jnp.einsum(
-        "gid,gim->dm", silu_all, per_image, precision=lax.Precision.HIGHEST
-    )
-    mod_bias_grad = jnp.sum(per_image, axis=(0, 1))
-    here = lax.dynamic_index_in_dim(per_image, lax.axis_index("dp"), 0, keepdims=False)
-    silu_term = jnp.einsum(
-        "bm,dm->bd", here, mod_weight.astype(F32), precision=lax.Precision.HIGHEST
-    )
-    cond_float = conditioning.astype(F32)
-    grad_silu = lax.psum(silu_term, "tensor")
-    silu_pull = jax.vjp(jax.nn.silu, cond_float)[1]
-    grad_conditioning = silu_pull(grad_silu)[0].astype(LOW)
-
-    def total(both):
-        pair = both[0].astype(F32) + other(both[1]).astype(F32)
-        return lax.psum(pair.astype(LOW), "dp").astype(F32)
-
-    qv_pair = qv_grad.reshape(PAIR, 2, qv_grad.shape[1])
-    whole_bias = jnp.concatenate([down_bias_grad, out_bias_grad])
     return (
-        block_out,
+        block_out.reshape(all_images, kept, width),
         grad_patches,
         grad_conditioning,
         mod_weight_grad,
-        mod_bias_grad,
-        total(qkv_grad),
-        total(qv_pair.astype(LOW)),
-        total(out_grad),
-        total(jnp.stack([out_bias_grad[0], out_bias_grad[0]]).astype(LOW)),
-        total(up_grad),
-        total(up_bias_grad.astype(LOW)),
-        total(down_grad),
-        total(jnp.stack([down_bias_grad[0], down_bias_grad[0]]).astype(LOW)),
+        mod_bias_grad[0],
+        qkv_total.reshape(qkv_weight.shape),
+        bias_total[1:3, :qkv_local],
+        out_total,
+        bias_total[7],
+        up_total,
+        bias_total[0, :units],
+        down_total,
+        bias_total[6],
     )
 
 

time: 653 us -> 419 us (0.64)
  blocking collectives: 125 us -> 0 us
  waiting for transfers between devices: 57.9 us -> 0 us
  other arithmetic: 19.1 us -> 2.61 us
  starting transfers between devices: 15.9 us -> 0 us
  between operations: 14.4 us -> 0.77 us
  matrix products: 6.67 us -> 0 us
    all_gather x2 -> x0, blocking collectives: 81.3 us -> none  [the longest x1 75.8 us: on_device(): every_mod = lax.all_gather(own_mod, ('dp', 'tensor'))]
    ppermute x14 -> x0, waiting for transfers between devices: 57.8 us -> none  [other(): return lax.ppermute(value, 'tensor', swap)]
    psum x2 -> x0, blocking collectives: 43.6 us -> none  [the longest x1 33.5 us: on_device(): grad_silu = lax.psum(silu_term, 'tensor')]
    convert_element_type x19 -> x0, other arithmetic: 18.5 us -> none  [the longest x14 16.2 us: total(): return lax.psum(pair.astype(LOW), 'dp').astype(F32)]
    ppermute x14 -> x0, starting transfers between devices: 15.8 us -> none  [other(): return lax.ppermute(value, 'tensor', swap)]
    squeeze x6 -> x0, local copies, waits for them, and re-layouts: 11.6 us -> none  [total(): pair = both[0].astype(F32) + other(both[1]).astype(F32)]
    unnamed x58 -> x31, local copies, waits for them, and re-layouts: 17.7 us -> 28.5 us
    ppermute x4 -> x0, local copies, waits for them, and re-layouts: 9.93 us -> none  [other(): return lax.ppermute(value, 'tensor', swap)]
  transfers between devices with their start and end apart: 15 -> 0, of which waited for: 2 -> 0; matrix products, arithmetic and copies ran while one was open for 9% -> 0% of each run, Pallas kernels for 32% -> 0%
where the time goes in v2:
time: 419 us; the launch traced here: 418 us
  Pallas kernels  373 us (89%)
  local copies, waits for them, and re-layouts  41.2 us (10%)
    pallas_call x1, Pallas kernels, attend_back(): pl.pallas_call(functools.partial(attend_back_kernel, sizes, groups), out_...  112 us
    pallas_call x1, Pallas kernels, feed(): pl.pallas_call(functools.partial(feed_kernel, sizes), out_shape=(shape((P...  96.1 us
    pallas_call x1, Pallas kernels, close(): pl.pallas_call(functools.partial(close_kernel, sizes, groups), out_shape=...  90.2 us
    pallas_call x1, Pallas kernels, attend(): pl.pallas_call(functools.partial(attend_kernel, sizes, groups), out_shape...  75.1 us
    unnamed x31, local copies, waits for them, and re-layouts  28.5 us

profile of v2, /device:TPU:0, one launch (start us, length us, event | category | flops | bytes accessed | tf_op | source)
XLA Modules:
  0.0 417.9 jit_solution(12080415656533429440)
XLA Ops:
  0.6 0.0 copy-start.4
  0.7 1.3 broadcast_in_dim.18.up_bias_own
  2.0 1.3 broadcast_in_dim.16.mod_bias
  3.3 1.3 broadcast_in_dim.17.out_bias
  4.5 1.3 broadcast_in_dim.19.down_bias
  5.8 1.3 broadcast_in_dim.15.index
  7.1 2.7 copy.30.up_own
  9.9 1.7 copy.29.qkv_own
  11.6 0.0 copy-done.3
  11.6 2.4 copy.28.mod_weight
  14.0 75.1 %attend.1 = (bf16[768,1152]{1,0:T(8,128)(2,1)}, bf16[2,3,768,144]{3,2,1,0:T(8,128)(2,1)}, bf16[2,768,144]{2,1,0:T(8,128)(2,1)}, bf16[192,1152]{1,0:T(8,128)(2,1)...) custom-call(s32[8]{0:T(128)} %count.5, ...), custom_call_target="tpu_custom_call" | custom-call | tf_op jit(solution)/shard_map/attend/pallas_call | solution.py:777
  89.1 96.1 %feed.1 = (bf16[2,1152,576]{2,1,0:T(8,128)(2,1)}, bf16[2,576,1152]{2,1,0:T(8,128)(2,1)}, f32[2,576]{1,0:T(2,128)}, f32[1,1152]{1,0:T(1,128)}, bf16[192,1152]{1,0...) custom-call(s32[8]{0:T(128)} %count.5, ...), custom_call_target="tpu_custom_call" | custom-call | tf_op jit(solution)/shard_map/feed/pallas_call | solution.py:1004
  185.2 0.0 copy-start.8
  185.2 0.0 copy-start.9
  185.2 111.9 %attend_back.1 = (bf16[2,3456,144]{2,1,0:T(8,128)(2,1)}, bf16[2,144,1152]{2,1,0:T(8,128)(2,1)}, f32[4,144]{1,0:T(4,128)}, f32[1,1152]{1,0:T(1,128)}, bf16[192,11...) custom-call(s32[8]{0:T(128)} %count.5, ...), custom_call_target="tpu_custom_call" | custom-call | tf_op jit(solution)/shard_map/attend_back/pallas_call | solution.py:1245
  297.2 0.8 fusion.1
  298.0 1.3 concatenate.7.biases
  299.3 1.3 pad_maximum_fusion.sums
  300.7 3.4 copy.36
  304.1 90.2 %close.1 = (bf16[8,256,1152]{2,1,0:T(8,128)(2,1)}, f32[3456,144]{1,0:T(8,128)}, f32[144,1152]{1,0:T(8,128)}, f32[8,1152]{1,0:T(8,128)}, f32[1152,864]{1,0:T(8,12...) custom-call(s32[8,1,192]{2,1,0:T(1,128)} %broadcast_in_dim.15.index, bf16[192,1152]{1,0:T(8,128)(2,1)} %get-tuple-element.70.grad_tokens, ...), custom_call_target="tpu_custom_call" | custom-call | tf_op jit(solution)/shard_map/close/pallas_call | solution.py:1532
  394.3 1.3 slice.28
  395.6 1.3 reduce
  396.8 1.3 slice_reduce_fusion.2
  398.2 1.5 slice_reduce_fusion
  399.7 3.5 copy.35
  403.2 5.7 %copy.34 = f32[1152,864]{0,1:T(8,128)} copy(f32[1152,864]{1,0:T(8,128)} %get-tuple-element.92) | data formatting | bytes 7962624
  408.9 1.8 copy.42
  410.7 1.8 copy-done
  412.5 2.4 copy.43
  414.9 0.6 copy.44
  415.5 0.8 copy.45
  416.4 1.5 copy.46
  (20 shorter events, 0.1 us)
Async XLA Ops:
  0.6 9.2 %copy-start.4 = (bf16[3,1152,144]{1,2,0:T(8,128)(2,1)S(1)}, bf16[3,1152,144]{1,2,0:T(8,128)(2,1)}, u32[]{:S(2)}) copy-start(bf16[3,1152,144]{1,2,0:T(8,128)(2,1)} %param.21) | copy-start | bytes 2985988
  7.1 4.5 %copy-start.3 = (bf16[1152,864]{0,1:T(8,128)(2,1)S(1)}, bf16[1152,864]{0,1:T(8,128)(2,1)}, u32[]{:S(2)}) copy-start(bf16[1152,864]{0,1:T(8,128)(2,1)} %param.19) | copy-start | bytes 5971972
  185.2 112.7 %copy-start.8 = (f32[2,576]{1,0:T(2,128)S(1)}, f32[2,576]{1,0:T(2,128)}, u32[]{:S(2)}) copy-start(f32[2,576]{1,0:T(2,128)} %get-tuple-element.73) | copy-start | bytes 13828
  185.2 112.8 %copy-start.9 = (f32[1,1152]{1,0:T(1,128)S(1)}, f32[1,1152]{1,0:T(1,128)}, u32[]{:S(2)}) copy-start(f32[1,1152]{1,0:T(1,128)} %get-tuple-element.75) | copy-start | bytes 13828
  185.2 114.1 %copy-start.7 = (f32[4,1152]{1,0:T(4,128)S(1)}, f32[4,1152]{1,0:T(4,128)}, u32[]{:S(2)}) copy-start(f32[4,1152]{1,0:T(4,128)} %get-tuple-element.72) | copy-start | bytes 55300
  403.2 5.7 %copy-start.1 = (bf16[1536,1152]{1,0:T(8,128)(2,1)S(1)}, bf16[1536,1152]{1,0:T(8,128)(2,1)}, u32[]{:S(2)}) copy-start(bf16[1536,1152]{1,0:T(8,128)(2,1)} %get-tuple-element.69) | copy-start | bytes 10616836
  408.9 3.6 copy-start
  412.5 2.4 copy-start.6
  412.5 3.0 copy-start.5
  412.5 3.9 copy-start.2

commit v3 on v2

--- a/solution.py
+++ b/solution.py
@@ -34,7 +34,30 @@
 
 def place(depth):
     me = lax.axis_index("tensor")
-    return me, me // PAIR, me % PAIR
+    return me, me % depth, me // depth
+
+
+def bits_of(depth):
+    return depth.bit_length() - 1
+
+
+def toward(spot, bit):
+    return (1 - 2 * ((spot // (1 << bit)) % 2)) * (1 << bit)
+
+
+def across(spot, offset, depth):
+    result = spot
+    for bit in range(bits_of(depth)):
+        result = result + ((offset // (1 << bit)) % 2) * toward(spot, bit)
+    return result
+
+
+def offset_between(left, right, depth):
+    result = 0
+    for bit in range(bits_of(depth)):
+        size = 1 << bit
+        result = result + ((left // size + right // size) % 2) * size
+    return result
 
 
 def meet(peers):
@@ -47,16 +70,17 @@
 
 
 def column_peers(depth):
-    me, up, side = place(depth)
+    me, spot, side = place(depth)
     group = lax.axis_index("dp")
-    return [(group, ((up + step) % depth) * PAIR + side) for step in range(1, depth)]
-
-
-def cube_peers(groups):
-    me = lax.axis_index("tensor")
+    return [(group, me + toward(spot, bit)) for bit in range(bits_of(depth))]
+
+
+def cube_peers(depth, groups):
+    me, spot, side = place(depth)
     group = lax.axis_index("dp")
+    other = me + depth * (1 - 2 * side)
     peers = [((group + step) % groups, me) for step in range(1, groups)]
-    return peers + [((group + step) % groups, me + 1 - 2 * (me % PAIR)) for step in range(groups)]
+    return peers + [((group + step) % groups, other) for step in range(groups)]
 
 
 def dot(left, right):
@@ -85,15 +109,17 @@
     return (grad - mean_grad - norm * mean_both) * spread
 
 
-class Gather:
+class Line:
     def __init__(self, buffer, share, depth, pieces, send, recv):
         self.buffer, self.share, self.depth, self.pieces = buffer, share, depth, pieces
         self.send, self.recv = send, recv
-        self.me, self.up, self.side = place(depth)
+        self.me = lax.axis_index("tensor")
+        self.up, self.side = self.me // PAIR, self.me % PAIR
 
     def piece(self, index, part):
         rows = self.share // self.pieces
-        return self.buffer.at[pl.ds(pl.multiple_of(index * self.share + part * rows, rows), rows), :]
+        start = (index * PAIR + self.side) * self.share + part * rows
+        return self.buffer.at[pl.ds(pl.multiple_of(start, rows), rows), :]
 
     def copy(self, way, step, part):
         source = self.up - (step - 1) * (1 - 2 * way)
@@ -127,30 +153,22 @@
         mixed = turn <= 2 * both
         way = jnp.where(mixed, (turn + 1) % 2, jnp.where(below > above, 0, 1))
         step = jnp.where(mixed, (turn + 1) // 2, turn - both)
-        step = jnp.where(turn == 0, 0, step)
         return way, step, self.up - step * (1 - 2 * way)
 
-    def take(self, turn):
+    def take(self, turn, then):
         way, step, source = self.arrival(turn)
         ahead = jnp.where(way == 0, self.up + 1 < self.depth, self.up >= 1)
-
-        @pl.when(turn > 0)
-        def _():
-            for part in range(self.pieces):
-                view = self.piece(source, part)
-                remote(
-                    view,
-                    view,
-                    self.send.at[way, step, part],
-                    self.recv.at[way, step, part],
-                    self.me,
-                ).wait_recv()
-
-                @pl.when(ahead)
-                def _():
-                    self.copy(way, step + 1, part).start()
-
-        return source
+        for part in range(self.pieces):
+            view = self.piece(source, part)
+            remote(
+                view, view, self.send.at[way, step, part], self.recv.at[way, step, part], self.me
+            ).wait_recv()
+
+            @pl.when(ahead)
+            def _():
+                self.copy(way, step + 1, part).start()
+
+            then(source, part)
 
     def close(self):
         for way in range(2):
@@ -162,55 +180,144 @@
                         self.copy(way, step, part).wait_send()
 
 
-class Reduce:
-    def __init__(self, terms, landing, share, depth, pieces, send, recv):
-        self.terms, self.landing, self.share, self.depth, self.pieces = (
-            terms,
-            landing,
-            share,
-            depth,
-            pieces,
-        )
-        self.send, self.recv = send, recv
-        self.me, self.up, self.side = place(depth)
+class Cube:
+    def __init__(self, share, depth, pieces):
+        self.share, self.depth, self.pieces = share, depth, pieces
+        self.me, self.spot, self.side = place(depth)
+        self.bits = bits_of(depth)
         self.rows = share // pieces
+
+    def order(self, part):
+        ways = list(range(self.bits))
+        return ways if part % 2 else ways[::-1]
 
     def span(self, index, part):
         return pl.ds(pl.multiple_of(index * self.share + part * self.rows, self.rows), self.rows)
 
-    def copy(self, way, owner, part):
-        target = self.up + 1 - 2 * way
-        slot = owner if way == 0 else jnp.where(owner == target, self.depth, owner)
+    def neighbour(self, bit):
+        return self.me + toward(self.spot, bit)
+
+
+class Gather(Cube):
+    def __init__(self, buffer, share, depth, pieces, send, recv):
+        super().__init__(share, depth, pieces)
+        self.buffer, self.send, self.recv = buffer, send, recv
+
+    def last(self, offset, part):
+        order = self.order(part)
+        return max(
+            (stage for stage in range(self.bits) if offset >> order[stage] & 1), default=-1
+        )
+
+    def copy(self, offset, stage, part):
+        bit = self.order(part)[stage]
+        view = self.buffer.at[self.span(across(self.spot, offset, self.depth), part), :]
         return remote(
-            self.terms.at[self.span(owner, part), :],
+            view,
+            view,
+            self.send.at[offset, stage, part],
+            self.recv.at[offset ^ (1 << bit), part],
+            self.neighbour(bit),
+        )
+
+    def landed(self, offset, part):
+        view = self.buffer.at[self.span(across(self.spot, offset, self.depth), part), :]
+        remote(
+            view, view, self.send.at[0, 0, part], self.recv.at[offset, part], self.me
+        ).wait_recv()
+
+    def sends(self, offset):
+        return [
+            (stage, part)
+            for part in range(self.pieces)
+            for stage in range(self.last(offset, part) + 1, self.bits)
+        ]
+
+    def open(self):
+        for stage, part in self.sends(0):
+            self.copy(0, stage, part).start()
+
+    def relay(self):
+        for offset in sorted(range(1, self.depth), key=lambda value: bin(value).count("1")):
+            for part in range(self.pieces):
+                first = self.last(offset, part) + 1
+                if first < self.bits:
+                    self.landed(offset, part)
+                    for stage in range(first, self.bits):
+                        self.copy(offset, stage, part).start()
+
+    def take(self, offset):
+        for member in range(1, self.depth):
+
+            @pl.when(offset == member)
+            def _():
+                for part in range(self.pieces):
+                    if self.last(member, part) + 1 == self.bits:
+                        self.landed(member, part)
+
+    def close(self):
+        for offset in range(self.depth):
+            for stage, part in self.sends(offset):
+                self.copy(offset, stage, part).wait_send()
+
+    @staticmethod
+    def scratch(depth, pieces):
+        return [DMA((depth, bits_of(depth), pieces)), DMA((depth, pieces))]
+
+
+class Reduce(Cube):
+    def __init__(self, terms, landing, share, depth, pieces, send, recv):
+        super().__init__(share, depth, pieces)
+        self.terms, self.landing, self.send, self.recv = terms, landing, send, recv
+
+    def slot(self, stage, offset, part):
+        order = self.order(part)
+        found = [
+            (level, member)
+            for level in range(self.bits)
+            for member in range(self.depth)
+            if not any(member >> order[below] & 1 for below in range(level + 1))
+        ]
+        return found.index((stage, offset))
+
+    def first(self, offset, part):
+        order = self.order(part)
+        return min(stage for stage in range(self.bits) if offset >> order[stage] & 1)
+
+    def copy(self, offset, part):
+        stage = self.first(offset, part)
+        bit = self.order(part)[stage]
+        slot = self.slot(stage, offset ^ (1 << bit), part)
+        return remote(
+            self.terms.at[self.span(across(self.spot, offset, self.depth), part), :],
             self.landing.at[self.span(slot, part), :],
-            self.send.at[owner, part],
+            self.send.at[offset, part],
             self.recv.at[slot, part],
-            target * PAIR + self.side,
+            self.neighbour(bit),
         )
 
     def landed(self, slot, part):
         view = self.landing.at[self.span(slot, part), :]
         remote(view, view, self.send.at[0, part], self.recv.at[slot, part], self.me).wait_recv()
 
-    def ready(self, owner):
-        @pl.when((self.up == 0) & (owner > 0))
-        def _():
-            for part in range(self.pieces):
-                self.copy(0, owner, part).start()
-
-        @pl.when((self.up == self.depth - 1) & (owner < self.depth - 1))
-        def _():
-            for part in range(self.pieces):
-                self.copy(1, owner, part).start()
-
-    def add(self, target, target_start, term_start, starts):
+    def ready(self, offset):
+        for member in range(1, self.depth):
+
+            @pl.when(offset == member)
+            def _():
+                for part in range(self.pieces):
+                    if self.first(member, part) == 0:
+                        self.copy(member, part).start()
+
+    def ready_share(self, index):
+        self.ready(offset_between(index, self.spot, self.depth))
+
+    def add(self, target, target_start, term_start, slots, part):
         def body(index, carry):
             offset = index * 16
-            value = self.terms[
-                pl.ds(pl.multiple_of(term_start + offset, 16), 16), :
-            ].astype(F32)
-            for start in starts:
+            value = self.terms[pl.ds(pl.multiple_of(term_start + offset, 16), 16), :].astype(F32)
+            for slot in slots:
+                start = slot * self.share + part * self.rows
                 value = value + self.landing[
                     pl.ds(pl.multiple_of(start + offset, 16), 16), :
                 ].astype(F32)
@@ -221,61 +328,40 @@
 
         lax.fori_loop(0, self.rows // 16, body, 0)
 
-    def relay(self, owner, part):
-        start = owner * self.share + part * self.rows
-
-        def pass_on(way):
-            self.landed(owner, part)
-            self.add(self.terms, start, start, [start])
-            self.copy(way, owner, part).start()
-
-        @pl.when((owner > self.up) & (self.up > 0))
-        def _():
-            pass_on(0)
-
-        @pl.when((owner < self.up) & (self.up < self.depth - 1))
-        def _():
-            pass_on(1)
+    def relay(self):
+        for level in range(1, self.bits):
+            for part in range(self.pieces):
+                for offset in range(1, self.depth):
+                    if self.first(offset, part) == level:
+                        slots = [self.slot(below, offset, part) for below in range(level)]
+                        for slot in slots:
+                            self.landed(slot, part)
+                        start = (
+                            across(self.spot, offset, self.depth) * self.share + part * self.rows
+                        )
+                        self.add(self.terms, start, start, slots, part)
+                        self.copy(offset, part).start()
 
     def finish(self, total):
-        start = self.up * self.share
-        end = self.depth * self.share
         for part in range(self.pieces):
+            slots = [self.slot(stage, 0, part) for stage in range(self.bits)]
+            for slot in slots:
+                self.landed(slot, part)
             skip = part * self.rows
-
-            @pl.when(self.up == 0)
-            def _():
-                self.landed(self.depth, part)
-                self.add(total, skip, start + skip, [end + skip])
-
-            @pl.when(self.up == self.depth - 1)
-            def _():
-                self.landed(self.up, part)
-                self.add(total, skip, start + skip, [start + skip])
-
-            @pl.when((self.up > 0) & (self.up < self.depth - 1))
-            def _():
-                self.landed(self.up, part)
-                self.landed(self.depth, part)
-                self.add(total, skip, start + skip, [start + skip, end + skip])
+            self.add(total, skip, self.spot * self.share + skip, slots, part)
 
     def close(self):
-        for owner in range(self.depth):
-
-            @pl.when(self.up != owner)
-            def _():
-                for part in range(self.pieces):
-                    remote(
-                        self.terms.at[self.span(owner, part), :],
-                        self.landing.at[self.span(owner, part), :],
-                        self.send.at[owner, part],
-                        self.recv.at[owner, part],
-                        self.me,
-                    ).wait_send()
+        for offset in range(1, self.depth):
+            for part in range(self.pieces):
+                self.copy(offset, part).wait_send()
+
+    @staticmethod
+    def scratch(depth, pieces):
+        return [DMA((depth, pieces)), DMA((depth - 1, pieces))]
 
 
 class Fold:
-    def __init__(self, source, scratch, out, groups, split):
+    def __init__(self, source, scratch, out, depth, groups, split):
         self.source, self.out, self.groups, self.split = source, out, groups, split
         self.stage, self.near, self.side_land, self.far, self.low, self.send, self.recv = scratch
         self.me = lax.axis_index("tensor")
@@ -283,7 +369,7 @@
         self.core = self.group % PAIR
         self.line = self.group // PAIR
         self.mate = self.group + 1 - 2 * self.core
-        self.partner = self.me + 1 - 2 * (self.me % PAIR)
+        self.partner = self.me + depth * (1 - 2 * (self.me // depth))
         self.lines = groups // PAIR
         self.rows = self.stage.shape[1]
         self.start = self.core * self.rows if split else 0
@@ -422,10 +508,8 @@
     def __init__(self, whole, share, depth, pieces, scratch):
         self.whole, self.share, self.depth, self.pieces = whole, share, depth, pieces
         send, recv, self.side_send, self.side_recv = scratch
-        self.me, self.up, self.side = place(depth)
-        self.half = depth * share
-        here = whole.at[pl.ds(pl.multiple_of(self.side * self.half, share), self.half), :]
-        self.gather = Gather(here, share, depth, pieces, send, recv)
+        self.line = Line(whole, share, depth, pieces, send, recv)
+        self.me, self.up, self.side = self.line.me, self.line.up, self.line.side
 
     @staticmethod
     def scratch(depth, pieces):
@@ -436,14 +520,29 @@
             DMA((depth, pieces)),
         ]
 
+    def peers(self):
+        group = lax.axis_index("dp")
+        line = [
+            (group, (self.up + step) % self.depth * PAIR + self.side)
+            for step in range(1, self.depth)
+        ]
+        return line + [(group, self.me + 1 - 2 * self.side)]
+
+    def peers_beyond(self, depth):
+        me, spot, side = place(depth)
+        group = lax.axis_index("dp")
+        return [
+            (group, (self.up + step) % self.depth * PAIR + self.side)
+            for step in range(1, self.depth)
+        ]
+
     def view(self, side, index, part):
         rows = self.share // self.pieces
-        start = side * self.half + index * self.share + part * rows
+        start = (index * PAIR + side) * self.share + part * rows
         return self.whole.at[pl.ds(pl.multiple_of(start, rows), rows), :]
 
     def own(self):
-        start = self.side * self.half + self.up * self.share
-        return self.whole.at[pl.ds(pl.multiple_of(start, self.share), self.share), :]
+        return self.whole.at[pl.ds(pl.multiple_of(self.me * self.share, self.share), self.share), :]
 
     def across(self, index, part):
         view = self.view(self.side, index, part)
@@ -456,14 +555,12 @@
         )
 
     def open(self):
-        self.gather.open()
+        self.line.open()
         for part in range(self.pieces):
             self.across(self.up, part).start()
 
     def take(self, turn):
-        source = self.gather.take(turn)
-        for part in range(self.pieces):
-            self.across(source, part).start()
+        self.line.take(turn, lambda source, part: self.across(source, part).start())
 
     def crossed(self, index):
         for part in range(self.pieces):
@@ -473,25 +570,67 @@
             ).wait_recv()
 
     def close(self):
-        self.gather.close()
+        self.line.close()
         for index in range(self.depth):
             for part in range(self.pieces):
                 self.across(index, part).wait_send()
 
 
-def far_first(turn, group, count):
-    low = group < count // 2
-    own = jnp.where(low, count - 1 - group, group)
-    moved = jnp.where(turn >= own, turn + 1, turn)
-    other = jnp.where(low, count - 1 - moved, moved)
-    return jnp.where(turn == count - 1, group, other)
-
-
-def near_first(turn, up, depth):
-    low = up < depth // 2
-    ahead = jnp.where(turn < depth - 1 - up, up + 1 + turn, depth - 2 - turn)
-    behind = jnp.where(turn < up, up - 1 - turn, turn + 1)
-    return jnp.where(low, ahead, behind)
+class Share:
+    def __init__(self, source, target, sems, depth, groups):
+        self.source, self.target = source, target
+        self.send, self.recv, self.near_send, self.near_recv = sems
+        self.me, _, side = place(depth)
+        self.group = lax.axis_index("dp")
+        self.partner = self.me + depth * (1 - 2 * side)
+        rows = source.shape[-2]
+        self.parts = groups if rows % (groups * 16) == 0 else PAIR if rows % (PAIR * 16) == 0 else 1
+        self.rows = rows // self.parts
+        self.mine = self.group % self.parts
+
+    def view(self, array, part):
+        rows = pl.ds(pl.multiple_of(part * self.rows, 16) if self.parts > 1 else 0, self.rows)
+        return array.at[:, rows, :] if len(array.shape) == 3 else array.at[rows, :]
+
+    def copy(self):
+        return remote(
+            self.view(self.source, self.mine),
+            self.view(self.target, self.mine),
+            self.send,
+            self.recv,
+            self.partner,
+        )
+
+    def mate(self, step):
+        base = self.group - self.mine
+        return base + (self.mine + step) % self.parts
+
+    def hand(self, step):
+        view = self.view(self.target, self.mine)
+        return remote(
+            view, view, self.near_send.at[step], self.near_recv.at[step], self.me, self.mate(step)
+        )
+
+    def start(self):
+        self.copy().start()
+
+    def pass_on(self):
+        self.copy().wait_recv()
+        for step in range(1, self.parts):
+            self.hand(step).start()
+
+    def wait(self):
+        for step in range(1, self.parts):
+            part = (self.mine + self.parts - step) % self.parts
+            view = self.view(self.target, part)
+            remote(
+                view, view, self.near_send.at[step], self.near_recv.at[step], self.me, self.group
+            ).wait_recv()
+
+    def close(self):
+        self.copy().wait_send()
+        for step in range(1, self.parts):
+            self.hand(step).wait_send()
 
 
 def head_mask(head, width):
@@ -570,16 +709,13 @@
     silu_recv,
     weight_send,
     weight_recv,
-    mate_send,
-    mate_recv,
+    near_send,
+    near_recv,
 ):
     depth, images, kept, share, pieces = sizes
     devices = depth * PAIR
     me, up, side = place(depth)
     group = lax.axis_index("dp")
-    core = group % PAIR
-    mate = group + 1 - 2 * core
-    partner = me + 1 - 2 * side
     width = patches.shape[2]
     scale = HD ** (-0.5)
     fold = depth // images
@@ -590,8 +726,11 @@
             patches.at[first + image], patch_rows.at[image], patch_sem.at[image]
         )
 
+    def image_at(turn):
+        return across(up // fold, images - 1 - turn, images)
+
     for turn in range(images):
-        fetch(far_first(turn, up // fold, images)).start()
+        fetch(image_at(turn)).start()
     meet(
         [(group, (me + step) % devices) for step in range(1, devices)]
         + [((group + step) % groups, me) for step in range(1, groups)]
@@ -626,50 +765,36 @@
     for copy in mod_copies + silu_copies:
         copy.start()
 
-    def part_of(array, which):
-        if len(array.shape) == 3:
-            rows = array.shape[1] // 2
-            return array.at[:, pl.ds(pl.multiple_of(which * rows, 16), rows), :]
-        rows = array.shape[0] // 2
-        return array.at[pl.ds(pl.multiple_of(which * rows, 16), rows), :]
-
-    halved = [(qkv_own, qkv_other), (up_own, up_other), (down_own, down_other)]
-    full = [(qv_own, qv_other), (out_own, out_other), (up_bias_own, up_bias_other)]
-
-    def half_copy(which):
-        source, target = halved[which]
-        return remote(
-            part_of(source, core),
-            part_of(target, core),
-            weight_send.at[which],
-            weight_recv.at[which],
-            partner,
-        )
-
-    def full_copy(which):
-        source, target = full[which]
-        return remote(
+    shares = [
+        Share(
             source,
             target,
-            weight_send.at[3 + which],
-            weight_recv.at[3 + which],
-            partner,
-        )
-
-    def mate_copy(which, half):
-        view = part_of(halved[which][1], half)
-        return remote(view, view, mate_send.at[which], mate_recv.at[which], me, mate)
-
-    full_copy(0).start()
-    half_copy(0).start()
-    full_copy(1).start()
-    full_copy(2).start()
-    half_copy(1).start()
-    half_copy(2).start()
+            (
+                weight_send.at[which],
+                weight_recv.at[which],
+                near_send.at[which],
+                near_recv.at[which],
+            ),
+            depth,
+            groups,
+        )
+        for which, (source, target) in enumerate(
+            (
+                (qv_own, qv_other),
+                (qkv_own, qkv_other),
+                (out_own, out_other),
+                (up_bias_own, up_bias_other),
+                (up_own, up_other),
+                (down_own, down_other),
+            )
+        )
+    ]
+    for member in shares:
+        member.start()
     reduce = Reduce(terms, landing, share, depth, pieces, send, recv)
 
     def pick_rows(turn, carry):
-        image = far_first(turn, up // fold, images)
+        image = image_at(turn)
         fetch(image).wait()
         rows = pl.ds(pl.multiple_of(image * kept, kept), kept)
         spots = lax.broadcasted_iota(jnp.int32, (patches.shape[1], kept), 0)
@@ -694,13 +819,13 @@
         return mod[pl.ds(first + image, 1), member * width : (member + 1) * width]
 
     def one(turn, carry):
-        image = far_first(turn, up // fold, images)
+        image = image_at(turn)
         rows = pl.ds(pl.multiple_of(image * kept, kept), kept)
 
         @pl.when(turn == images - 1)
         def _():
-            half_copy(0).wait_recv()
-            mate_copy(0, core).start()
+            shares[0].pass_on()
+            shares[1].pass_on()
 
         norm, _ = norm_parts(tokens[rows, :].astype(F32))
         normed = (norm * (1.0 + block(image, 1)) + block(image, 0)).astype(LOW)
@@ -712,7 +837,7 @@
         return carry
 
     def two(turn, carry):
-        image = far_first(turn, up // fold, images)
+        image = image_at(turn)
         rows = pl.ds(pl.multiple_of(image * kept, kept), kept)
         key_live = lax.broadcasted_iota(jnp.int32, (1, kept), 1) < count[first + image]
         attended = attend_shard(
@@ -722,22 +847,18 @@
         branch = dot(attended_out[0, rows, :], out_own[...]) + dot(attended, out_other[...])
         terms[rows, :] = branch.astype(LOW)
         for part in range(fold):
-            reduce.ready(image * fold + part)
+            reduce.ready_share(image * fold + part)
         return carry
 
     lax.fori_loop(0, images, one, 0)
-    full_copy(0).wait_recv()
-    full_copy(1).wait_recv()
-    mate_copy(0, 1 - core).wait_recv()
+    shares[2].pass_on()
+    for member in shares[:3]:
+        member.wait()
     lax.fori_loop(0, images, two, 0)
-    for turn in range(depth - 1):
-        for part in range(pieces):
-            reduce.relay(far_first(turn, up, depth), part)
-        if turn == 0:
-            half_copy(1).wait_recv()
-            mate_copy(1, core).start()
-    half_copy(2).wait_recv()
-    mate_copy(2, core).start()
+    shares[3].pass_on()
+    shares[4].pass_on()
+    reduce.relay()
+    shares[5].pass_on()
     reduce.finish(total)
     image = (up * share) // kept
     own = tokens[pl.ds(pl.multiple_of(up * share, share), share), :]
@@ -749,19 +870,16 @@
     norm, _ = norm_parts(mid)
     normed_two_out[...] = (norm * (1.0 + block(image, 4)) + block(image, 3)).astype(LOW)
     reduce.close()
-    full_copy(2).wait_recv()
-    mate_copy(1, 1 - core).wait_recv()
-    mate_copy(2, 1 - core).wait_recv()
+    for member in shares[3:]:
+        member.wait()
     for step in range(1, groups):
         source = (group + groups - step) % groups
         view = silu_all.at[source]
         remote(
-            view, view, silu_send.at[step], silu_recv.at[step], me, mate
+            view, view, silu_send.at[step], silu_recv.at[step], me, group
         ).wait_recv()
-    for which in range(3):
-        half_copy(which).wait_send()
-        full_copy(which).wait_send()
-        mate_copy(which, core).wait_send()
+    for member in shares:
+        member.close()
     for copy in mod_copies + silu_copies:
         copy.wait_send()
 
@@ -799,21 +917,22 @@
             pltpu.VMEM((images, spots, width), LOW),
             pltpu.VMEM((rows, width), LOW),
             pltpu.VMEM((rows, width), LOW),
-            pltpu.VMEM((rows + share, width), LOW),
+            pltpu.VMEM((rows - share, width), LOW),
             pltpu.VMEM((share, width), F32),
             pltpu.VMEM((cond.shape[0], mod_weight.shape[1]), LOW),
             pltpu.VMEM((devices, cond.shape[0], mod_weight.shape[1]), LOW),
             DMA((images,)),
-            DMA((depth, pieces)),
-            DMA((depth + 1, pieces)),
+        ]
+        + Reduce.scratch(depth, pieces)
+        + [
             DMA((devices,)),
             DMA((devices,)),
             DMA((groups,)),
             DMA((groups,)),
             DMA((6,)),
             DMA((6,)),
-            DMA((3,)),
-            DMA((3,)),
+            DMA((6, groups)),
+            DMA((6, groups)),
         ],
         compiler_params=pltpu.CompilerParams(
             collective_id=1, has_side_effects=True, vmem_limit_bytes=60 << 20
@@ -928,32 +1047,34 @@
         terms[rows, :] = back.astype(LOW)
         mlp_terms[rows, :] = mlp.astype(LOW)
         for part in range(fold):
-            reduce.ready(image * fold + part)
+            reduce.ready_share(image * fold + part)
 
     if fold == 1:
 
         def turn_of(turn, carry):
-            one(gather.take(turn))
+            @pl.when(turn == 1)
+            def _():
+                gather.relay()
+
+            offset = turn + (turn // 2) * (1 - 2 * (turn % 2))
+            gather.take(offset)
+            one(across(up, offset, depth))
             return carry
 
         lax.fori_loop(0, depth, turn_of, 0)
     else:
-
-        def take_of(turn, carry):
-            gather.take(turn)
-            return carry
 
         def image_of(image, carry):
             one(image)
             return carry
 
-        lax.fori_loop(0, depth, take_of, 0)
+        gather.relay()
+        for offset in range(1, depth):
+            gather.take(offset)
         lax.fori_loop(0, images, image_of, 0)
-    for owner in range(depth):
-        mlp_reduce.ready(owner)
-    for turn in range(depth - 1):
-        for part in range(pieces):
-            reduce.relay(near_first(turn, up, depth), part)
+    for offset in range(1, depth):
+        mlp_reduce.ready(depth - offset)
+    reduce.relay()
     for shard in range(PAIR):
 
         def tile(step, carry):
@@ -965,10 +1086,8 @@
             return carry
 
         lax.fori_loop(0, width // 128, tile, 0)
+    mlp_reduce.relay()
     reduce.finish(total)
-    for turn in range(depth - 1):
-        for part in range(pieces):
-            mlp_reduce.relay(far_first(turn, up, depth), part)
     for shard in range(PAIR):
         up_bias_grad[shard : shard + 1, :] = sum(up_sums[shard, image] for image in range(images))
     down_bias_grad[...] = sum(down_sums[image] for image in range(images))
@@ -1022,22 +1141,19 @@
             pltpu.VMEM((PAIR, rows, units), LOW),
             pltpu.VMEM((rows, width), LOW),
             pltpu.VMEM((rows, width), LOW),
-            pltpu.VMEM((rows + share, width), LOW),
+            pltpu.VMEM((rows - share, width), LOW),
             pltpu.VMEM((rows, width), LOW),
-            pltpu.VMEM((rows + share, width), LOW),
+            pltpu.VMEM((rows - share, width), LOW),
             pltpu.VMEM((share, width), F32),
             pltpu.VMEM((share, width), F32),
             pltpu.VMEM((PAIR, images, 1, units), F32),
             pltpu.VMEM((images, 1, width), F32),
             DMA((images,)),
             DMA,
-            DMA((2, depth, pieces)),
-            DMA((2, depth, pieces)),
-            DMA((depth, pieces)),
-            DMA((depth + 1, pieces)),
-            DMA((depth, pieces)),
-            DMA((depth + 1, pieces)),
-        ],
+        ]
+        + Gather.scratch(depth, pieces)
+        + Reduce.scratch(depth, pieces)
+        + Reduce.scratch(depth, pieces),
         compiler_params=pltpu.CompilerParams(
             collective_id=2, has_side_effects=True, vmem_limit_bytes=60 << 20
         ),
@@ -1093,15 +1209,15 @@
     scale = HD ** (-0.5)
     fold = depth // images
     first = side * images
-    up_fold = Fold(up_grad, rest[:7], up_total, groups, True)
-    down_fold = Fold(down_grad, rest[7:14], down_total, groups, True)
+    up_fold = Fold(up_grad, rest[:7], up_total, depth, groups, True)
+    down_fold = Fold(down_grad, rest[7:14], down_total, depth, groups, True)
     spread = Spread(block_out, share, depth, pieces, rest[14:18])
     own_rows = pl.ds(pl.multiple_of(up * share, share), share)
     own_copy = pltpu.make_async_copy(grad_own, grads.at[own_rows, :], own_sem.at[0])
     own_copy.start()
     block_copy = pltpu.make_async_copy(block_own, spread.own(), own_sem.at[1])
     block_copy.start()
-    meet(column_peers(depth) + cube_peers(groups))
+    meet(column_peers(depth) + cube_peers(depth, groups) + spread.peers_beyond(depth))
     own_copy.wait()
     gather = Gather(grads, share, depth, pieces, gather_send, gather_recv)
     reduce = Reduce(terms, landing, share, depth, pieces, send, recv)
@@ -1145,55 +1261,57 @@
                     qv_sums[row, image] = jnp.sum(low.astype(F32), axis=0, keepdims=True)
         terms[rows, :] = back.astype(LOW)
         for part in range(fold):
-            reduce.ready(image * fold + part)
+            reduce.ready_share(image * fold + part)
 
     if fold == 1:
 
         def turn_of(turn, carry):
-            one(gather.take(turn))
+            @pl.when(turn == 1)
+            def _():
+                gather.relay()
+
+            offset = turn + (turn // 2) * (1 - 2 * (turn % 2))
+            gather.take(offset)
+            one(across(up, offset, depth))
 
             @pl.when(turn == 0)
             def _():
                 up_fold.two()
                 down_fold.two()
+
+            @pl.when(turn == 1)
+            def _():
                 spread.open()
 
             @pl.when(turn == 2)
             def _():
                 up_fold.three()
 
-            @pl.when(turn >= 2)
-            def _():
-                spread.take(turn - 1)
-
             return carry
 
         lax.fori_loop(0, depth, turn_of, 0)
     else:
-
-        def take_of(turn, carry):
-            gather.take(turn)
-            return carry
 
         def image_of(image, carry):
             one(image)
             return carry
 
-        def spread_of(turn, carry):
-            spread.take(turn)
-            return carry
-
-        lax.fori_loop(0, depth, take_of, 0)
+        gather.relay()
+        for offset in range(1, depth):
+            gather.take(offset)
         up_fold.two()
         down_fold.two()
         spread.open()
         lax.fori_loop(0, images, image_of, 0)
         up_fold.three()
-        lax.fori_loop(1, depth - 1, spread_of, 0)
+
+    def spread_of(turn, carry):
+        spread.take(turn)
+        return carry
+
+    reduce.relay()
+    lax.fori_loop(1, depth - 1, spread_of, 0)
     down_fold.three()
-    for turn in range(depth - 1):
-        for part in range(pieces):
-            reduce.relay(near_first(turn, up, depth), part)
     spread.take(depth - 1)
     up_fold.four()
     for shard in range(PAIR):
@@ -1261,16 +1379,14 @@
             pltpu.VMEM((rows, width), LOW),
             pltpu.VMEM((PAIR, 3, rows, local), LOW),
             pltpu.VMEM((rows, width), LOW),
-            pltpu.VMEM((rows + share, width), LOW),
+            pltpu.VMEM((rows - share, width), LOW),
             pltpu.VMEM((share, width), F32),
             pltpu.VMEM((2 * PAIR, images, 1, local), F32),
             pltpu.VMEM((images, 1, width), F32),
             DMA((2,)),
-            DMA((2, depth, pieces)),
-            DMA((2, depth, pieces)),
-            DMA((depth, pieces)),
-            DMA((depth + 1, pieces)),
         ]
+        + Gather.scratch(depth, pieces)
+        + Reduce.scratch(depth, pieces)
         + Fold.scratch(up_grad.shape, groups, True)
         + Fold.scratch(down_grad.shape, groups, True)
         + Spread.scratch(depth, pieces),
@@ -1331,8 +1447,8 @@
     columns = mod_weight.shape[1]
     span = sum_land.shape[2]
     spread = Spread(whole, share, depth, pieces, rest[:4])
-    qkv_fold = Fold(qkv_grad, rest[4:11], qkv_total, groups, True)
-    out_fold = Fold(out_grad, rest[11:18], out_total, groups, False)
+    qkv_fold = Fold(qkv_grad, rest[4:11], qkv_total, depth, groups, True)
+    out_fold = Fold(out_grad, rest[11:18], out_total, depth, groups, False)
     own_copy = pltpu.make_async_copy(grad_tokens, spread.own(), own_sem)
     own_copy.start()
     barrier = pltpu.get_barrier_semaphore()
@@ -1381,7 +1497,7 @@
     sum_land[flat] = sum_row[:, pl.ds(aligned(me), span)]
     slot = side * groups + group
     bias_land[slot] = biases[...]
-    partner = me + 1 - 2 * side
+    partner = me + depth * (1 - 2 * side)
 
     def bias_copy(step):
         crossed = step // groups
@@ -1410,7 +1526,7 @@
     total_images = images * PAIR
 
     def image_of(device):
-        return (device % PAIR) * images + (device // PAIR) * share // kept
+        return device * share // kept
 
     source = lax.broadcasted_iota(jnp.int32, (everyone, groups * total_images), 0)
     target = lax.broadcasted_iota(jnp.int32, (everyone, groups * total_images), 1)
@@ -1464,7 +1580,6 @@
         remote(view, view, bias_send.at[step], bias_recv.at[step], me).wait_recv()
     rows = biases.shape[0]
     result = jnp.zeros((rows, width), F32)
-    swapped = lax.broadcasted_iota(jnp.int32, (rows, 1), 0) < 6
     for member in range(PAIR * groups):
         value = bias_land[member]
         turned = jnp.concatenate([value[3:6, :], value[0:3, :], value[6:, :]], axis=0)
@@ -1490,18 +1605,14 @@
         pick = jnp.where(spots == index[image], 1.0, 0.0).astype(LOW)
         grad_patches[image] = dot(pick, whole[rows, :]).astype(LOW)
 
-    def own_side(image, carry):
-        place_image(side * images + image)
+    for index_of in range(depth):
+        spread.crossed(index_of)
+
+    def put(image, carry):
+        place_image(image)
         return carry
 
-    def other_side(image, carry):
-        for part in range(depth // images):
-            spread.crossed(image * (depth // images) + part)
-        place_image((1 - side) * images + image)
-        return carry
-
-    lax.fori_loop(0, images, own_side, 0)
-    lax.fori_loop(0, images, other_side, 0)
+    lax.fori_loop(0, PAIR * images, put, 0)
     qkv_fold.five()
     out_fold.five()
     spread.close()

time: 419 us -> 455 us (1.086)
  Pallas kernels: 373 us -> 410 us
    pallas_call x1, Pallas kernels: 96.1 us -> 57.6 us  [feed(): pl.pallas_call(functools.partial(feed_kernel, sizes), out_shape=(shape((P...]
    pallas_call x1, Pallas kernels: 75.1 us -> 108 us  [attend(): pl.pallas_call(functools.partial(attend_kernel, sizes, groups), out_shape...]
    pallas_call x1, Pallas kernels: 90.2 us -> 118 us  [close(): pl.pallas_call(functools.partial(close_kernel, sizes, groups), out_shape=...]
    pallas_call x1, Pallas kernels: 112 us -> 126 us  [attend_back(): pl.pallas_call(functools.partial(attend_back_kernel, sizes, groups), out_...]
where the time goes in v3:
time: 455 us
  Pallas kernels  410 us (90%)
  local copies, waits for them, and re-layouts  41.2 us (9%)
    pallas_call x1, Pallas kernels, attend_back(): pl.pallas_call(functools.partial(attend_back_kernel, sizes, groups), out_...  126 us
    pallas_call x1, Pallas kernels, close(): pl.pallas_call(functools.partial(close_kernel, sizes, groups), out_shape=...  118 us
    pallas_call x1, Pallas kernels, attend(): pl.pallas_call(functools.partial(attend_kernel, sizes, groups), out_shape...  108 us
    pallas_call x1, Pallas kernels, feed(): pl.pallas_call(functools.partial(feed_kernel, sizes), out_shape=(shape((P...  57.6 us
    unnamed x31, local copies, waits for them, and re-layouts  28.5 us

profile of v3, /device:TPU:0, one launch (start us, length us, event | category | flops | bytes accessed | tf_op | source)
XLA Modules:
  0.0 454.6 jit_solution(14165344351481795054)
XLA Ops:
  0.7 1.3 broadcast_in_dim.18.up_bias_own
  2.0 1.3 broadcast_in_dim.16.mod_bias
  3.3 1.3 broadcast_in_dim.17.out_bias
  4.5 1.3 broadcast_in_dim.19.down_bias
  5.8 1.3 broadcast_in_dim.15.index
  7.1 2.7 copy.30.up_own
  9.9 1.7 copy.29.qkv_own
  11.6 2.4 copy.28.mod_weight
  14.0 108.0 %attend.1 = (bf16[768,1152]{1,0:T(8,128)(2,1)}, bf16[2,3,768,144]{3,2,1,0:T(8,128)(2,1)}, bf16[2,768,144]{2,1,0:T(8,128)(2,1)}, bf16[192,1152]{1,0:T(8,128)(2,1)...) custom-call(s32[8]{0:T(128)} %count.5, ...), custom_call_target="tpu_custom_call" | custom-call | tf_op jit(solution)/shard_map/attend/pallas_call | solution.py:895
  122.0 57.6 %feed.1 = (bf16[2,1152,576]{2,1,0:T(8,128)(2,1)}, bf16[2,576,1152]{2,1,0:T(8,128)(2,1)}, f32[2,576]{1,0:T(2,128)}, f32[1,1152]{1,0:T(1,128)}, bf16[192,1152]{1,0...) custom-call(s32[8]{0:T(128)} %count.5, ...), custom_call_target="tpu_custom_call" | custom-call | tf_op jit(solution)/shard_map/feed/pallas_call | solution.py:1123
  179.6 126.5 %attend_back.1 = (bf16[2,3456,144]{2,1,0:T(8,128)(2,1)}, bf16[2,144,1152]{2,1,0:T(8,128)(2,1)}, f32[4,144]{1,0:T(4,128)}, f32[1,1152]{1,0:T(1,128)}, bf16[192,11...) custom-call(s32[8]{0:T(128)} %count.5, ...), custom_call_target="tpu_custom_call" | custom-call | tf_op jit(solution)/shard_map/attend_back/pallas_call | solution.py:1363
  306.1 0.8 fusion.1
  306.9 0.0 copy-done.9
  306.9 1.3 concatenate.7.biases
  308.3 0.0 copy-done.7
  308.3 1.3 pad_maximum_fusion.sums
  309.6 3.4 copy.36
  313.0 117.9 %close.1 = (bf16[8,256,1152]{2,1,0:T(8,128)(2,1)}, f32[3456,144]{1,0:T(8,128)}, f32[144,1152]{1,0:T(8,128)}, f32[8,1152]{1,0:T(8,128)}, f32[1152,864]{1,0:T(8,12...) custom-call(s32[8,1,192]{2,1,0:T(1,128)} %broadcast_in_dim.15.index, bf16[192,1152]{1,0:T(8,128)(2,1)} %get-tuple-element.70.grad_tokens, ...), custom_call_target="tpu_custom_call" | custom-call | tf_op jit(solution)/shard_map/close/pallas_call | solution.py:1643
  430.9 1.3 slice.28
  432.2 1.3 reduce
  433.5 1.3 slice_reduce_fusion.2
  434.8 1.5 slice_reduce_fusion
  436.3 3.5 copy.35
  439.9 5.7 %copy.34 = f32[1152,864]{0,1:T(8,128)} copy(f32[1152,864]{1,0:T(8,128)} %get-tuple-element.92) | data formatting | bytes 7962624
  445.6 0.0 copy-done.1
  445.6 1.8 copy.42
  447.4 1.8 copy-done
  449.2 2.4 copy.43
  451.6 0.6 copy.44
  452.2 0.8 copy.45
  453.0 0.0 copy-done.2
  453.1 1.5 copy.46
  (20 shorter events, 0.1 us)
Async XLA Ops:
  0.6 9.2 %copy-start.4 = (bf16[3,1152,144]{1,2,0:T(8,128)(2,1)S(1)}, bf16[3,1152,144]{1,2,0:T(8,128)(2,1)}, u32[]{:S(2)}) copy-start(bf16[3,1152,144]{1,2,0:T(8,128)(2,1)} %param.21) | copy-start | bytes 2985988
  7.1 4.5 copy-start.3
  179.6 127.3 %copy-start.8 = (f32[2,576]{1,0:T(2,128)S(1)}, f32[2,576]{1,0:T(2,128)}, u32[]{:S(2)}) copy-start(f32[2,576]{1,0:T(2,128)} %get-tuple-element.73) | copy-start | bytes 13828
  179.6 127.3 %copy-start.9 = (f32[1,1152]{1,0:T(1,128)S(1)}, f32[1,1152]{1,0:T(1,128)}, u32[]{:S(2)}) copy-start(f32[1,1152]{1,0:T(1,128)} %get-tuple-element.75) | copy-start | bytes 13828
  179.6 128.7 %copy-start.7 = (f32[4,1152]{1,0:T(4,128)S(1)}, f32[4,1152]{1,0:T(4,128)}, u32[]{:S(2)}) copy-start(f32[4,1152]{1,0:T(4,128)} %get-tuple-element.72) | copy-start | bytes 55300
  439.9 5.7 %copy-start.1 = (bf16[1536,1152]{1,0:T(8,128)(2,1)S(1)}, bf16[1536,1152]{1,0:T(8,128)(2,1)}, u32[]{:S(2)}) copy-start(bf16[1536,1152]{1,0:T(8,128)(2,1)} %get-tuple-element.69) | copy-start | bytes 10616836
  445.6 3.6 copy-start
  449.2 2.4 copy-start.6
  449.2 3.0 copy-start.5
  449.2 3.9 copy-start.2

commit v4 on v3

--- a/solution.py
+++ b/solution.py
@@ -81,6 +81,34 @@
     other = me + depth * (1 - 2 * side)
     peers = [((group + step) % groups, me) for step in range(1, groups)]
     return peers + [((group + step) % groups, other) for step in range(groups)]
+
+
+def padded(rows, groups):
+    return -(-rows // (16 * groups)) * 16 * groups
+
+
+def lanes(columns):
+    return -(-columns // 128) * 128
+
+
+def row_spots(width, units, local, mods):
+    spots = {}
+    start = 0
+    for name, size in (
+        ("out", width),
+        ("down", width),
+        ("up", units),
+        ("query", local),
+        ("value", local),
+        ("mod", mods),
+    ):
+        spots[name] = start
+        start += lanes(size)
+    return spots, start
+
+
+def tile_of(width):
+    return 384 if width % 384 == 0 else 128
 
 
 def dot(left, right):
@@ -361,59 +389,86 @@
 
 
 class Fold:
-    def __init__(self, source, scratch, out, depth, groups, split):
-        self.source, self.out, self.groups, self.split = source, out, groups, split
-        self.stage, self.near, self.side_land, self.far, self.low, self.send, self.recv = scratch
+    def __init__(self, source, scratch, out, depth, groups):
+        self.source, self.out = source, out
+        (
+            self.stage,
+            self.near,
+            self.land,
+            self.part,
+            self.side_land,
+            self.low,
+            self.send,
+            self.recv,
+        ) = scratch
         self.me = lax.axis_index("tensor")
         self.group = lax.axis_index("dp")
+        self.lines = groups // PAIR
         self.core = self.group % PAIR
         self.line = self.group // PAIR
         self.mate = self.group + 1 - 2 * self.core
         self.partner = self.me + depth * (1 - 2 * (self.me // depth))
-        self.lines = groups // PAIR
-        self.rows = self.stage.shape[1]
-        self.start = self.core * self.rows if split else 0
+        self.rows = self.part.shape[1]
+        self.half = self.rows * self.lines
 
     @staticmethod
-    def scratch(shape, groups, split):
+    def scratch(shape, groups):
         _, rows, width = shape
-        half = rows // 2 if split else rows
         lines = groups // PAIR
+        part = rows // groups
         return [
-            pltpu.VMEM((PAIR, half, width), LOW),
-            pltpu.VMEM((PAIR, half, width), LOW),
-            pltpu.VMEM((half, width), LOW),
-            pltpu.VMEM((lines, half, width), LOW),
+            pltpu.VMEM((PAIR, part * lines, width), LOW),
+            pltpu.VMEM((PAIR, part * lines, width), LOW),
+            pltpu.VMEM((lines, PAIR, part, width), LOW),
+            pltpu.VMEM((PAIR, part, width), LOW),
+            pltpu.VMEM((part, width), LOW),
             pltpu.VMEM((rows, width), LOW),
-            DMA((3 + lines,)),
-            DMA((3 + lines,)),
+            DMA((2 + 3 * lines,)),
+            DMA((2 + 3 * lines,)),
         ]
 
-    def each(self, body):
-        step = 48 if self.rows % 48 == 0 else self.rows
+    def each(self, rows, body):
+        step = 48 if rows % 48 == 0 else 16 if rows % 16 == 0 else rows
 
         def run(index, carry):
             body(pl.multiple_of(index * step, step), step)
             return carry
 
-        lax.fori_loop(0, self.rows // step, run, 0)
+        lax.fori_loop(0, rows // step, run, 0)
 
     def window(self, start, size):
-        return pl.ds(pl.multiple_of(start, 16) if self.split else start, size)
+        return pl.ds(pl.multiple_of(start, 16), size)
+
+    def behind(self, step):
+        return (self.line + self.lines - step) % self.lines
+
+    def block(self, core, line):
+        return self.low.at[self.window(core * self.half + line * self.rows, self.rows), :]
 
     def near_copy(self):
-        if self.split:
-            away = self.window((1 - self.core) * self.rows, self.rows)
-            source = self.source.at[:, away, :]
-        else:
-            source = self.source
         return remote(
-            source, self.near, self.send.at[0], self.recv.at[0], self.me, self.mate
+            self.source.at[:, self.window((1 - self.core) * self.half, self.half), :],
+            self.near,
+            self.send.at[0],
+            self.recv.at[0],
+            self.me,
+            self.mate,
+        )
+
+    def cross_copy(self, step):
+        line = (self.line + step) % self.lines
+        return remote(
+            self.stage.at[:, self.window(line * self.rows, self.rows), :],
+            self.land.at[self.line],
+            self.send.at[2 + step],
+            self.recv.at[2 + step],
+            self.me,
+            line * PAIR + self.core,
         )
 
     def side_copy(self):
         return remote(
-            self.stage.at[1],
+            self.part.at[1],
             self.side_land,
             self.send.at[1],
             self.recv.at[1],
@@ -421,20 +476,23 @@
             self.group,
         )
 
-    def far_copy(self, step):
+    def line_copy(self, step):
         line = (self.line + step) % self.lines
+        view = self.block(self.core, self.line)
+        slot = 2 + self.lines + step
         return remote(
-            self.far.at[self.line],
-            self.far.at[self.line],
-            self.send.at[2 + step],
-            self.recv.at[2 + step],
+            view,
+            view,
+            self.send.at[slot],
+            self.recv.at[slot],
             self.me,
             line * PAIR + self.core,
         )
 
-    def mate_copy(self, core):
-        view = self.low.at[self.window(core * self.rows, self.rows), :]
-        return remote(view, view, self.send.at[2], self.recv.at[2], self.me, self.mate)
+    def mate_copy(self, core, line):
+        view = self.block(core, line)
+        slot = 2 + 2 * self.lines + line
+        return remote(view, view, self.send.at[slot], self.recv.at[slot], self.me, self.mate)
 
     def one(self):
         self.near_copy().start()
@@ -443,65 +501,77 @@
         self.near_copy().wait_recv()
 
         def add(at, size):
+            rows = self.window(at, size)
             for shard in range(PAIR):
-                mine = self.source[shard, self.window(self.start + at, size), :].astype(F32)
-                rows = self.window(at, size)
+                mine = self.source[shard, self.window(self.core * self.half + at, size), :]
                 self.stage[shard, rows, :] = (
-                    mine + self.near[shard, rows, :].astype(F32)
+                    mine.astype(F32) + self.near[shard, rows, :].astype(F32)
                 ).astype(LOW)
 
-        self.each(add)
-        self.side_copy().start()
+        self.each(self.half, add)
+        for step in range(1, self.lines):
+            self.cross_copy(step).start()
 
     def three(self):
-        self.side_copy().wait_recv()
-
-        def add(at, size):
-            rows = self.window(at, size)
-            self.far[self.line, rows, :] = (
-                self.stage[0, rows, :].astype(F32) + self.side_land[rows, :].astype(F32)
-            ).astype(LOW)
-
-        self.each(add)
         for step in range(1, self.lines):
-            self.far_copy(step).start()
-
-    def four(self):
-        for step in range(1, self.lines):
-            line = (self.line + self.lines - step) % self.lines
-            view = self.far.at[line]
+            view = self.land.at[self.behind(step)]
             remote(
                 view, view, self.send.at[2 + step], self.recv.at[2 + step], self.me, self.mate
             ).wait_recv()
 
         def add(at, size):
             rows = self.window(at, size)
-            value = self.far[0, rows, :].astype(F32)
-            for line in range(1, self.lines):
-                value = value + self.far[line, rows, :].astype(F32)
-            low = value.astype(LOW)
-            spot = self.window(self.start + at, size)
-            self.low[spot, :] = low
-            self.out[spot, :] = low.astype(F32)
-
-        self.each(add)
-        if self.split:
-            self.mate_copy(self.core).start()
+            for shard in range(PAIR):
+                value = self.stage[
+                    shard, self.window(self.line * self.rows + at, size), :
+                ].astype(F32)
+                for step in range(1, self.lines):
+                    value = value + self.land[self.behind(step), shard, rows, :].astype(F32)
+                self.part[shard, rows, :] = value.astype(LOW)
+
+        self.each(self.rows, add)
+        self.side_copy().start()
+
+    def four(self):
+        self.side_copy().wait_recv()
+
+        def add(at, size):
+            rows = self.window(at, size)
+            value = self.part[0, rows, :].astype(F32) + self.side_land[rows, :].astype(F32)
+            spot = self.window(self.core * self.half + self.line * self.rows + at, size)
+            self.low[spot, :] = value.astype(LOW)
+
+        self.each(self.rows, add)
+        for step in range(1, self.lines):
+            self.line_copy(step).start()
+        self.mate_copy(self.core, self.line).start()
 
     def five(self):
-        if self.split:
-            self.mate_copy(1 - self.core).wait_recv()
-
-            def put(at, size):
-                spot = self.window((1 - self.core) * self.rows + at, size)
-                self.out[spot, :] = self.low[spot, :].astype(F32)
-
-            self.each(put)
-            self.mate_copy(self.core).wait_send()
+        for step in range(1, self.lines):
+            line = self.behind(step)
+            view = self.block(self.core, line)
+            slot = 2 + self.lines + step
+            remote(
+                view, view, self.send.at[slot], self.recv.at[slot], self.me, self.mate
+            ).wait_recv()
+            self.mate_copy(self.core, line).start()
+
+    def six(self):
+        for line in range(self.lines):
+            self.mate_copy(1 - self.core, line).wait_recv()
+
+        def put(at, size):
+            rows = pl.ds(at, size)
+            self.out[rows, :] = self.low[rows, :].astype(F32)
+
+        self.each(self.out.shape[0], put)
         self.near_copy().wait_send()
         self.side_copy().wait_send()
         for step in range(1, self.lines):
-            self.far_copy(step).wait_send()
+            self.cross_copy(step).wait_send()
+            self.line_copy(step).wait_send()
+        for line in range(self.lines):
+            self.mate_copy(self.core, line).wait_send()
 
 
 class Spread:
@@ -577,38 +647,66 @@
 
 
 class Share:
-    def __init__(self, source, target, sems, depth, groups):
+    def __init__(self, source, target, send, recv, which, depth, groups):
         self.source, self.target = source, target
-        self.send, self.recv, self.near_send, self.near_recv = sems
+        self.send, self.recv, self.which = send, recv, which
         self.me, _, side = place(depth)
         self.group = lax.axis_index("dp")
         self.partner = self.me + depth * (1 - 2 * side)
-        rows = source.shape[-2]
-        self.parts = groups if rows % (groups * 16) == 0 else PAIR if rows % (PAIR * 16) == 0 else 1
-        self.rows = rows // self.parts
-        self.mine = self.group % self.parts
-
-    def view(self, array, part):
-        rows = pl.ds(pl.multiple_of(part * self.rows, 16) if self.parts > 1 else 0, self.rows)
-        return array.at[:, rows, :] if len(array.shape) == 3 else array.at[rows, :]
+        rows = source.shape[0]
+        self.all_lines = groups // PAIR
+        self.cores = PAIR if rows % (PAIR * 16) == 0 else 1
+        self.lines = self.all_lines if rows % (groups * 16) == 0 else 1
+        self.rows = rows // (self.cores * self.lines)
+        self.core = self.group % PAIR
+        self.line = self.group // PAIR
+        self.my_core = self.core if self.cores > 1 else 0
+        self.my_line = self.line if self.lines > 1 else 0
+
+    @staticmethod
+    def scratch(members, groups):
+        lines = groups // PAIR
+        return [DMA((members, 1 + 2 * lines)), DMA((members, 1 + 2 * lines))]
+
+    def view(self, array, core, line):
+        if self.cores == 1:
+            return array
+        start = (core * self.lines + line) * self.rows
+        return array.at[pl.ds(pl.multiple_of(start, 16), self.rows), :]
+
+    def behind(self, step):
+        return (self.line + self.lines - step) % self.lines
 
     def copy(self):
         return remote(
-            self.view(self.source, self.mine),
-            self.view(self.target, self.mine),
-            self.send,
-            self.recv,
+            self.view(self.source, self.my_core, self.my_line),
+            self.view(self.target, self.my_core, self.my_line),
+            self.send.at[self.which, 0],
+            self.recv.at[self.which, 0],
             self.partner,
         )
 
-    def mate(self, step):
-        base = self.group - self.mine
-        return base + (self.mine + step) % self.parts
-
     def hand(self, step):
-        view = self.view(self.target, self.mine)
+        view = self.view(self.target, self.my_core, self.my_line)
         return remote(
-            view, view, self.near_send.at[step], self.near_recv.at[step], self.me, self.mate(step)
+            view,
+            view,
+            self.send.at[self.which, step],
+            self.recv.at[self.which, step],
+            self.me,
+            (self.line + step) % self.lines * PAIR + self.core,
+        )
+
+    def mate(self, core, line):
+        view = self.view(self.target, core, line)
+        slot = self.all_lines + line
+        return remote(
+            view,
+            view,
+            self.send.at[self.which, slot],
+            self.recv.at[self.which, slot],
+            self.me,
+            self.group + 1 - 2 * self.core,
         )
 
     def start(self):
@@ -616,21 +714,37 @@
 
     def pass_on(self):
         self.copy().wait_recv()
-        for step in range(1, self.parts):
+        for step in range(1, self.lines):
             self.hand(step).start()
+        if self.cores > 1:
+            self.mate(self.core, self.my_line).start()
+
+    def relay(self):
+        for step in range(1, self.lines):
+            line = self.behind(step)
+            view = self.view(self.target, self.core, line)
+            remote(
+                view,
+                view,
+                self.send.at[self.which, step],
+                self.recv.at[self.which, step],
+                self.me,
+                self.group,
+            ).wait_recv()
+            self.mate(self.core, line).start()
 
     def wait(self):
-        for step in range(1, self.parts):
-            part = (self.mine + self.parts - step) % self.parts
-            view = self.view(self.target, part)
-            remote(
-                view, view, self.near_send.at[step], self.near_recv.at[step], self.me, self.group
-            ).wait_recv()
+        if self.cores > 1:
+            for line in range(self.lines):
+                self.mate(1 - self.core, line).wait_recv()
 
     def close(self):
         self.copy().wait_send()
-        for step in range(1, self.parts):
+        for step in range(1, self.lines):
             self.hand(step).wait_send()
+        if self.cores > 1:
+            for line in range(self.lines):
+                self.mate(self.core, line).wait_send()
 
 
 def head_mask(head, width):
@@ -646,11 +760,13 @@
     return raised / jnp.sum(raised, axis=-1, keepdims=True)
 
 
-def attend_shard(normed, qkv, qv, proj_out, shard, rows, key_live, scale):
-    local = qkv.shape[2]
-    queries = (dot(normed, qkv[0]) + qv[0:1, :].astype(F32)).astype(LOW)
-    keys = dot(normed, qkv[1]).astype(LOW)
-    values = (dot(normed, qkv[2]) + qv[1:2, :].astype(F32)).astype(LOW)
+def attend_shard(normed, heads, row, spots, proj_out, shard, rows, key_live, scale):
+    local = heads.shape[0] // 4
+    query_bias = row[:, spots["query"] : spots["query"] + local]
+    value_bias = row[:, spots["value"] : spots["value"] + local]
+    queries = (dot_nt(normed, heads[0:local, :]) + query_bias).astype(LOW)
+    keys = dot_nt(normed, heads[local : 2 * local, :]).astype(LOW)
+    values = (dot_nt(normed, heads[2 * local : 3 * local, :]) + value_bias).astype(LOW)
     proj_out[shard, 0, rows, :] = queries
     proj_out[shard, 1, rows, :] = keys
     proj_out[shard, 2, rows, :] = values
@@ -670,14 +786,10 @@
     patches,
     cond,
     mod_weight,
-    mod_bias,
-    qkv_own,
-    qv_own,
-    out_own,
-    out_bias,
+    heads_own,
     up_own,
     down_own,
-    up_bias_own,
+    row_own,
     normed_out,
     proj_out,
     attended_out,
@@ -687,12 +799,10 @@
     normed_two_out,
     mod,
     silu_all,
-    qkv_other,
-    qv_other,
-    out_other,
+    heads_other,
     up_other,
     down_other,
-    up_bias_other,
+    row_other,
     patch_rows,
     tokens,
     terms,
@@ -709,14 +819,15 @@
     silu_recv,
     weight_send,
     weight_recv,
-    near_send,
-    near_recv,
 ):
     depth, images, kept, share, pieces = sizes
     devices = depth * PAIR
     me, up, side = place(depth)
     group = lax.axis_index("dp")
     width = patches.shape[2]
+    local = heads_own.shape[0] // 4
+    mods = mod_weight.shape[0]
+    spots, _ = row_spots(width, up_own.shape[0], local, mods)
     scale = HD ** (-0.5)
     fold = depth // images
     first = side * images
@@ -738,7 +849,9 @@
     value = cond[...].astype(F32)
     silu = (value / (1.0 + jnp.exp(-value))).astype(LOW)
     silu_all[group] = silu
-    local_mod = (dot(silu, mod_weight[...]) + mod_bias[...].astype(F32)).astype(LOW)
+    local_mod = (
+        dot_nt(silu, mod_weight[...]) + row_own[:, spots["mod"] : spots["mod"] + mods]
+    ).astype(LOW)
     mod_mine[...] = local_mod
     mod_gathered[me] = local_mod
     mod_copies = [
@@ -766,24 +879,11 @@
         copy.start()
 
     shares = [
-        Share(
-            source,
-            target,
-            (
-                weight_send.at[which],
-                weight_recv.at[which],
-                near_send.at[which],
-                near_recv.at[which],
-            ),
-            depth,
-            groups,
-        )
+        Share(source, target, weight_send, weight_recv, which, depth, groups)
         for which, (source, target) in enumerate(
             (
-                (qv_own, qv_other),
-                (qkv_own, qkv_other),
-                (out_own, out_other),
-                (up_bias_own, up_bias_other),
+                (row_own, row_other),
+                (heads_own, heads_other),
                 (up_own, up_other),
                 (down_own, down_other),
             )
@@ -797,11 +897,10 @@
         image = image_at(turn)
         fetch(image).wait()
         rows = pl.ds(pl.multiple_of(image * kept, kept), kept)
-        spots = lax.broadcasted_iota(jnp.int32, (patches.shape[1], kept), 0)
+        positions = lax.broadcasted_iota(jnp.int32, (patches.shape[1], kept), 0)
         slots = lax.broadcasted_iota(jnp.int32, (patches.shape[1], kept), 1)
-        pick = jnp.where(
-            (spots == index[first + image]) & (slots < count[first + image]), 1.0, 0.0
-        )
+        listed = index[pl.ds(first + image, 1), :]
+        pick = jnp.where((positions == listed) & (slots < count[first + image]), 1.0, 0.0)
         tokens[rows, :] = dot_tn(pick.astype(LOW), patch_rows[image]).astype(LOW)
         return carry
 
@@ -822,17 +921,21 @@
         image = image_at(turn)
         rows = pl.ds(pl.multiple_of(image * kept, kept), kept)
 
-        @pl.when(turn == images - 1)
+        @pl.when(turn == images - 2)
         def _():
             shares[0].pass_on()
             shares[1].pass_on()
+
+        @pl.when(turn == images - 1)
+        def _():
+            shares[1].relay()
 
         norm, _ = norm_parts(tokens[rows, :].astype(F32))
         normed = (norm * (1.0 + block(image, 1)) + block(image, 0)).astype(LOW)
         normed_out[rows, :] = normed
         key_live = lax.broadcasted_iota(jnp.int32, (1, kept), 1) < count[first + image]
         attended_out[0, rows, :] = attend_shard(
-            normed, qkv_own, qv_own, proj_out, 0, rows, key_live, scale
+            normed, heads_own, row_own, spots, proj_out, 0, rows, key_live, scale
         )
         return carry
 
@@ -841,36 +944,37 @@
         rows = pl.ds(pl.multiple_of(image * kept, kept), kept)
         key_live = lax.broadcasted_iota(jnp.int32, (1, kept), 1) < count[first + image]
         attended = attend_shard(
-            normed_out[rows, :], qkv_other, qv_other, proj_out, 1, rows, key_live, scale
+            normed_out[rows, :], heads_other, row_other, spots, proj_out, 1, rows, key_live, scale
         )
         attended_out[1, rows, :] = attended
-        branch = dot(attended_out[0, rows, :], out_own[...]) + dot(attended, out_other[...])
+        branch = dot(attended_out[0, rows, :], heads_own[3 * local :, :]) + dot(
+            attended, heads_other[3 * local :, :]
+        )
         terms[rows, :] = branch.astype(LOW)
         for part in range(fold):
             reduce.ready_share(image * fold + part)
         return carry
 
     lax.fori_loop(0, images, one, 0)
+    shares[1].wait()
+    lax.fori_loop(0, images, two, 0)
     shares[2].pass_on()
-    for member in shares[:3]:
-        member.wait()
-    lax.fori_loop(0, images, two, 0)
+    reduce.relay()
+    shares[2].relay()
     shares[3].pass_on()
-    shares[4].pass_on()
-    reduce.relay()
-    shares[5].pass_on()
     reduce.finish(total)
     image = (up * share) // kept
     own = tokens[pl.ds(pl.multiple_of(up * share, share), share), :]
     tokens_own[...] = own
-    branch = total[...] + out_bias[...].astype(F32)
+    branch = total[...] + row_own[:, spots["out"] : spots["out"] + width]
     branch_out[...] = branch
     mid = own.astype(F32) + block(image, 2) * branch
     mid_out[...] = mid
     norm, _ = norm_parts(mid)
     normed_two_out[...] = (norm * (1.0 + block(image, 4)) + block(image, 3)).astype(LOW)
+    shares[3].relay()
     reduce.close()
-    for member in shares[3:]:
+    for member in shares[2:]:
         member.wait()
     for step in range(1, groups):
         source = (group + groups - step) % groups
@@ -886,9 +990,10 @@
 
 def attend(sizes, groups, args):
     depth, images, kept, share, pieces = sizes
-    (count, index, patches, cond, mod_weight, mod_bias, qkv, qv, out, out_bias, up, down, up_bias) = args
+    count, index, patches, cond, mod_weight, heads, up, down, row = args
     spots, width = patches.shape[1:]
-    local = out.shape[0]
+    local = heads.shape[0] // 4
+    mods = mod_weight.shape[0]
     rows = images * kept
     shape = jax.ShapeDtypeStruct
     devices = depth * PAIR
@@ -902,25 +1007,23 @@
             shape((share, width), F32),
             shape((share, width), F32),
             shape((share, width), LOW),
-            shape((cond.shape[0], devices * mod_weight.shape[1]), F32),
+            shape((cond.shape[0], devices * mods), F32),
             shape((groups,) + cond.shape, LOW),
-            shape(qkv.shape, LOW),
-            shape(qv.shape, LOW),
-            shape(out.shape, LOW),
+            shape(heads.shape, LOW),
             shape(up.shape, LOW),
             shape(down.shape, LOW),
-            shape(up_bias.shape, LOW),
+            shape(row.shape, F32),
         ),
-        in_specs=[SM, VM, HB] + [VM] * 10,
-        out_specs=(VM,) * 15,
+        in_specs=[SM, VM, HB] + [VM] * 6,
+        out_specs=(VM,) * 13,
         scratch_shapes=[
             pltpu.VMEM((images, spots, width), LOW),
             pltpu.VMEM((rows, width), LOW),
             pltpu.VMEM((rows, width), LOW),
             pltpu.VMEM((rows - share, width), LOW),
             pltpu.VMEM((share, width), F32),
-            pltpu.VMEM((cond.shape[0], mod_weight.shape[1]), LOW),
-            pltpu.VMEM((devices, cond.shape[0], mod_weight.shape[1]), LOW),
+            pltpu.VMEM((cond.shape[0], mods), LOW),
+            pltpu.VMEM((devices, cond.shape[0], mods), LOW),
             DMA((images,)),
         ]
         + Reduce.scratch(depth, pieces)
@@ -929,11 +1032,8 @@
             DMA((devices,)),
             DMA((groups,)),
             DMA((groups,)),
-            DMA((6,)),
-            DMA((6,)),
-            DMA((6, groups)),
-            DMA((6, groups)),
-        ],
+        ]
+        + Share.scratch(4, groups),
         compiler_params=pltpu.CompilerParams(
             collective_id=1, has_side_effects=True, vmem_limit_bytes=60 << 20
         ),
@@ -949,11 +1049,10 @@
     mod,
     up_own,
     up_other,
-    up_bias_own,
-    up_bias_other,
+    row_own,
+    row_other,
     down_own,
     down_other,
-    down_bias,
     mid,
     branch,
     up_grad,
@@ -989,6 +1088,8 @@
     depth, images, kept, share, pieces = sizes
     me, up, side = place(depth)
     width = normed_own.shape[1]
+    units = up_own.shape[0]
+    spots, _ = row_spots(width, units, 1, 1)
     fold = depth // images
     first = side * images
     own_rows = pl.ds(pl.multiple_of(up * share, share), share)
@@ -1025,10 +1126,11 @@
         source = normed[rows, :]
         mlp = None
         back = None
-        for shard, (weight_up, bias, weight_down) in enumerate(
-            ((up_own, up_bias_own, down_own), (up_other, up_bias_other, down_other))
+        for shard, (weight_up, row, weight_down) in enumerate(
+            ((up_own, row_own, down_own), (up_other, row_other, down_other))
         ):
-            pre = dot(source, weight_up[...]) + bias[...].astype(F32)
+            bias = row[:, spots["up"] : spots["up"] + units]
+            pre = dot_nt(source, weight_up[...]) + bias
             square = pre * pre
             bent = jnp.tanh(GELU_ROOT * pre * (1.0 + GELU_CUBE * square))
             half = 0.5 * (1.0 + bent)
@@ -1041,13 +1143,14 @@
             grad_pre[shard, rows, :] = low_grad
             up_sums[shard, image] = jnp.sum(low_grad.astype(F32), axis=0, keepdims=True)
             mlp_part = dot(low_hidden, weight_down[...])
-            back_part = dot_nt(low_grad, weight_up[...])
+            back_part = dot(low_grad, weight_up[...])
             mlp = mlp_part if mlp is None else mlp + mlp_part
             back = back_part if back is None else back + back_part
         terms[rows, :] = back.astype(LOW)
         mlp_terms[rows, :] = mlp.astype(LOW)
         for part in range(fold):
             reduce.ready_share(image * fold + part)
+            mlp_reduce.ready_share(image * fold + part)
 
     if fold == 1:
 
@@ -1072,21 +1175,26 @@
         for offset in range(1, depth):
             gather.take(offset)
         lax.fori_loop(0, images, image_of, 0)
-    for offset in range(1, depth):
-        mlp_reduce.ready(depth - offset)
     reduce.relay()
+    mlp_reduce.relay()
+    wide = tile_of(width)
     for shard in range(PAIR):
 
         def tile(step, carry):
-            columns = pl.ds(pl.multiple_of(step * 128, 128), 128)
-            up_grad[shard, columns, :] = dot_tn(
-                normed[:, columns], grad_pre[shard]
+            columns = pl.ds(pl.multiple_of(step * wide, 128), wide)
+            up_grad[shard, 0:units, columns] = dot_tn(
+                grad_pre[shard], normed[:, columns]
             ).astype(LOW)
-            down_grad[shard, :, columns] = dot_tn(hidden[shard], grad_mlp[:, columns]).astype(LOW)
+            down_grad[shard, 0:units, columns] = dot_tn(
+                hidden[shard], grad_mlp[:, columns]
+            ).astype(LOW)
             return carry
 
-        lax.fori_loop(0, width // 128, tile, 0)
-    mlp_reduce.relay()
+        lax.fori_loop(0, width // wide, tile, 0)
+        if units < up_grad.shape[1]:
+            rest = jnp.zeros((up_grad.shape[1] - units, width), LOW)
+            up_grad[shard, units:, :] = rest
+            down_grad[shard, units:, :] = rest
     reduce.finish(total)
     for shard in range(PAIR):
         up_bias_grad[shard : shard + 1, :] = sum(up_sums[shard, image] for image in range(images))
@@ -1106,7 +1214,7 @@
     sums_out[1:2, :] = jnp.sum(back, axis=0, keepdims=True)
     sums_out[2:3, :] = jnp.sum(back * norm, axis=0, keepdims=True)
     mlp_reduce.finish(mlp_total)
-    mlp = mlp_total[...] + down_bias[...].astype(F32)
+    mlp = mlp_total[...] + row_own[:, spots["down"] : spots["down"] + width]
     sums_out[3:4, :] = jnp.sum(grad_out * mlp, axis=0, keepdims=True)
     block_own[...] = jnp.where(live, mid[...] + block(image, 5) * mlp, 0.0).astype(LOW)
     gather.close()
@@ -1114,17 +1222,17 @@
     mlp_reduce.close()
 
 
-def feed(sizes, args):
+def feed(sizes, groups, args):
     depth, images, kept, share, pieces = sizes
     width = args[1].shape[1]
-    units = args[4].shape[1]
+    units = args[4].shape[0]
     rows = images * kept
     shape = jax.ShapeDtypeStruct
     return pl.pallas_call(
         functools.partial(feed_kernel, sizes),
         out_shape=(
-            shape((PAIR, width, units), LOW),
-            shape((PAIR, units, width), LOW),
+            shape((PAIR, padded(units, groups), width), LOW),
+            shape((PAIR, padded(units, groups), width), LOW),
             shape((PAIR, units), F32),
             shape((1, width), F32),
             shape((share, width), LOW),
@@ -1132,7 +1240,7 @@
             shape((share, width), LOW),
             shape((4, width), F32),
         ),
-        in_specs=[SM, VM, HB] + [VM] * 10,
+        in_specs=[SM, VM, HB] + [VM] * 9,
         out_specs=(VM,) * 8,
         scratch_shapes=[
             pltpu.VMEM((rows, width), LOW),
@@ -1169,18 +1277,15 @@
     normed,
     proj,
     attended,
-    qkv_own,
-    qkv_other,
-    out_own,
-    out_other,
+    heads_own,
+    heads_other,
     mod,
     tokens_own,
     grad_mid,
     block_own,
     up_grad,
     down_grad,
-    qkv_grad,
-    out_grad,
+    heads_grad,
     qv_grad,
     out_bias_grad,
     grad_tokens,
@@ -1205,13 +1310,13 @@
     depth, images, kept, share, pieces = sizes
     me, up, side = place(depth)
     width = grad_own.shape[1]
-    local = out_own.shape[0]
+    local = heads_own.shape[0] // 4
     scale = HD ** (-0.5)
     fold = depth // images
     first = side * images
-    up_fold = Fold(up_grad, rest[:7], up_total, depth, groups, True)
-    down_fold = Fold(down_grad, rest[7:14], down_total, depth, groups, True)
-    spread = Spread(block_out, share, depth, pieces, rest[14:18])
+    up_fold = Fold(up_grad, rest[:8], up_total, depth, groups)
+    down_fold = Fold(down_grad, rest[8:16], down_total, depth, groups)
+    spread = Spread(block_out, share, depth, pieces, rest[16:20])
     own_rows = pl.ds(pl.multiple_of(up * share, share), share)
     own_copy = pltpu.make_async_copy(grad_own, grads.at[own_rows, :], own_sem.at[0])
     own_copy.start()
@@ -1232,8 +1337,8 @@
         grad = grads[rows, :]
         out_sums[image] = jnp.sum(grad.astype(F32), axis=0, keepdims=True)
         back = None
-        for shard, (qkv, out) in enumerate(((qkv_own, out_own), (qkv_other, out_other))):
-            grad_att = dot_nt(grad, out[...]).astype(LOW)
+        for shard, heads in enumerate((heads_own, heads_other)):
+            grad_att = dot_nt(grad, heads[3 * local :, :]).astype(LOW)
             queries = proj[shard, 0, rows, :]
             keys = proj[shard, 1, rows, :]
             values = proj[shard, 2, rows, :]
@@ -1254,7 +1359,7 @@
             for member, value in enumerate((grad_q * scale, grad_k * scale, grad_v)):
                 low = value.astype(LOW)
                 grad_proj[shard, member, rows, :] = low
-                part = dot_nt(low, qkv[member])
+                part = dot(low, heads[member * local : (member + 1) * local, :])
                 back = part if back is None else back + part
                 if member != 1:
                     row = 2 * shard + member // 2
@@ -1286,6 +1391,10 @@
             @pl.when(turn == 2)
             def _():
                 up_fold.three()
+
+            @pl.when(turn == 3)
+            def _():
+                down_fold.three()
 
             return carry
 
@@ -1304,6 +1413,7 @@
         spread.open()
         lax.fori_loop(0, images, image_of, 0)
         up_fold.three()
+        down_fold.three()
 
     def spread_of(turn, carry):
         spread.take(turn)
@@ -1311,24 +1421,31 @@
 
     reduce.relay()
     lax.fori_loop(1, depth - 1, spread_of, 0)
-    down_fold.three()
-    spread.take(depth - 1)
     up_fold.four()
+    down_fold.four()
+    wide = tile_of(width)
     for shard in range(PAIR):
 
         def tile(step, carry):
-            columns = pl.ds(pl.multiple_of(step * 128, 128), 128)
+            columns = pl.ds(pl.multiple_of(step * wide, 128), wide)
             source = normed[:, columns]
             for member in range(3):
-                start = member * width + step * 128
-                qkv_grad[shard, pl.ds(pl.multiple_of(start, 128), 128), :] = dot_tn(
-                    source, grad_proj[shard, member]
+                heads_grad[shard, member * local : (member + 1) * local, columns] = dot_tn(
+                    grad_proj[shard, member], source
                 ).astype(LOW)
-            out_grad[shard, :, columns] = dot_tn(attended[shard], grads[:, columns]).astype(LOW)
+            heads_grad[shard, 3 * local : 4 * local, columns] = dot_tn(
+                attended[shard], grads[:, columns]
+            ).astype(LOW)
             return carry
 
-        lax.fori_loop(0, width // 128, tile, 0)
-    down_fold.four()
+        lax.fori_loop(0, width // wide, tile, 0)
+        if 4 * local < heads_grad.shape[1]:
+            heads_grad[shard, 4 * local :, :] = jnp.zeros(
+                (heads_grad.shape[1] - 4 * local, width), LOW
+            )
+    up_fold.five()
+    spread.take(depth - 1)
+    down_fold.five()
     reduce.finish(total)
     for row in range(2 * PAIR):
         qv_grad[row : row + 1, :] = sum(qv_sums[row, image] for image in range(images))
@@ -1344,8 +1461,8 @@
     grad_tokens[...] = jnp.where(live, grad, 0.0).astype(LOW)
     sums_out[0:1, :] = jnp.sum(back, axis=0, keepdims=True)
     sums_out[1:2, :] = jnp.sum(back * norm, axis=0, keepdims=True)
-    up_fold.five()
-    down_fold.five()
+    up_fold.six()
+    down_fold.six()
     for index in range(depth):
         spread.crossed(index)
     spread.close()
@@ -1356,25 +1473,24 @@
 def attend_back(sizes, groups, args):
     depth, images, kept, share, pieces = sizes
     width = args[1].shape[1]
-    local = args[7].shape[0]
-    up_grad, down_grad = args[-2:]
+    local = args[5].shape[0] // 4
+    up_grad, down_grad, units = args[-3:]
     rows = images * kept
     shape = jax.ShapeDtypeStruct
     return pl.pallas_call(
         functools.partial(attend_back_kernel, sizes, groups),
         out_shape=(
-            shape((PAIR, 3 * width, local), LOW),
-            shape((PAIR, local, width), LOW),
+            shape((PAIR, padded(4 * local, groups), width), LOW),
             shape((2 * PAIR, local), F32),
             shape((1, width), F32),
             shape((share, width), LOW),
             shape((2, width), F32),
             shape((PAIR * rows, width), LOW),
-            shape(up_grad.shape[1:], F32),
-            shape(down_grad.shape[1:], F32),
+            shape((units, width), F32),
+            shape((units, width), F32),
         ),
-        in_specs=[SM] + [VM] * 14,
-        out_specs=(VM,) * 9,
+        in_specs=[SM] + [VM] * 12,
+        out_specs=(VM,) * 8,
         scratch_shapes=[
             pltpu.VMEM((rows, width), LOW),
             pltpu.VMEM((PAIR, 3, rows, local), LOW),
@@ -1387,14 +1503,14 @@
         ]
         + Gather.scratch(depth, pieces)
         + Reduce.scratch(depth, pieces)
-        + Fold.scratch(up_grad.shape, groups, True)
-        + Fold.scratch(down_grad.shape, groups, True)
+        + Fold.scratch(up_grad.shape, groups)
+        + Fold.scratch(down_grad.shape, groups)
         + Spread.scratch(depth, pieces),
         compiler_params=pltpu.CompilerParams(
             collective_id=3, has_side_effects=True, vmem_limit_bytes=62 << 20
         ),
         name="attend_back",
-    )(*args)
+    )(*args[:-1])
 
 
 def split_low(value):
@@ -1409,21 +1525,24 @@
     groups,
     index,
     grad_tokens,
-    sums,
-    biases,
-    qkv_grad,
-    out_grad,
+    sums_one,
+    sums_two,
+    up_bias_grad,
+    qv_grad,
+    down_bias_grad,
+    out_bias_grad,
+    heads_grad,
     silu_all,
     mod_weight,
     cond,
     grad_patches,
-    qkv_total,
-    out_total,
+    heads_total,
     bias_total,
     mod_weight_grad,
     mod_bias_grad,
     grad_cond,
     whole,
+    biases,
     sum_row,
     sum_land,
     bias_land,
@@ -1440,15 +1559,15 @@
     depth, images, kept, share, pieces = sizes
     devices = depth * PAIR
     everyone = devices * groups
-    me, up, side = place(depth)
+    me, _, side = place(depth)
+    up = me // PAIR
     group = lax.axis_index("dp")
     flat = group * devices + me
     width = grad_tokens.shape[1]
-    columns = mod_weight.shape[1]
+    columns = mod_weight.shape[0]
     span = sum_land.shape[2]
     spread = Spread(whole, share, depth, pieces, rest[:4])
-    qkv_fold = Fold(qkv_grad, rest[4:11], qkv_total, depth, groups, True)
-    out_fold = Fold(out_grad, rest[11:18], out_total, depth, groups, False)
+    fold = Fold(heads_grad, rest[4:12], heads_total, depth, groups)
     own_copy = pltpu.make_async_copy(grad_tokens, spread.own(), own_sem)
     own_copy.start()
     barrier = pltpu.get_barrier_semaphore()
@@ -1466,15 +1585,15 @@
     lax.fori_loop(1, everyone, greet, 0)
     pl.semaphore_wait(barrier, everyone - 1)
     own_copy.wait()
+    fold.one()
     spread.open()
-    qkv_fold.one()
-    out_fold.one()
 
     def aligned(device):
         return pl.multiple_of((device * columns) // 128 * 128, 128)
 
     for member in range(6):
-        sum_row[:, member * width : (member + 1) * width] = sums[member : member + 1, :]
+        part = sums_one[member : member + 1, :] if member < 2 else sums_two[member - 2 : member - 1, :]
+        sum_row[:, member * width : (member + 1) * width] = part
     sum_row[:, 6 * width :] = jnp.zeros((1, sum_row.shape[1] - 6 * width), F32)
 
     def sum_copy(step):
@@ -1495,6 +1614,13 @@
 
     lax.fori_loop(1, everyone, send_sum, 0)
     sum_land[flat] = sum_row[:, pl.ds(aligned(me), span)]
+    units, local = up_bias_grad.shape[1], qv_grad.shape[1]
+    biases[...] = jnp.zeros(biases.shape, F32)
+    for shard in range(PAIR):
+        biases[3 * shard : 3 * shard + 1, 0:units] = up_bias_grad[shard : shard + 1, :]
+        biases[3 * shard + 1 : 3 * shard + 3, 0:local] = qv_grad[2 * shard : 2 * shard + 2, :]
+    biases[6:7, :] = down_bias_grad[...]
+    biases[7:8, :] = out_bias_grad[...]
     slot = side * groups + group
     bias_land[slot] = biases[...]
     partner = me + depth * (1 - 2 * side)
@@ -1509,8 +1635,7 @@
 
     for step in range(1, PAIR * groups):
         bias_copy(step).start()
-    qkv_fold.two()
-    out_fold.two()
+    fold.two()
 
     def wait_sum(step, carry):
         source = (flat + everyone - step) % everyone
@@ -1540,8 +1665,9 @@
     ).astype(LOW)
     parts = split_low(grads)
     spread.take(1)
+    fold.three()
     mod_weight_grad[...] = (
-        dot_tn(silu_rows, parts[0]) + dot_tn(silu_rows, parts[1]) + dot_tn(silu_rows, parts[2])
+        dot_tn(parts[0], silu_rows) + dot_tn(parts[1], silu_rows) + dot_tn(parts[2], silu_rows)
     )
     source = lax.broadcasted_iota(jnp.int32, (total_images, everyone), 1)
     target = lax.broadcasted_iota(jnp.int32, (total_images, everyone), 0)
@@ -1551,9 +1677,9 @@
     mine = dot(chosen, parts[0]) + dot(chosen, parts[1]) + dot(chosen, parts[2])
     parts = split_low(mine)
     term = (
-        dot_nt(parts[0], mod_weight[...])
-        + dot_nt(parts[1], mod_weight[...])
-        + dot_nt(parts[2], mod_weight[...])
+        dot(parts[0], mod_weight[...])
+        + dot(parts[1], mod_weight[...])
+        + dot(parts[2], mod_weight[...])
     )
     cond_land[me] = term
 
@@ -1568,10 +1694,9 @@
 
     for step in range(1, devices):
         cond_copy(step).start()
-    qkv_fold.three()
-    out_fold.three()
-    for turn in range(2, depth):
+    for turn in range(2, depth - 1):
         spread.take(turn)
+    fold.four()
     for step in range(1, PAIR * groups):
         crossed = step // groups
         source_group = (group + groups - step % groups) % groups
@@ -1596,25 +1721,30 @@
     value = cond[...].astype(F32)
     gate = 1.0 / (1.0 + jnp.exp(-value))
     grad_cond[...] = (back * (gate + value * gate * (1.0 - gate))).astype(LOW)
-    qkv_fold.four()
-    out_fold.four()
 
     def place_image(image):
         rows = pl.ds(pl.multiple_of(image * kept, kept), kept)
-        spots = lax.broadcasted_iota(jnp.int32, (grad_patches.shape[1], kept), 0)
-        pick = jnp.where(spots == index[image], 1.0, 0.0).astype(LOW)
+        positions = lax.broadcasted_iota(jnp.int32, (grad_patches.shape[1], kept), 0)
+        pick = jnp.where(positions == index[pl.ds(image, 1), :], 1.0, 0.0).astype(LOW)
         grad_patches[image] = dot(pick, whole[rows, :]).astype(LOW)
 
-    for index_of in range(depth):
-        spread.crossed(index_of)
-
-    def put(image, carry):
-        place_image(image)
+    both = PAIR * share // kept
+
+    def put(where):
+        spread.crossed(where)
+        for image in range(both):
+            place_image(where * both + image)
+
+    def arrived(turn, carry):
+        put(spread.line.arrival(turn)[2])
         return carry
 
-    lax.fori_loop(0, PAIR * images, put, 0)
-    qkv_fold.five()
-    out_fold.five()
+    put(up)
+    lax.fori_loop(1, depth - 1, arrived, 0)
+    spread.take(depth - 1)
+    fold.five()
+    put(spread.line.arrival(depth - 1)[2])
+    fold.six()
     spread.close()
 
     def done_sum(step, carry):
@@ -1630,10 +1760,12 @@
 
 def close(sizes, groups, args):
     depth, images, kept, share, pieces = sizes
-    index, grad_tokens, sums, biases, qkv_grad, out_grad, silu_all, mod_weight, cond, spots = args
+    index, grad_tokens = args[:2]
+    heads_grad, silu_all, mod_weight, cond, local, spots = args[-6:]
     devices = depth * PAIR
     width = grad_tokens.shape[1]
-    columns = mod_weight.shape[1]
+    columns = mod_weight.shape[0]
+    biases = (8, width)
     span = max(-(-((device * columns) % 128 + columns) // 128) * 128 for device in range(devices))
     long = max((device * columns) // 128 * 128 + span for device in range(devices))
     long = max(long, 6 * width + 128)
@@ -1644,20 +1776,20 @@
         functools.partial(close_kernel, sizes, groups),
         out_shape=(
             shape((PAIR * images, spots, width), LOW),
-            shape(qkv_grad.shape[1:], F32),
-            shape(out_grad.shape[1:], F32),
-            shape(biases.shape, F32),
+            shape((4 * local, width), F32),
+            shape(biases, F32),
             shape(mod_weight.shape, F32),
             shape((1, columns), F32),
             shape(cond.shape, LOW),
         ),
-        in_specs=[VM] * 9,
-        out_specs=(VM,) * 7,
+        in_specs=[VM] * 12,
+        out_specs=(VM,) * 6,
         scratch_shapes=[
             pltpu.VMEM((rows, width), LOW),
+            pltpu.VMEM(biases, F32),
             pltpu.VMEM((1, long), F32),
             pltpu.VMEM((everyone, 1, span), F32),
-            pltpu.VMEM((PAIR * groups,) + biases.shape, F32),
+            pltpu.VMEM((PAIR * groups,) + biases, F32),
             pltpu.VMEM((devices,) + cond.shape, F32),
             DMA,
             DMA((everyone,)),
@@ -1668,13 +1800,12 @@
             DMA((devices,)),
         ]
         + Spread.scratch(depth, pieces)
-        + Fold.scratch(qkv_grad.shape, groups, True)
-        + Fold.scratch(out_grad.shape, groups, False),
+        + Fold.scratch(heads_grad.shape, groups),
         compiler_params=pltpu.CompilerParams(
             collective_id=4, has_side_effects=True, vmem_limit_bytes=62 << 20
         ),
         name="close",
-    )(*args[:-1])
+    )(*args[:-2])
 
 
 def on_device(
@@ -1703,9 +1834,22 @@
     pieces = 4 if share % 64 == 0 else 2
     sizes = (depth, images, kept, share, pieces)
     groups = lax.axis_size("dp")
-    index = keep_index[:, None, :]
-    qkv_local, units = qkv_weight.shape[2], up_weight.shape[1]
-    up_bias_row = up_bias[None, :]
+    local, units, mods = qkv_weight.shape[2], up_weight.shape[1], mod_weight.shape[1]
+    up = up_weight.T
+    mod_rows = mod_weight.T
+    heads = jnp.concatenate(
+        [jnp.swapaxes(qkv_weight, 1, 2).reshape(3 * local, width), out_weight], axis=0
+    )
+
+    def spaced(value):
+        return jnp.pad(value.astype(F32), (0, lanes(value.shape[0]) - value.shape[0]))
+
+    row = jnp.concatenate(
+        [
+            spaced(value)
+            for value in (out_bias, down_bias, up_bias, qv_bias[0], qv_bias[1], mod_bias)
+        ]
+    )[None, :]
     (
         normed_one,
         proj,
@@ -1716,30 +1860,14 @@
         normed_two,
         mod,
         silu_all,
-        qkv_other,
-        qv_other,
-        out_other,
+        heads_other,
         up_other,
         down_other,
-        up_bias_other,
+        row_other,
     ) = attend(
         sizes,
         groups,
-        (
-            keep_count,
-            index,
-            patches,
-            conditioning,
-            mod_weight,
-            mod_bias[None, :],
-            qkv_weight,
-            qv_bias,
-            out_weight,
-            out_bias[None, :],
-            up_weight,
-            down_weight,
-            up_bias_row,
-        ),
+        (keep_count, keep_index, patches, conditioning, mod_rows, heads, up, down_weight, row),
     )
     (
         up_grad,
@@ -1752,25 +1880,24 @@
         sums_two,
     ) = feed(
         sizes,
+        groups,
         (
             keep_count,
             normed_two,
             out_cotangent,
             mod,
-            up_weight,
+            up,
             up_other,
-            up_bias_row,
-            up_bias_other,
+            row,
+            row_other,
             down_weight,
             down_other,
-            down_bias[None, :],
             mid,
             branch,
         ),
     )
     (
-        qkv_grad,
-        out_grad,
+        heads_grad,
         qv_grad,
         out_bias_grad,
         grad_tokens,
@@ -1787,54 +1914,41 @@
             normed_one,
             proj,
             attended,
-            qkv_weight,
-            qkv_other,
-            out_weight,
-            out_other,
+            heads,
+            heads_other,
             mod,
             tokens_own,
             grad_mid,
             block_own,
             up_grad,
             down_grad,
+            units,
         ),
     )
-
-    def row(value):
-        return jnp.pad(value, ((0, 0), (0, width - value.shape[1])))
-
-    biases = jnp.concatenate(
-        [
-            row(up_bias_grad[0:1]),
-            row(qv_grad[0:2]),
-            row(up_bias_grad[1:2]),
-            row(qv_grad[2:4]),
-            down_bias_grad,
-            out_bias_grad,
-        ]
-    )
-    sums = jnp.concatenate([sums_one, sums_two])
     (
         grad_patches,
-        qkv_total,
-        out_total,
+        heads_total,
         bias_total,
-        mod_weight_grad,
+        mod_rows_grad,
         mod_bias_grad,
         grad_conditioning,
     ) = close(
         sizes,
         groups,
         (
-            index,
+            keep_index,
             grad_tokens,
-            sums,
-            biases,
-            qkv_grad,
-            out_grad,
+            sums_one,
+            sums_two,
+            up_bias_grad,
+            qv_grad,
+            down_bias_grad,
+            out_bias_grad,
+            heads_grad,
             silu_all,
-            mod_weight,
+            mod_rows,
             conditioning,
+            local,
             patches.shape[1],
         ),
     )
@@ -1842,13 +1956,13 @@
         block_out.reshape(all_images, kept, width),
         grad_patches,
         grad_conditioning,
-        mod_weight_grad,
+        mod_rows_grad.T,
         mod_bias_grad[0],
-        qkv_total.reshape(qkv_weight.shape),
-        bias_total[1:3, :qkv_local],
-        out_total,
+        jnp.swapaxes(heads_total[: 3 * local].reshape(3, local, width), 1, 2),
+        bias_total[1:3, :local],
+        heads_total[3 * local :],
         bias_total[7],
-        up_total,
+        up_total.T,
         bias_total[0, :units],
         down_total,
         bias_total[6],

time: 455 us -> 350 us (0.77)
  Pallas kernels: 410 us -> 315 us
  local copies, waits for them, and re-layouts: 41.2 us -> 29.4 us
    pallas_call x1, Pallas kernels: 118 us -> 76.4 us  [close(): pl.pallas_call(functools.partial(close_kernel, sizes, groups), out_shape=...]
    pallas_call x1, Pallas kernels: 126 us -> 95.8 us  [attend_back(): pl.pallas_call(functools.partial(attend_back_kernel, sizes, groups), out_...]
    pallas_call x1, Pallas kernels: 108 us -> 83.4 us  [attend(): pl.pallas_call(functools.partial(attend_kernel, sizes, groups), out_shape...]
    unnamed x31 -> x23, local copies, waits for them, and re-layouts: 28.5 us -> 17.2 us
    broadcast_in_dim x5 -> x1, local copies, waits for them, and re-layouts: 6.48 us -> 0.62 us  [on_device(): jnp.concatenate([spaced(value) for value in (out_bias, down_bias, up_bias...]
    slice x3 -> x4, local copies, waits for them, and re-layouts: 2.04 us -> 7.13 us  [the longest x1 2.96 us: on_device(): heads_total[:3 * local].reshape(3, local, width)]
where the time goes in v4:
time: 350 us; the launch traced here: 349 us
  Pallas kernels  315 us (90%)
  local copies, waits for them, and re-layouts  29.4 us (8%)
  other arithmetic  3.76 us (1%)
    pallas_call x1, Pallas kernels, attend_back(): pl.pallas_call(functools.partial(attend_back_kernel, sizes, groups), out_...  95.8 us
    pallas_call x1, Pallas kernels, attend(): pl.pallas_call(functools.partial(attend_kernel, sizes, groups), out_shape...  83.4 us
    pallas_call x1, Pallas kernels, close(): pl.pallas_call(functools.partial(close_kernel, sizes, groups), out_shape=...  76.4 us
    pallas_call x1, Pallas kernels, feed(): pl.pallas_call(functools.partial(feed_kernel, sizes), out_shape=(shape((P...  59.6 us
    unnamed x23, local copies, waits for them, and re-layouts  17.2 us

profile of v4, /device:TPU:0, one launch (start us, length us, event | category | flops | bytes accessed | tf_op | source)
XLA Modules:
  0.0 349.0 jit_solution(11543287763929836005)
XLA Ops:
  0.6 0.8 slice_reduce_fusion.3
  1.4 0.7 pad.22
  2.1 0.7 pad.19
  2.8 0.9 dynamic-update-slice
  3.7 0.9 dynamic-update-slice.1
  4.6 0.2 dynamic-update-slice.2
  4.8 0.2 dynamic-update-slice.3
  5.0 0.2 dynamic-update-slice.4
  5.2 0.2 dynamic-update-slice.5
  5.4 0.6 reshape.42.row_own
  6.0 2.5 pad_maximum_fusion.heads_own
  8.5 83.4 %attend.1 = (bf16[768,1152]{1,0:T(8,128)(2,1)}, bf16[2,3,768,144]{3,2,1,0:T(8,128)(2,1)}, bf16[2,768,144]{2,1,0:T(8,128)(2,1)}, bf16[192,1152]{1,0:T(8,128)(2,1)...) custom-call(s32[8]{0:T(128)} %count.5, ...), custom_call_target="tpu_custom_call" | custom-call | tf_op jit(solution)/shard_map/attend/pallas_call | solution.py:1000
  91.9 59.6 %feed.1 = (bf16[2,576,1152]{2,1,0:T(8,128)(2,1)}, bf16[2,576,1152]{2,1,0:T(8,128)(2,1)}, f32[2,576]{1,0:T(2,128)}, f32[1,1152]{1,0:T(1,128)}, bf16[192,1152]{1,0...) custom-call(s32[8]{0:T(128)} %count.5, ...), custom_call_target="tpu_custom_call" | custom-call | tf_op jit(solution)/shard_map/feed/pallas_call | solution.py:1231
  151.5 95.8 %attend_back.1 = (bf16[2,576,1152]{2,1,0:T(8,128)(2,1)}, f32[4,144]{1,0:T(4,128)}, f32[1,1152]{1,0:T(1,128)}, bf16[192,1152]{1,0:T(8,128)(2,1)}, f32[2,1152]{1,0...) custom-call(s32[8]{0:T(128)} %count.5, ...), custom_call_target="tpu_custom_call" | custom-call | tf_op jit(solution)/shard_map/attend_back/pallas_call | solution.py:1480
  247.3 76.4 %close.1 = (bf16[8,256,1152]{2,1,0:T(8,128)(2,1)}, f32[576,1152]{1,0:T(8,128)}, f32[8,1152]{1,0:T(8,128)}, f32[864,1152]{1,0:T(8,128)}, f32[1,864]{1,0:T(1,128)}, /*index=5*/bf16[8,1152]{1,0:T(8,128)(2,1)}) custom-call(s32[8,192]{1,0:T(8,128)} %index.3, bf16[192,1152]{1,0:T(8,128)(2,1)} %get-tuple-element.66.grad_tokens, ...), custom_call_target="tpu_custom_call" | custom-call | tf_op jit(solution)/shard_map/close/pallas_call | solution.py:1775
  323.7 1.3 slice.27
  325.0 1.3 reduce.2
  326.3 1.3 slice_reduce_fusion.2
  327.6 1.5 slice_reduce_fusion
  329.1 2.1 slice.28
  331.2 3.0 slice.26
  334.2 0.0 copy-done.2
  334.2 1.8 copy.40
  336.0 1.8 copy-done
  337.8 2.4 copy.41
  340.2 0.6 copy.42
  340.8 0.8 copy-done.1
  341.6 2.0 copy.43
  343.7 1.2 copy-done.4
  344.8 1.5 copy.44
  346.3 1.2 copy-done.3
  347.5 1.5 copy.45
  (10 shorter events, 0.0 us)
Async XLA Ops:
  329.1 5.1 %copy-start.2 = (bf16[1536,1152]{1,0:T(8,128)(2,1)S(1)}, bf16[1536,1152]{1,0:T(8,128)(2,1)}, u32[]{:S(2)}) copy-start(bf16[1536,1152]{1,0:T(8,128)(2,1)} %get-tuple-element.65) | copy-start | bytes 10616836
  334.2 3.6 %copy-start = (bf16[8,256,1152]{2,1,0:T(8,128)(2,1)S(1)}, bf16[8,256,1152]{2,1,0:T(8,128)(2,1)}, u32[]{:S(2)}) copy-start(bf16[8,256,1152]{2,1,0:T(8,128)(2,1)} %get-tuple-element.101) | copy-start | bytes 14155780
  337.8 2.4 copy-start.5
  337.8 3.9 %copy-start.1 = (f32[864,1152]{1,0:T(8,128)S(1)}, f32[864,1152]{1,0:T(8,128)}, u32[]{:S(2)}) copy-start(f32[864,1152]{1,0:T(8,128)} %get-tuple-element.77) | copy-start | bytes 11943940
  341.6 3.2 copy-start.4
  344.8 2.7 copy-start.3

commit v5 on v4

--- a/solution.py
+++ b/solution.py
@@ -778,12 +778,13 @@
     return attended.astype(LOW)
 
 
-def attend_kernel(
+def ahead_kernel(
     sizes,
     groups,
     count,
     index,
     patches,
+    cotangent,
     cond,
     mod_weight,
     heads_own,
@@ -794,15 +795,22 @@
     proj_out,
     attended_out,
     tokens_own,
-    mid_out,
-    branch_out,
-    normed_two_out,
     mod,
     silu_all,
     heads_other,
+    up_grad,
+    down_grad,
+    up_bias_grad,
+    down_bias_grad,
+    block_own,
+    grad_mid_out,
+    grad_branch_out,
+    sums_out,
     up_other,
     down_other,
     row_other,
+    mid_out,
+    branch_out,
     patch_rows,
     tokens,
     terms,
@@ -819,6 +827,7 @@
     silu_recv,
     weight_send,
     weight_recv,
+    *rest,
 ):
     depth, images, kept, share, pieces = sizes
     devices = depth * PAIR
@@ -839,6 +848,39 @@
 
     def image_at(turn):
         return across(up // fold, images - 1 - turn, images)
+
+    (
+        normed_two,
+        cot,
+        hidden,
+        grad_pre,
+        grad_mlp,
+        back_terms,
+        back_landing,
+        mlp_terms,
+        mlp_landing,
+        back_part,
+        mlp_part,
+        back_total,
+        mlp_total,
+        up_sums,
+        down_sums,
+        cot_sem,
+        gather_send,
+        gather_recv,
+        back_send,
+        back_recv,
+        mlp_send,
+        mlp_recv,
+    ) = rest
+    units = up_own.shape[0]
+
+    def fetch_cotangent(image):
+        return pltpu.make_async_copy(
+            cotangent.at[first + image],
+            cot.at[pl.ds(pl.multiple_of(image * kept, kept), kept), :],
+            cot_sem.at[image],
+        )
 
     for turn in range(images):
         fetch(image_at(turn)).start()
@@ -889,9 +931,21 @@
             )
         )
     ]
-    for member in shares:
-        member.start()
+    outer = up // (depth // PAIR) == side
+    shares[0].start()
+    shares[1].start()
+
+    @pl.when(jnp.logical_not(outer))
+    def _():
+        shares[2].start()
+        shares[3].start()
+
+    for image in range(images):
+        fetch_cotangent(image).start()
     reduce = Reduce(terms, landing, share, depth, pieces, send, recv)
+    gather = Gather(normed_two, share, depth, pieces, gather_send, gather_recv)
+    back_reduce = Reduce(back_terms, back_landing, share, depth, pieces, back_send, back_recv)
+    mlp_reduce = Reduce(mlp_terms, mlp_landing, share, depth, pieces, mlp_send, mlp_recv)
 
     def pick_rows(turn, carry):
         image = image_at(turn)
@@ -921,14 +975,10 @@
         image = image_at(turn)
         rows = pl.ds(pl.multiple_of(image * kept, kept), kept)
 
-        @pl.when(turn == images - 2)
+        @pl.when(turn == images - 1)
         def _():
             shares[0].pass_on()
             shares[1].pass_on()
-
-        @pl.when(turn == images - 1)
-        def _():
-            shares[1].relay()
 
         norm, _ = norm_parts(tokens[rows, :].astype(F32))
         normed = (norm * (1.0 + block(image, 1)) + block(image, 0)).astype(LOW)
@@ -956,26 +1006,151 @@
         return carry
 
     lax.fori_loop(0, images, one, 0)
+    shares[1].relay()
     shares[1].wait()
     lax.fori_loop(0, images, two, 0)
+
+    @pl.when(outer)
+    def _():
+        shares[2].start()
+        shares[3].start()
+
+    reduce.relay()
     shares[2].pass_on()
-    reduce.relay()
-    shares[2].relay()
-    shares[3].pass_on()
     reduce.finish(total)
     image = (up * share) // kept
-    own = tokens[pl.ds(pl.multiple_of(up * share, share), share), :]
+    own_rows = pl.ds(pl.multiple_of(up * share, share), share)
+    own = tokens[own_rows, :]
     tokens_own[...] = own
     branch = total[...] + row_own[:, spots["out"] : spots["out"] + width]
     branch_out[...] = branch
     mid = own.astype(F32) + block(image, 2) * branch
     mid_out[...] = mid
     norm, _ = norm_parts(mid)
-    normed_two_out[...] = (norm * (1.0 + block(image, 4)) + block(image, 3)).astype(LOW)
+    normed_two[own_rows, :] = (norm * (1.0 + block(image, 4)) + block(image, 3)).astype(LOW)
+    shares[2].relay()
+    gather.open()
+
+    def half_pass(rows, shard, weight_up, row, weight_down):
+        source = normed_two[rows, :]
+        grad = grad_mlp[rows, :]
+        bias = row[:, spots["up"] : spots["up"] + units]
+        pre = dot_nt(source, weight_up[...]) + bias
+        square = pre * pre
+        bent = jnp.tanh(GELU_ROOT * pre * (1.0 + GELU_CUBE * square))
+        half = 0.5 * (1.0 + bent)
+        low_hidden = (pre * half).astype(LOW)
+        hidden[shard, rows, :] = low_hidden
+        slope = half + 0.5 * pre * (1.0 - bent * bent) * (
+            GELU_ROOT * (1.0 + 3.0 * GELU_CUBE * square)
+        )
+        low_grad = (slope * dot_nt(grad, weight_down[...])).astype(LOW)
+        grad_pre[shard, rows, :] = low_grad
+        sums = jnp.sum(low_grad.astype(F32), axis=0, keepdims=True)
+        return dot(low_hidden, weight_down[...]), dot(low_grad, weight_up[...]), sums
+
+    def own_pass(image):
+        fetch_cotangent(image).wait()
+        rows = pl.ds(pl.multiple_of(image * kept, kept), kept)
+        live = lax.broadcasted_iota(jnp.int32, (kept, 1), 0) < count[first + image]
+        grad = jnp.where(live, cot[rows, :].astype(F32), 0.0)
+        grad = (block(image, 5) * grad).astype(LOW)
+        grad_mlp[rows, :] = grad
+        down_sums[image] = jnp.sum(grad.astype(F32), axis=0, keepdims=True)
+        mlp, back, sums = half_pass(rows, 0, up_own, row_own, down_own)
+        up_sums[0, image] = sums
+        mlp_part[rows, :] = mlp
+        back_part[rows, :] = back
+
+    def other_pass(image):
+        rows = pl.ds(pl.multiple_of(image * kept, kept), kept)
+        mlp, back, sums = half_pass(rows, 1, up_other, row_other, down_other)
+        up_sums[1, image] = sums
+        back_terms[rows, :] = (back_part[rows, :] + back).astype(LOW)
+        mlp_terms[rows, :] = (mlp_part[rows, :] + mlp).astype(LOW)
+        for part in range(fold):
+            back_reduce.ready_share(image * fold + part)
+            mlp_reduce.ready_share(image * fold + part)
+
+    if fold == 1:
+
+        def own_turn(turn, carry):
+            @pl.when(turn == 1)
+            def _():
+                gather.relay()
+
+            offset = turn + (turn // 2) * (1 - 2 * (turn % 2))
+            gather.take(offset)
+            own_pass(across(up, offset, depth))
+
+            @pl.when(turn == 1)
+            def _():
+                shares[3].pass_on()
+
+            return carry
+
+        lax.fori_loop(0, depth, own_turn, 0)
+    else:
+
+        def own_image(image, carry):
+            own_pass(image)
+            return carry
+
+        gather.relay()
+        for offset in range(1, depth):
+            gather.take(offset)
+        shares[3].pass_on()
+        lax.fori_loop(0, images, own_image, 0)
     shares[3].relay()
-    reduce.close()
     for member in shares[2:]:
         member.wait()
+
+    def other_turn(turn, carry):
+        other_pass(image_at(turn))
+        return carry
+
+    lax.fori_loop(0, images, other_turn, 0)
+    back_reduce.relay()
+    mlp_reduce.relay()
+    wide = tile_of(width)
+    for shard in range(PAIR):
+
+        def tile(step, carry):
+            columns = pl.ds(pl.multiple_of(step * wide, 128), wide)
+            up_grad[shard, 0:units, columns] = dot_tn(
+                grad_pre[shard], normed_two[:, columns]
+            ).astype(LOW)
+            down_grad[shard, 0:units, columns] = dot_tn(
+                hidden[shard], grad_mlp[:, columns]
+            ).astype(LOW)
+            return carry
+
+        lax.fori_loop(0, width // wide, tile, 0)
+        if units < up_grad.shape[1]:
+            rest_rows = jnp.zeros((up_grad.shape[1] - units, width), LOW)
+            up_grad[shard, units:, :] = rest_rows
+            down_grad[shard, units:, :] = rest_rows
+    back_reduce.finish(back_total)
+    for shard in range(PAIR):
+        up_bias_grad[shard : shard + 1, :] = sum(up_sums[shard, member] for member in range(images))
+    down_bias_grad[...] = sum(down_sums[member] for member in range(images))
+    live = (
+        lax.broadcasted_iota(jnp.int32, (share, 1), 0) + (up * share) % kept
+        < count[first + image]
+    )
+    grad_out = jnp.where(live, cot[own_rows, :].astype(F32), 0.0)
+    norm, spread = norm_parts(mid_out[...])
+    back = back_total[...]
+    grad_mid = grad_out + norm_back(norm, spread, back * (1.0 + block(image, 4)))
+    grad_mid_out[...] = grad_mid
+    grad_branch_out[...] = (block(image, 2) * grad_mid).astype(LOW)
+    sums_out[0:1, :] = jnp.sum(grad_mid * branch_out[...], axis=0, keepdims=True)
+    sums_out[1:2, :] = jnp.sum(back, axis=0, keepdims=True)
+    sums_out[2:3, :] = jnp.sum(back * norm, axis=0, keepdims=True)
+    mlp_reduce.finish(mlp_total)
+    mlp = mlp_total[...] + row_own[:, spots["down"] : spots["down"] + width]
+    sums_out[3:4, :] = jnp.sum(grad_out * mlp, axis=0, keepdims=True)
+    block_own[...] = jnp.where(live, mid_out[...] + block(image, 5) * mlp, 0.0).astype(LOW)
     for step in range(1, groups):
         source = (group + groups - step) % groups
         view = silu_all.at[source]
@@ -986,37 +1161,49 @@
         member.close()
     for copy in mod_copies + silu_copies:
         copy.wait_send()
-
-
-def attend(sizes, groups, args):
+    reduce.close()
+    gather.close()
+    back_reduce.close()
+    mlp_reduce.close()
+
+
+def ahead(sizes, groups, args):
     depth, images, kept, share, pieces = sizes
-    count, index, patches, cond, mod_weight, heads, up, down, row = args
+    count, index, patches, cotangent, cond, mod_weight, heads, up, down, row = args
     spots, width = patches.shape[1:]
     local = heads.shape[0] // 4
     mods = mod_weight.shape[0]
+    units = up.shape[0]
     rows = images * kept
     shape = jax.ShapeDtypeStruct
     devices = depth * PAIR
     return pl.pallas_call(
-        functools.partial(attend_kernel, sizes, groups),
+        functools.partial(ahead_kernel, sizes, groups),
         out_shape=(
             shape((rows, width), LOW),
             shape((PAIR, 3, rows, local), LOW),
             shape((PAIR, rows, local), LOW),
             shape((share, width), LOW),
-            shape((share, width), F32),
-            shape((share, width), F32),
-            shape((share, width), LOW),
             shape((cond.shape[0], devices * mods), F32),
             shape((groups,) + cond.shape, LOW),
             shape(heads.shape, LOW),
-            shape(up.shape, LOW),
-            shape(down.shape, LOW),
-            shape(row.shape, F32),
+            shape((PAIR, padded(units, groups), width), LOW),
+            shape((PAIR, padded(units, groups), width), LOW),
+            shape((PAIR, units), F32),
+            shape((1, width), F32),
+            shape((share, width), LOW),
+            shape((share, width), F32),
+            shape((share, width), LOW),
+            shape((4, width), F32),
         ),
-        in_specs=[SM, VM, HB] + [VM] * 6,
-        out_specs=(VM,) * 13,
+        in_specs=[SM, VM, HB, HB] + [VM] * 6,
+        out_specs=(VM,) * 15,
         scratch_shapes=[
+            pltpu.VMEM(up.shape, LOW),
+            pltpu.VMEM(down.shape, LOW),
+            pltpu.VMEM(row.shape, F32),
+            pltpu.VMEM((share, width), F32),
+            pltpu.VMEM((share, width), F32),
             pltpu.VMEM((images, spots, width), LOW),
             pltpu.VMEM((rows, width), LOW),
             pltpu.VMEM((rows, width), LOW),
@@ -1033,216 +1220,8 @@
             DMA((groups,)),
             DMA((groups,)),
         ]
-        + Share.scratch(4, groups),
-        compiler_params=pltpu.CompilerParams(
-            collective_id=1, has_side_effects=True, vmem_limit_bytes=60 << 20
-        ),
-        name="attend",
-    )(*args)
-
-
-def feed_kernel(
-    sizes,
-    count,
-    normed_own,
-    cotangent,
-    mod,
-    up_own,
-    up_other,
-    row_own,
-    row_other,
-    down_own,
-    down_other,
-    mid,
-    branch,
-    up_grad,
-    down_grad,
-    up_bias_grad,
-    down_bias_grad,
-    block_own,
-    grad_mid_out,
-    grad_branch_out,
-    sums_out,
-    normed,
-    cot,
-    hidden,
-    grad_pre,
-    grad_mlp,
-    terms,
-    landing,
-    mlp_terms,
-    mlp_landing,
-    total,
-    mlp_total,
-    up_sums,
-    down_sums,
-    cot_sem,
-    own_sem,
-    gather_send,
-    gather_recv,
-    send,
-    recv,
-    mlp_send,
-    mlp_recv,
-):
-    depth, images, kept, share, pieces = sizes
-    me, up, side = place(depth)
-    width = normed_own.shape[1]
-    units = up_own.shape[0]
-    spots, _ = row_spots(width, units, 1, 1)
-    fold = depth // images
-    first = side * images
-    own_rows = pl.ds(pl.multiple_of(up * share, share), share)
-    own_copy = pltpu.make_async_copy(normed_own, normed.at[own_rows, :], own_sem)
-    own_copy.start()
-
-    def fetch(image):
-        return pltpu.make_async_copy(
-            cotangent.at[first + image],
-            cot.at[pl.ds(pl.multiple_of(image * kept, kept), kept), :],
-            cot_sem.at[image],
-        )
-
-    for image in range(images):
-        fetch(image).start()
-    meet(column_peers(depth))
-    own_copy.wait()
-    gather = Gather(normed, share, depth, pieces, gather_send, gather_recv)
-    reduce = Reduce(terms, landing, share, depth, pieces, send, recv)
-    mlp_reduce = Reduce(mlp_terms, mlp_landing, share, depth, pieces, mlp_send, mlp_recv)
-    gather.open()
-
-    def block(image, member):
-        return mod[pl.ds(image, 1), member * width : (member + 1) * width]
-
-    def one(image):
-        fetch(image).wait()
-        rows = pl.ds(pl.multiple_of(image * kept, kept), kept)
-        live = lax.broadcasted_iota(jnp.int32, (kept, 1), 0) < count[first + image]
-        grad = jnp.where(live, cot[rows, :].astype(F32), 0.0)
-        grad = (block(first + image, 5) * grad).astype(LOW)
-        grad_mlp[rows, :] = grad
-        down_sums[image] = jnp.sum(grad.astype(F32), axis=0, keepdims=True)
-        source = normed[rows, :]
-        mlp = None
-        back = None
-        for shard, (weight_up, row, weight_down) in enumerate(
-            ((up_own, row_own, down_own), (up_other, row_other, down_other))
-        ):
-            bias = row[:, spots["up"] : spots["up"] + units]
-            pre = dot_nt(source, weight_up[...]) + bias
-            square = pre * pre
-            bent = jnp.tanh(GELU_ROOT * pre * (1.0 + GELU_CUBE * square))
-            half = 0.5 * (1.0 + bent)
-            low_hidden = (pre * half).astype(LOW)
-            hidden[shard, rows, :] = low_hidden
-            slope = half + 0.5 * pre * (1.0 - bent * bent) * (
-                GELU_ROOT * (1.0 + 3.0 * GELU_CUBE * square)
-            )
-            low_grad = (slope * dot_nt(grad, weight_down[...])).astype(LOW)
-            grad_pre[shard, rows, :] = low_grad
-            up_sums[shard, image] = jnp.sum(low_grad.astype(F32), axis=0, keepdims=True)
-            mlp_part = dot(low_hidden, weight_down[...])
-            back_part = dot(low_grad, weight_up[...])
-            mlp = mlp_part if mlp is None else mlp + mlp_part
-            back = back_part if back is None else back + back_part
-        terms[rows, :] = back.astype(LOW)
-        mlp_terms[rows, :] = mlp.astype(LOW)
-        for part in range(fold):
-            reduce.ready_share(image * fold + part)
-            mlp_reduce.ready_share(image * fold + part)
-
-    if fold == 1:
-
-        def turn_of(turn, carry):
-            @pl.when(turn == 1)
-            def _():
-                gather.relay()
-
-            offset = turn + (turn // 2) * (1 - 2 * (turn % 2))
-            gather.take(offset)
-            one(across(up, offset, depth))
-            return carry
-
-        lax.fori_loop(0, depth, turn_of, 0)
-    else:
-
-        def image_of(image, carry):
-            one(image)
-            return carry
-
-        gather.relay()
-        for offset in range(1, depth):
-            gather.take(offset)
-        lax.fori_loop(0, images, image_of, 0)
-    reduce.relay()
-    mlp_reduce.relay()
-    wide = tile_of(width)
-    for shard in range(PAIR):
-
-        def tile(step, carry):
-            columns = pl.ds(pl.multiple_of(step * wide, 128), wide)
-            up_grad[shard, 0:units, columns] = dot_tn(
-                grad_pre[shard], normed[:, columns]
-            ).astype(LOW)
-            down_grad[shard, 0:units, columns] = dot_tn(
-                hidden[shard], grad_mlp[:, columns]
-            ).astype(LOW)
-            return carry
-
-        lax.fori_loop(0, width // wide, tile, 0)
-        if units < up_grad.shape[1]:
-            rest = jnp.zeros((up_grad.shape[1] - units, width), LOW)
-            up_grad[shard, units:, :] = rest
-            down_grad[shard, units:, :] = rest
-    reduce.finish(total)
-    for shard in range(PAIR):
-        up_bias_grad[shard : shard + 1, :] = sum(up_sums[shard, image] for image in range(images))
-    down_bias_grad[...] = sum(down_sums[image] for image in range(images))
-    image = first + (up * share) // kept
-    place_in = (up * share) % kept
-    live = (
-        lax.broadcasted_iota(jnp.int32, (share, 1), 0) + place_in < count[image]
-    )
-    grad_out = jnp.where(live, cot[own_rows, :].astype(F32), 0.0)
-    norm, spread = norm_parts(mid[...])
-    back = total[...]
-    grad_mid = grad_out + norm_back(norm, spread, back * (1.0 + block(image, 4)))
-    grad_mid_out[...] = grad_mid
-    grad_branch_out[...] = (block(image, 2) * grad_mid).astype(LOW)
-    sums_out[0:1, :] = jnp.sum(grad_mid * branch[...], axis=0, keepdims=True)
-    sums_out[1:2, :] = jnp.sum(back, axis=0, keepdims=True)
-    sums_out[2:3, :] = jnp.sum(back * norm, axis=0, keepdims=True)
-    mlp_reduce.finish(mlp_total)
-    mlp = mlp_total[...] + row_own[:, spots["down"] : spots["down"] + width]
-    sums_out[3:4, :] = jnp.sum(grad_out * mlp, axis=0, keepdims=True)
-    block_own[...] = jnp.where(live, mid[...] + block(image, 5) * mlp, 0.0).astype(LOW)
-    gather.close()
-    reduce.close()
-    mlp_reduce.close()
-
-
-def feed(sizes, groups, args):
-    depth, images, kept, share, pieces = sizes
-    width = args[1].shape[1]
-    units = args[4].shape[0]
-    rows = images * kept
-    shape = jax.ShapeDtypeStruct
-    return pl.pallas_call(
-        functools.partial(feed_kernel, sizes),
-        out_shape=(
-            shape((PAIR, padded(units, groups), width), LOW),
-            shape((PAIR, padded(units, groups), width), LOW),
-            shape((PAIR, units), F32),
-            shape((1, width), F32),
-            shape((share, width), LOW),
-            shape((share, width), F32),
-            shape((share, width), LOW),
-            shape((4, width), F32),
-        ),
-        in_specs=[SM, VM, HB] + [VM] * 9,
-        out_specs=(VM,) * 8,
-        scratch_shapes=[
+        + Share.scratch(4, groups)
+        + [
             pltpu.VMEM((rows, width), LOW),
             pltpu.VMEM((rows, width), LOW),
             pltpu.VMEM((PAIR, rows, units), LOW),
@@ -1252,20 +1231,21 @@
             pltpu.VMEM((rows - share, width), LOW),
             pltpu.VMEM((rows, width), LOW),
             pltpu.VMEM((rows - share, width), LOW),
+            pltpu.VMEM((rows, width), F32),
+            pltpu.VMEM((rows, width), F32),
             pltpu.VMEM((share, width), F32),
             pltpu.VMEM((share, width), F32),
             pltpu.VMEM((PAIR, images, 1, units), F32),
             pltpu.VMEM((images, 1, width), F32),
             DMA((images,)),
-            DMA,
         ]
         + Gather.scratch(depth, pieces)
         + Reduce.scratch(depth, pieces)
         + Reduce.scratch(depth, pieces),
         compiler_params=pltpu.CompilerParams(
-            collective_id=2, has_side_effects=True, vmem_limit_bytes=60 << 20
+            collective_id=1, has_side_effects=True, vmem_limit_bytes=62 << 20
         ),
-        name="feed",
+        name="ahead",
     )(*args)
 
 
@@ -1855,21 +1835,9 @@
         proj,
         attended,
         tokens_own,
-        mid,
-        branch,
-        normed_two,
         mod,
         silu_all,
         heads_other,
-        up_other,
-        down_other,
-        row_other,
-    ) = attend(
-        sizes,
-        groups,
-        (keep_count, keep_index, patches, conditioning, mod_rows, heads, up, down_weight, row),
-    )
-    (
         up_grad,
         down_grad,
         up_bias_grad,
@@ -1878,22 +1846,20 @@
         grad_mid,
         grad_branch,
         sums_two,
-    ) = feed(
+    ) = ahead(
         sizes,
         groups,
         (
             keep_count,
-            normed_two,
+            keep_index,
+            patches,
             out_cotangent,
-            mod,
+            conditioning,
+            mod_rows,
+            heads,
             up,
-            up_other,
+            down_weight,
             row,
-            row_other,
-            down_weight,
-            down_other,
-            mid,
-            branch,
         ),
     )
     (

time: 350 us -> 339 us (0.969)
  Pallas kernels: 315 us -> 305 us
    pallas_call x2 -> x1, Pallas kernels: 143 us -> 132 us  [ahead(): pl.pallas_call(functools.partial(ahead_kernel, sizes, groups), out_shape=...]
where the time goes in v5:
time: 339 us
  Pallas kernels  305 us (90%)
  local copies, waits for them, and re-layouts  29.4 us (9%)
  other arithmetic  3.76 us (1%)
    pallas_call x1, Pallas kernels, ahead(): pl.pallas_call(functools.partial(ahead_kernel, sizes, groups), out_shape=...  132 us
    pallas_call x1, Pallas kernels, attend_back(): pl.pallas_call(functools.partial(attend_back_kernel, sizes, groups), out_...  95.4 us
    pallas_call x1, Pallas kernels, close(): pl.pallas_call(functools.partial(close_kernel, sizes, groups), out_shape=...  77.1 us
    unnamed x23, local copies, waits for them, and re-layouts  17.2 us

profile of v5, /device:TPU:0, one launch (start us, length us, event | category | flops | bytes accessed | tf_op | source)
XLA Modules:
  0.0 338.7 jit_solution(7510428472867300157)
XLA Ops:
  0.6 0.8 slice_reduce_fusion.3
  1.4 0.7 pad.22
  2.1 0.7 pad.19
  2.8 0.9 dynamic-update-slice
  3.7 0.9 dynamic-update-slice.1
  4.6 0.2 dynamic-update-slice.2
  4.8 0.2 dynamic-update-slice.3
  5.0 0.2 dynamic-update-slice.4
  5.2 0.2 dynamic-update-slice.5
  5.4 0.6 reshape.42.row_own
  6.0 2.5 pad_maximum_fusion.heads_own
  8.5 132.4 %ahead.1 = (bf16[768,1152]{1,0:T(8,128)(2,1)}, bf16[2,3,768,144]{3,2,1,0:T(8,128)(2,1)}, bf16[2,768,144]{2,1,0:T(8,128)(2,1)}, bf16[192,1152]{1,0:T(8,128)(2,1)}...) custom-call(s32[8]{0:T(128)} %count.3, ...), custom_call_target="tpu_custom_call" | custom-call | tf_op jit(solution)/shard_map/ahead/pallas_call | solution.py:1180
  140.8 95.4 %attend_back.1 = (bf16[2,576,1152]{2,1,0:T(8,128)(2,1)}, f32[4,144]{1,0:T(4,128)}, f32[1,1152]{1,0:T(1,128)}, bf16[192,1152]{1,0:T(8,128)(2,1)}, f32[2,1152]{1,0...) custom-call(s32[8]{0:T(128)} %count.3, ...), custom_call_target="tpu_custom_call" | custom-call | tf_op jit(solution)/shard_map/attend_back/pallas_call | solution.py:1460
  236.3 77.1 %close.1 = (bf16[8,256,1152]{2,1,0:T(8,128)(2,1)}, f32[576,1152]{1,0:T(8,128)}, f32[8,1152]{1,0:T(8,128)}, f32[864,1152]{1,0:T(8,128)}, f32[1,864]{1,0:T(1,128)}, /*index=5*/bf16[8,1152]{1,0:T(8,128)(2,1)}) custom-call(s32[8,192]{1,0:T(8,128)} %index.3, bf16[192,1152]{1,0:T(8,128)(2,1)} %get-tuple-element.54.grad_tokens, ...), custom_call_target="tpu_custom_call" | custom-call | tf_op jit(solution)/shard_map/close/pallas_call | solution.py:1755
  313.4 1.3 slice.27
  314.7 1.3 reduce.2
  316.0 1.3 slice_reduce_fusion.2
  317.3 1.5 slice_reduce_fusion
  318.8 2.1 slice.28
  320.9 3.0 slice.26
  323.9 0.0 copy-done.2
  323.9 1.8 copy.40
  325.7 1.8 copy-done
  327.5 2.4 copy.41
  329.9 0.0 copy-done.5
  329.9 0.6 copy.42
  330.5 0.8 copy-done.1
  331.3 2.0 copy.43
  333.4 1.2 copy-done.4
  334.5 1.5 copy.44
  336.0 1.2 copy-done.3
  337.2 1.5 copy.45
  (9 shorter events, 0.0 us)
Async XLA Ops:
  318.8 5.1 %copy-start.2 = (bf16[1536,1152]{1,0:T(8,128)(2,1)S(1)}, bf16[1536,1152]{1,0:T(8,128)(2,1)}, u32[]{:S(2)}) copy-start(bf16[1536,1152]{1,0:T(8,128)(2,1)} %get-tuple-element.53) | copy-start | bytes 10616836
  323.9 3.6 %copy-start = (bf16[8,256,1152]{2,1,0:T(8,128)(2,1)S(1)}, bf16[8,256,1152]{2,1,0:T(8,128)(2,1)}, u32[]{:S(2)}) copy-start(bf16[8,256,1152]{2,1,0:T(8,128)(2,1)} %get-tuple-element.89) | copy-start | bytes 14155780
  327.5 2.4 copy-start.5
  327.5 3.9 %copy-start.1 = (f32[864,1152]{1,0:T(8,128)S(1)}, f32[864,1152]{1,0:T(8,128)}, u32[]{:S(2)}) copy-start(f32[864,1152]{1,0:T(8,128)} %get-tuple-element.65) | copy-start | bytes 11943940
  331.3 3.2 copy-start.4
  334.5 2.7 copy-start.3

commit v6 on v5

--- a/solution.py
+++ b/solution.py
@@ -389,15 +389,14 @@
 
 
 class Fold:
-    def __init__(self, source, scratch, out, depth, groups):
-        self.source, self.out = source, out
+    def __init__(self, source, scratch, low, depth, groups):
+        self.source, self.low = source, low
         (
             self.stage,
             self.near,
             self.land,
             self.part,
             self.side_land,
-            self.low,
             self.send,
             self.recv,
         ) = scratch
@@ -422,7 +421,6 @@
             pltpu.VMEM((lines, PAIR, part, width), LOW),
             pltpu.VMEM((PAIR, part, width), LOW),
             pltpu.VMEM((part, width), LOW),
-            pltpu.VMEM((rows, width), LOW),
             DMA((2 + 3 * lines,)),
             DMA((2 + 3 * lines,)),
         ]
@@ -559,12 +557,6 @@
     def six(self):
         for line in range(self.lines):
             self.mate_copy(1 - self.core, line).wait_recv()
-
-        def put(at, size):
-            rows = pl.ds(at, size)
-            self.out[rows, :] = self.low[rows, :].astype(F32)
-
-        self.each(self.out.shape[0], put)
         self.near_copy().wait_send()
         self.side_copy().wait_send()
         for step in range(1, self.lines):
@@ -1294,9 +1286,9 @@
     scale = HD ** (-0.5)
     fold = depth // images
     first = side * images
-    up_fold = Fold(up_grad, rest[:8], up_total, depth, groups)
-    down_fold = Fold(down_grad, rest[8:16], down_total, depth, groups)
-    spread = Spread(block_out, share, depth, pieces, rest[16:20])
+    up_fold = Fold(up_grad, rest[:7], up_total, depth, groups)
+    down_fold = Fold(down_grad, rest[7:14], down_total, depth, groups)
+    spread = Spread(block_out, share, depth, pieces, rest[14:18])
     own_rows = pl.ds(pl.multiple_of(up * share, share), share)
     own_copy = pltpu.make_async_copy(grad_own, grads.at[own_rows, :], own_sem.at[0])
     own_copy.start()
@@ -1454,7 +1446,7 @@
     depth, images, kept, share, pieces = sizes
     width = args[1].shape[1]
     local = args[5].shape[0] // 4
-    up_grad, down_grad, units = args[-3:]
+    up_grad, down_grad = args[-2:]
     rows = images * kept
     shape = jax.ShapeDtypeStruct
     return pl.pallas_call(
@@ -1466,8 +1458,8 @@
             shape((share, width), LOW),
             shape((2, width), F32),
             shape((PAIR * rows, width), LOW),
-            shape((units, width), F32),
-            shape((units, width), F32),
+            shape(up_grad.shape[1:], LOW),
+            shape(down_grad.shape[1:], LOW),
         ),
         in_specs=[SM] + [VM] * 12,
         out_specs=(VM,) * 8,
@@ -1490,7 +1482,7 @@
             collective_id=3, has_side_effects=True, vmem_limit_bytes=62 << 20
         ),
         name="attend_back",
-    )(*args[:-1])
+    )(*args)
 
 
 def split_low(value):
@@ -1503,7 +1495,6 @@
 def close_kernel(
     sizes,
     groups,
-    index,
     grad_tokens,
     sums_one,
     sums_two,
@@ -1515,13 +1506,13 @@
     silu_all,
     mod_weight,
     cond,
-    grad_patches,
+    whole,
     heads_total,
     bias_total,
-    mod_weight_grad,
+    grads_out,
+    silu_out,
     mod_bias_grad,
     grad_cond,
-    whole,
     biases,
     sum_row,
     sum_land,
@@ -1540,14 +1531,13 @@
     devices = depth * PAIR
     everyone = devices * groups
     me, _, side = place(depth)
-    up = me // PAIR
     group = lax.axis_index("dp")
     flat = group * devices + me
     width = grad_tokens.shape[1]
     columns = mod_weight.shape[0]
     span = sum_land.shape[2]
     spread = Spread(whole, share, depth, pieces, rest[:4])
-    fold = Fold(heads_grad, rest[4:12], heads_total, depth, groups)
+    fold = Fold(heads_grad, rest[4:11], heads_total, depth, groups)
     own_copy = pltpu.make_async_copy(grad_tokens, spread.own(), own_sem)
     own_copy.start()
     barrier = pltpu.get_barrier_semaphore()
@@ -1637,7 +1627,7 @@
     target = lax.broadcasted_iota(jnp.int32, (everyone, groups * total_images), 1)
     row_image = source // devices * total_images + image_of(source % devices)
     chosen = jnp.where(row_image == target, 1.0, 0.0).astype(LOW)
-    silu_rows = dot(
+    silu_out[...] = dot(
         chosen,
         jnp.concatenate([silu_all[member].astype(F32) for member in range(groups)], axis=0).astype(
             LOW
@@ -1646,9 +1636,7 @@
     parts = split_low(grads)
     spread.take(1)
     fold.three()
-    mod_weight_grad[...] = (
-        dot_tn(parts[0], silu_rows) + dot_tn(parts[1], silu_rows) + dot_tn(parts[2], silu_rows)
-    )
+    grads_out[...] = grads.T
     source = lax.broadcasted_iota(jnp.int32, (total_images, everyone), 1)
     target = lax.broadcasted_iota(jnp.int32, (total_images, everyone), 0)
     chosen = jnp.where(
@@ -1701,29 +1689,10 @@
     value = cond[...].astype(F32)
     gate = 1.0 / (1.0 + jnp.exp(-value))
     grad_cond[...] = (back * (gate + value * gate * (1.0 - gate))).astype(LOW)
-
-    def place_image(image):
-        rows = pl.ds(pl.multiple_of(image * kept, kept), kept)
-        positions = lax.broadcasted_iota(jnp.int32, (grad_patches.shape[1], kept), 0)
-        pick = jnp.where(positions == index[pl.ds(image, 1), :], 1.0, 0.0).astype(LOW)
-        grad_patches[image] = dot(pick, whole[rows, :]).astype(LOW)
-
-    both = PAIR * share // kept
-
-    def put(where):
-        spread.crossed(where)
-        for image in range(both):
-            place_image(where * both + image)
-
-    def arrived(turn, carry):
-        put(spread.line.arrival(turn)[2])
-        return carry
-
-    put(up)
-    lax.fori_loop(1, depth - 1, arrived, 0)
     spread.take(depth - 1)
     fold.five()
-    put(spread.line.arrival(depth - 1)[2])
+    for where in range(depth):
+        spread.crossed(where)
     fold.six()
     spread.close()
 
@@ -1740,8 +1709,8 @@
 
 def close(sizes, groups, args):
     depth, images, kept, share, pieces = sizes
-    index, grad_tokens = args[:2]
-    heads_grad, silu_all, mod_weight, cond, local, spots = args[-6:]
+    grad_tokens = args[0]
+    heads_grad, silu_all, mod_weight, cond = args[-4:]
     devices = depth * PAIR
     width = grad_tokens.shape[1]
     columns = mod_weight.shape[0]
@@ -1755,17 +1724,17 @@
     return pl.pallas_call(
         functools.partial(close_kernel, sizes, groups),
         out_shape=(
-            shape((PAIR * images, spots, width), LOW),
-            shape((4 * local, width), F32),
+            shape((rows, width), LOW),
+            shape(heads_grad.shape[1:], LOW),
             shape(biases, F32),
-            shape(mod_weight.shape, F32),
+            shape((columns, everyone), F32),
+            shape((everyone, width), LOW),
             shape((1, columns), F32),
             shape(cond.shape, LOW),
         ),
-        in_specs=[VM] * 12,
-        out_specs=(VM,) * 6,
+        in_specs=[VM] * 11,
+        out_specs=(VM,) * 7,
         scratch_shapes=[
-            pltpu.VMEM((rows, width), LOW),
             pltpu.VMEM(biases, F32),
             pltpu.VMEM((1, long), F32),
             pltpu.VMEM((everyone, 1, span), F32),
@@ -1785,7 +1754,130 @@
             collective_id=4, has_side_effects=True, vmem_limit_bytes=62 << 20
         ),
         name="close",
-    )(*args[:-2])
+    )(*args)
+
+
+def settle_kernel(
+    index,
+    whole,
+    block,
+    up_low,
+    down_low,
+    heads_low,
+    mod_grads,
+    silu_rows,
+    biases,
+    mod_bias,
+    cond,
+    block_out,
+    grad_patches,
+    grad_cond,
+    mod_rows_grad,
+    mod_bias_grad,
+    qkv_grad,
+    qv_grad,
+    out_grad,
+    out_bias_grad,
+    up_grad,
+    up_bias_grad,
+    down_grad,
+    down_bias_grad,
+):
+    members, kept, _ = block_out.shape
+    step = pl.program_id(0)
+    local, units = out_grad.shape[0], up_bias_grad.shape[1]
+    for member in range(members):
+        rows = slice(member * kept, (member + 1) * kept)
+        block_out[member] = block[rows, :]
+        positions = lax.broadcasted_iota(jnp.int32, (grad_patches.shape[1], kept), 0)
+        listed = index[pl.ds(step * members + member, 1), :]
+        pick = jnp.where(positions == listed, 1.0, 0.0).astype(LOW)
+        grad_patches[member] = dot(pick, whole[rows, :]).astype(LOW)
+    parts = split_low(mod_grads[...])
+    silu = silu_rows[...]
+    mod_rows_grad[...] = dot(parts[0], silu) + dot(parts[1], silu) + dot(parts[2], silu)
+    up_grad[...] = up_low[...].astype(F32)
+    down_grad[...] = down_low[...].astype(F32)
+
+    @pl.when(step == 0)
+    def _():
+        for member in range(3):
+            qkv_grad[member] = heads_low[member * local : (member + 1) * local, :].astype(F32)
+        out_grad[...] = heads_low[3 * local : 4 * local, :].astype(F32)
+        grad_cond[...] = cond[...]
+        mod_bias_grad[...] = mod_bias[...]
+        qv_grad[...] = biases[1:3, 0:local]
+        up_bias_grad[...] = biases[0:1, 0:units]
+        down_bias_grad[...] = biases[6:7, :]
+        out_bias_grad[...] = biases[7:8, :]
+
+
+def settle(local, units, spots, args):
+    index, whole, block, up_low, down_low, heads_low, mod_grads, silu_rows, biases, mod_bias, cond = args
+    images, kept = index.shape
+    width = whole.shape[1]
+    mods = mod_bias.shape[1]
+    steps = 4 if units % 64 == 0 and mods % 32 == 0 else 2
+    members = images // steps
+    shape = jax.ShapeDtypeStruct
+
+    def full(array):
+        return pl.BlockSpec(array.shape, lambda step: (0,) * len(array.shape))
+
+    def part(array, rows):
+        rest = array.shape[1:]
+        return pl.BlockSpec((rows,) + rest, lambda step: (step,) + (0,) * len(rest))
+
+    outs = (
+        shape((images, kept, width), LOW),
+        shape((images, spots, width), LOW),
+        shape(cond.shape, LOW),
+        shape((mods, width), F32),
+        shape((1, mods), F32),
+        shape((3, local, width), F32),
+        shape((2, local), F32),
+        shape((local, width), F32),
+        shape((1, width), F32),
+        shape((units, width), F32),
+        shape((1, units), F32),
+        shape((units, width), F32),
+        shape((1, width), F32),
+    )
+    return pl.pallas_call(
+        settle_kernel,
+        grid=(steps,),
+        out_shape=outs,
+        in_specs=[
+            full(index),
+            part(whole, members * kept),
+            part(block, members * kept),
+            part(up_low, units // steps),
+            part(down_low, units // steps),
+            full(heads_low),
+            part(mod_grads, mods // steps),
+            full(silu_rows),
+            full(biases),
+            full(mod_bias),
+            full(cond),
+        ],
+        out_specs=(
+            part(outs[0], members),
+            part(outs[1], members),
+            full(outs[2]),
+            part(outs[3], mods // steps),
+            full(outs[4]),
+            full(outs[5]),
+            full(outs[6]),
+            full(outs[7]),
+            full(outs[8]),
+            part(outs[9], units // steps),
+            full(outs[10]),
+            part(outs[11], units // steps),
+            full(outs[12]),
+        ),
+        compiler_params=pltpu.CompilerParams(vmem_limit_bytes=60 << 20),
+        name="settle",
+    )(*args)
 
 
 def on_device(
@@ -1888,21 +1980,20 @@
             block_own,
             up_grad,
             down_grad,
-            units,
         ),
     )
     (
-        grad_patches,
+        grad_whole,
         heads_total,
         bias_total,
-        mod_rows_grad,
-        mod_bias_grad,
-        grad_conditioning,
+        mod_grads,
+        silu_rows,
+        mod_bias_total,
+        cond_total,
     ) = close(
         sizes,
         groups,
         (
-            keep_index,
             grad_tokens,
             sums_one,
             sums_two,
@@ -1914,24 +2005,54 @@
             silu_all,
             mod_rows,
             conditioning,
-            local,
-            patches.shape[1],
+        ),
+    )
+    (
+        block_out,
+        grad_patches,
+        grad_conditioning,
+        mod_rows_grad,
+        mod_bias_grad,
+        qkv_grad,
+        qv_bias_grad,
+        out_weight_grad,
+        out_bias_grad,
+        up_rows_grad,
+        up_bias_grad,
+        down_weight_grad,
+        down_bias_grad,
+    ) = settle(
+        local,
+        units,
+        patches.shape[1],
+        (
+            keep_index,
+            grad_whole,
+            block_out,
+            up_total,
+            down_total,
+            heads_total,
+            mod_grads,
+            silu_rows,
+            bias_total,
+            mod_bias_total,
+            cond_total,
         ),
     )
     return (
-        block_out.reshape(all_images, kept, width),
+        block_out,
         grad_patches,
         grad_conditioning,
         mod_rows_grad.T,
         mod_bias_grad[0],
-        jnp.swapaxes(heads_total[: 3 * local].reshape(3, local, width), 1, 2),
-        bias_total[1:3, :local],
-        heads_total[3 * local :],
-        bias_total[7],
-        up_total.T,
-        bias_total[0, :units],
-        down_total,
-        bias_total[6],
+        jnp.swapaxes(qkv_grad, 1, 2),
+        qv_bias_grad,
+        out_weight_grad,
+        out_bias_grad[0],
+        up_rows_grad.T,
+        up_bias_grad[0],
+        down_weight_grad,
+        down_bias_grad[0],
     )
 
 

time: 339 us -> 327 us (0.965)
  local copies, waits for them, and re-layouts: 29.4 us -> 5.34 us
  Pallas kernels: 305 us -> 313 us
  other arithmetic: 3.76 us -> 7.66 us
    unnamed x23 -> x5, local copies, waits for them, and re-layouts: 17.2 us -> 2.36 us
    pallas_call x0 -> x1, Pallas kernels: none -> 13 us  [settle(): pl.pallas_call(settle_kernel, grid=(steps,), out_shape=outs, in_specs=[fu...]
    slice x5 -> x0, local copies, waits for them, and re-layouts: 9.16 us -> none  [the longest x1 2.96 us: on_device(): heads_total[:3 * local].reshape(3, local, width)]
    pallas_call x1, Pallas kernels: 77.1 us -> 73 us  [close(): pl.pallas_call(functools.partial(close_kernel, sizes, groups), out_shape=...]
    pallas_call x1 -> x4, other arithmetic: 1.28 us -> 5.19 us  [settle(): pl.pallas_call(settle_kernel, grid=(steps,), out_shape=outs, in_specs=[fu...]
where the time goes in v6:
time: 327 us
  Pallas kernels  313 us (96%)
  other arithmetic  7.66 us (2%)
  local copies, waits for them, and re-layouts  5.34 us (2%)
    pallas_call x1, Pallas kernels, ahead(): pl.pallas_call(functools.partial(ahead_kernel, sizes, groups), out_shape=...  132 us
    pallas_call x1, Pallas kernels, attend_back(): pl.pallas_call(functools.partial(attend_back_kernel, sizes, groups), out_...  94.6 us
    pallas_call x1, Pallas kernels, close(): pl.pallas_call(functools.partial(close_kernel, sizes, groups), out_shape=...  73 us
    pallas_call x1, Pallas kernels, settle(): pl.pallas_call(settle_kernel, grid=(steps,), out_shape=outs, in_specs=[fu...  13 us

profile of v6, /device:TPU:0, one launch (start us, length us, event | category | flops | bytes accessed | tf_op | source)
XLA Modules:
  0.0 326.7 jit_solution(10715805423141268387)
XLA Ops:
  0.6 0.8 slice_reduce_fusion
  1.4 0.7 pad.22
  2.1 0.7 pad.19
  2.8 0.9 dynamic-update-slice
  3.7 0.9 dynamic-update-slice.1
  4.6 0.2 dynamic-update-slice.2
  4.8 0.2 dynamic-update-slice.3
  5.0 0.2 dynamic-update-slice.4
  5.2 0.2 dynamic-update-slice.5
  5.4 0.6 reshape.34.row_own
  6.0 2.5 pad_maximum_fusion.heads_own
  8.5 132.4 %ahead.1 = (bf16[768,1152]{1,0:T(8,128)(2,1)}, bf16[2,3,768,144]{3,2,1,0:T(8,128)(2,1)}, bf16[2,768,144]{2,1,0:T(8,128)(2,1)}, bf16[192,1152]{1,0:T(8,128)(2,1)}...) custom-call(s32[8]{0:T(128)} %count.3, ...), custom_call_target="tpu_custom_call" | custom-call | tf_op jit(solution)/shard_map/ahead/pallas_call | solution.py:1172
  140.9 94.6 %attend_back.1 = (bf16[2,576,1152]{2,1,0:T(8,128)(2,1)}, f32[4,144]{1,0:T(4,128)}, f32[1,1152]{1,0:T(1,128)}, bf16[192,1152]{1,0:T(8,128)(2,1)}, f32[2,1152]{1,0...) custom-call(s32[8]{0:T(128)} %count.3, ...), custom_call_target="tpu_custom_call" | custom-call | tf_op jit(solution)/shard_map/attend_back/pallas_call | solution.py:1452
  235.5 73.0 %close.1 = (bf16[1536,1152]{1,0:T(8,128)(2,1)}, bf16[576,1152]{1,0:T(8,128)(2,1)}, f32[8,1152]{1,0:T(8,128)}, f32[864,32]{1,0:T(8,128)}, bf16[32,1152]{1,0:T(8,1...) custom-call(bf16[192,1152]{1,0:T(8,128)(2,1)} %get-tuple-element.67.grad_tokens, ...), custom_call_target="tpu_custom_call" | custom-call | tf_op jit(solution)/shard_map/close/pallas_call | solution.py:1724
  308.5 13.0 %settle.1 = (bf16[8,192,1152]{2,1,0:T(8,128)(2,1)}, bf16[8,256,1152]{2,1,0:T(8,128)(2,1)}, bf16[8,1152]{1,0:T(8,128)(2,1)}, f32[864,1152]{1,0:T(8,128)}, f32[1,8...) custom-call(s32[8,192]{1,0:T(8,128)} %index.3, ...), custom_call_target="tpu_custom_call" | custom-call | tf_op jit(solution)/shard_map/settle/pallas_call | solution.py:1846
  321.5 1.3 reduce.2
  322.8 1.3 reduce.4
  324.1 1.3 reduce.3
  325.4 1.3 reduce.5
  (3 shorter events, 0.0 us)

commit v7 on v6

--- a/solution.py
+++ b/solution.py
@@ -777,12 +777,17 @@
     index,
     patches,
     cotangent,
+    qkv,
+    out_weight,
     cond,
     mod_weight,
-    heads_own,
     up_own,
     down_own,
-    row_own,
+    mod_bias,
+    qv_bias,
+    out_bias,
+    up_bias,
+    down_bias,
     normed_out,
     proj_out,
     attended_out,
@@ -798,6 +803,9 @@
     grad_mid_out,
     grad_branch_out,
     sums_out,
+    heads_own,
+    row_own,
+    heads_sem,
     up_other,
     down_other,
     row_other,
@@ -874,6 +882,26 @@
             cot_sem.at[image],
         )
 
+    def fetch_heads(member):
+        return pltpu.make_async_copy(
+            qkv.at[member] if member < 3 else out_weight,
+            heads_own.at[pl.ds(member * local, local), :],
+            heads_sem.at[member],
+        )
+
+    for member in range(4):
+        fetch_heads(member).start()
+    row_own[...] = jnp.zeros(row_own.shape, F32)
+    for name, bias in (
+        ("out", out_bias[...]),
+        ("down", down_bias[...]),
+        ("up", up_bias[...]),
+        ("query", qv_bias[0:1, :]),
+        ("value", qv_bias[1:2, :]),
+        ("mod", mod_bias[...]),
+    ):
+        size = bias.shape[-1]
+        row_own[:, spots[name] : spots[name] + size] = bias.astype(F32).reshape(1, size)
     for turn in range(images):
         fetch(image_at(turn)).start()
     meet(
@@ -923,6 +951,8 @@
             )
         )
     ]
+    for member in range(4):
+        fetch_heads(member).wait()
     outer = up // (depth // PAIR) == side
     shares[0].start()
     shares[1].start()
@@ -1161,12 +1191,14 @@
 
 def ahead(sizes, groups, args):
     depth, images, kept, share, pieces = sizes
-    count, index, patches, cotangent, cond, mod_weight, heads, up, down, row = args
+    patches, cotangent, qkv, out_weight, cond, mod_weight, up, down = args[2:10]
     spots, width = patches.shape[1:]
-    local = heads.shape[0] // 4
+    local = out_weight.shape[0]
     mods = mod_weight.shape[0]
     units = up.shape[0]
     rows = images * kept
+    heads = (4 * local, width)
+    row = (1, row_spots(width, units, local, mods)[1])
     shape = jax.ShapeDtypeStruct
     devices = depth * PAIR
     return pl.pallas_call(
@@ -1178,7 +1210,7 @@
             shape((share, width), LOW),
             shape((cond.shape[0], devices * mods), F32),
             shape((groups,) + cond.shape, LOW),
-            shape(heads.shape, LOW),
+            shape(heads, LOW),
             shape((PAIR, padded(units, groups), width), LOW),
             shape((PAIR, padded(units, groups), width), LOW),
             shape((PAIR, units), F32),
@@ -1188,12 +1220,15 @@
             shape((share, width), LOW),
             shape((4, width), F32),
         ),
-        in_specs=[SM, VM, HB, HB] + [VM] * 6,
+        in_specs=[SM, VM] + [HB] * 4 + [VM] * 9,
         out_specs=(VM,) * 15,
         scratch_shapes=[
+            pltpu.VMEM(heads, LOW),
+            pltpu.VMEM(row, F32),
+            DMA((4,)),
             pltpu.VMEM(up.shape, LOW),
             pltpu.VMEM(down.shape, LOW),
-            pltpu.VMEM(row.shape, F32),
+            pltpu.VMEM(row, F32),
             pltpu.VMEM((share, width), F32),
             pltpu.VMEM((share, width), F32),
             pltpu.VMEM((images, spots, width), LOW),
@@ -1249,7 +1284,8 @@
     normed,
     proj,
     attended,
-    heads_own,
+    qkv_own,
+    out_own,
     heads_other,
     mod,
     tokens_own,
@@ -1282,7 +1318,7 @@
     depth, images, kept, share, pieces = sizes
     me, up, side = place(depth)
     width = grad_own.shape[1]
-    local = heads_own.shape[0] // 4
+    local = out_own.shape[0]
     scale = HD ** (-0.5)
     fold = depth // images
     first = side * images
@@ -1309,8 +1345,13 @@
         grad = grads[rows, :]
         out_sums[image] = jnp.sum(grad.astype(F32), axis=0, keepdims=True)
         back = None
-        for shard, heads in enumerate((heads_own, heads_other)):
-            grad_att = dot_nt(grad, heads[3 * local :, :]).astype(LOW)
+        for shard in range(PAIR):
+            weights_in = [
+                heads_other[member * local : (member + 1) * local, :] if shard else qkv_own[member]
+                for member in range(3)
+            ]
+            weights_out = heads_other[3 * local :, :] if shard else out_own[...]
+            grad_att = dot_nt(grad, weights_out).astype(LOW)
             queries = proj[shard, 0, rows, :]
             keys = proj[shard, 1, rows, :]
             values = proj[shard, 2, rows, :]
@@ -1331,7 +1372,7 @@
             for member, value in enumerate((grad_q * scale, grad_k * scale, grad_v)):
                 low = value.astype(LOW)
                 grad_proj[shard, member, rows, :] = low
-                part = dot(low, heads[member * local : (member + 1) * local, :])
+                part = dot(low, weights_in[member])
                 back = part if back is None else back + part
                 if member != 1:
                     row = 2 * shard + member // 2
@@ -1445,7 +1486,7 @@
 def attend_back(sizes, groups, args):
     depth, images, kept, share, pieces = sizes
     width = args[1].shape[1]
-    local = args[5].shape[0] // 4
+    local = args[6].shape[0]
     up_grad, down_grad = args[-2:]
     rows = images * kept
     shape = jax.ShapeDtypeStruct
@@ -1461,7 +1502,7 @@
             shape(up_grad.shape[1:], LOW),
             shape(down_grad.shape[1:], LOW),
         ),
-        in_specs=[SM] + [VM] * 12,
+        in_specs=[SM] + [VM] * 13,
         out_specs=(VM,) * 8,
         scratch_shapes=[
             pltpu.VMEM((rows, width), LOW),
@@ -1785,7 +1826,7 @@
 ):
     members, kept, _ = block_out.shape
     step = pl.program_id(0)
-    local, units = out_grad.shape[0], up_bias_grad.shape[1]
+    local, units = out_grad.shape[0], up_bias_grad.shape[0]
     for member in range(members):
         rows = slice(member * kept, (member + 1) * kept)
         block_out[member] = block[rows, :]
@@ -1805,11 +1846,11 @@
             qkv_grad[member] = heads_low[member * local : (member + 1) * local, :].astype(F32)
         out_grad[...] = heads_low[3 * local : 4 * local, :].astype(F32)
         grad_cond[...] = cond[...]
-        mod_bias_grad[...] = mod_bias[...]
+        mod_bias_grad[...] = mod_bias[...].reshape(mod_bias_grad.shape)
         qv_grad[...] = biases[1:3, 0:local]
-        up_bias_grad[...] = biases[0:1, 0:units]
-        down_bias_grad[...] = biases[6:7, :]
-        out_bias_grad[...] = biases[7:8, :]
+        up_bias_grad[...] = biases[0:1, 0:units].reshape(up_bias_grad.shape)
+        down_bias_grad[...] = biases[6:7, :].reshape(down_bias_grad.shape)
+        out_bias_grad[...] = biases[7:8, :].reshape(out_bias_grad.shape)
 
 
 def settle(local, units, spots, args):
@@ -1833,15 +1874,15 @@
         shape((images, spots, width), LOW),
         shape(cond.shape, LOW),
         shape((mods, width), F32),
-        shape((1, mods), F32),
+        shape((mods,), F32),
         shape((3, local, width), F32),
         shape((2, local), F32),
         shape((local, width), F32),
-        shape((1, width), F32),
+        shape((width,), F32),
         shape((units, width), F32),
-        shape((1, units), F32),
+        shape((units,), F32),
         shape((units, width), F32),
-        shape((1, width), F32),
+        shape((width,), F32),
     )
     return pl.pallas_call(
         settle_kernel,
@@ -1906,22 +1947,10 @@
     pieces = 4 if share % 64 == 0 else 2
     sizes = (depth, images, kept, share, pieces)
     groups = lax.axis_size("dp")
-    local, units, mods = qkv_weight.shape[2], up_weight.shape[1], mod_weight.shape[1]
+    local, units = qkv_weight.shape[2], up_weight.shape[1]
     up = up_weight.T
     mod_rows = mod_weight.T
-    heads = jnp.concatenate(
-        [jnp.swapaxes(qkv_weight, 1, 2).reshape(3 * local, width), out_weight], axis=0
-    )
-
-    def spaced(value):
-        return jnp.pad(value.astype(F32), (0, lanes(value.shape[0]) - value.shape[0]))
-
-    row = jnp.concatenate(
-        [
-            spaced(value)
-            for value in (out_bias, down_bias, up_bias, qv_bias[0], qv_bias[1], mod_bias)
-        ]
-    )[None, :]
+    qkv = jnp.swapaxes(qkv_weight, 1, 2)
     (
         normed_one,
         proj,
@@ -1946,12 +1975,17 @@
             keep_index,
             patches,
             out_cotangent,
+            qkv,
+            out_weight,
             conditioning,
             mod_rows,
-            heads,
             up,
             down_weight,
-            row,
+            mod_bias,
+            qv_bias,
+            out_bias,
+            up_bias,
+            down_bias,
         ),
     )
     (
@@ -1972,7 +2006,8 @@
             normed_one,
             proj,
             attended,
-            heads,
+            qkv,
+            out_weight,
             heads_other,
             mod,
             tokens_own,
@@ -2044,15 +2079,15 @@
         grad_patches,
         grad_conditioning,
         mod_rows_grad.T,
-        mod_bias_grad[0],
+        mod_bias_grad,
         jnp.swapaxes(qkv_grad, 1, 2),
         qv_bias_grad,
         out_weight_grad,
-        out_bias_grad[0],
+        out_bias_grad,
         up_rows_grad.T,
-        up_bias_grad[0],
+        up_bias_grad,
         down_weight_grad,
-        down_bias_grad[0],
+        down_bias_grad,
     )
 
 

time: 327 us -> 314 us (0.960)
  other arithmetic: 7.66 us -> 0 us
  local copies, waits for them, and re-layouts: 5.34 us -> 0 us
    pallas_call x4 -> x0, other arithmetic: 5.19 us -> none  [settle(): pl.pallas_call(settle_kernel, grid=(steps,), out_shape=outs, in_specs=[fu...]
where the time goes in v7:
time: 314 us; the launch traced here: 313 us
  Pallas kernels  312 us (99%)
    pallas_call x1, Pallas kernels, ahead(): pl.pallas_call(functools.partial(ahead_kernel, sizes, groups), out_shape=...  132 us
    pallas_call x1, Pallas kernels, attend_back(): pl.pallas_call(functools.partial(attend_back_kernel, sizes, groups), out_...  94.8 us
    pallas_call x1, Pallas kernels, close(): pl.pallas_call(functools.partial(close_kernel, sizes, groups), out_shape=...  72.6 us
    pallas_call x1, Pallas kernels, settle(): pl.pallas_call(settle_kernel, grid=(steps,), out_shape=outs, in_specs=[fu...  13 us

profile of v7, /device:TPU:0, one launch (start us, length us, event | category | flops | bytes accessed | tf_op | source)
XLA Modules:
  0.0 313.0 jit_solution(12741655167389917799)
XLA Ops:
  0.6 131.9 %ahead.1 = (bf16[768,1152]{1,0:T(8,128)(2,1)}, bf16[2,3,768,144]{3,2,1,0:T(8,128)(2,1)}, bf16[2,768,144]{2,1,0:T(8,128)(2,1)}, bf16[192,1152]{1,0:T(8,128)(2,1)}...) custom-call(s32[8]{0:T(128)} %count.3, ...), custom_call_target="tpu_custom_call" | custom-call | tf_op jit(solution)/shard_map/ahead/pallas_call | solution.py:1204
  132.5 94.8 %attend_back.1 = (bf16[2,576,1152]{2,1,0:T(8,128)(2,1)}, f32[4,144]{1,0:T(4,128)}, f32[1,1152]{1,0:T(1,128)}, bf16[192,1152]{1,0:T(8,128)(2,1)}, f32[2,1152]{1,0...) custom-call(s32[8]{0:T(128)} %count.3, ...), custom_call_target="tpu_custom_call" | custom-call | tf_op jit(solution)/shard_map/attend_back/pallas_call | solution.py:1493
  227.3 72.6 %close.1 = (bf16[1536,1152]{1,0:T(8,128)(2,1)}, bf16[576,1152]{1,0:T(8,128)(2,1)}, f32[8,1152]{1,0:T(8,128)}, f32[864,32]{1,0:T(8,128)}, bf16[32,1152]{1,0:T(8,1...) custom-call(bf16[192,1152]{1,0:T(8,128)(2,1)} %get-tuple-element.67.grad_tokens, ...), custom_call_target="tpu_custom_call" | custom-call | tf_op jit(solution)/shard_map/close/pallas_call | solution.py:1765
  299.9 13.0 %settle.1 = (bf16[8,192,1152]{2,1,0:T(8,128)(2,1)}, bf16[8,256,1152]{2,1,0:T(8,128)(2,1)}, bf16[8,1152]{1,0:T(8,128)(2,1)}, f32[864,1152]{1,0:T(8,128)}, f32[864...) custom-call(s32[8,192]{1,0:T(8,128)} %index.3, ...), custom_call_target="tpu_custom_call" | custom-call | tf_op jit(solution)/shard_map/settle/pallas_call | solution.py:1887

commit v8 on v7

--- a/solution.py
+++ b/solution.py
@@ -788,9 +788,9 @@
     out_bias,
     up_bias,
     down_bias,
-    normed_out,
-    proj_out,
-    attended_out,
+    normed_kept,
+    proj_kept,
+    attended_kept,
     tokens_own,
     mod,
     silu_all,
@@ -803,6 +803,10 @@
     grad_mid_out,
     grad_branch_out,
     sums_out,
+    normed_out,
+    proj_out,
+    attended_out,
+    keep_sem,
     heads_own,
     row_own,
     heads_sem,
@@ -1031,6 +1035,18 @@
     shares[1].relay()
     shares[1].wait()
     lax.fori_loop(0, images, two, 0)
+    keeps = [
+        pltpu.make_async_copy(source, target, keep_sem.at[member])
+        for member, (source, target) in enumerate(
+            (
+                (normed_out, normed_kept),
+                (proj_out, proj_kept),
+                (attended_out, attended_kept),
+            )
+        )
+    ]
+    for copy in keeps:
+        copy.start()
 
     @pl.when(outer)
     def _():
@@ -1179,6 +1195,8 @@
         remote(
             view, view, silu_send.at[step], silu_recv.at[step], me, group
         ).wait_recv()
+    for copy in keeps:
+        copy.wait()
     for member in shares:
         member.close()
     for copy in mod_copies + silu_copies:
@@ -1221,8 +1239,12 @@
             shape((4, width), F32),
         ),
         in_specs=[SM, VM] + [HB] * 4 + [VM] * 9,
-        out_specs=(VM,) * 15,
+        out_specs=(HB,) * 3 + (VM,) * 12,
         scratch_shapes=[
+            pltpu.VMEM((rows, width), LOW),
+            pltpu.VMEM((PAIR, 3, rows, local), LOW),
+            pltpu.VMEM((PAIR, rows, local), LOW),
+            DMA((3,)),
             pltpu.VMEM(heads, LOW),
             pltpu.VMEM(row, F32),
             DMA((4,)),
@@ -1281,9 +1303,9 @@
     groups,
     count,
     grad_own,
-    normed,
+    normed_kept,
     proj,
-    attended,
+    attended_kept,
     qkv_own,
     out_own,
     heads_other,
@@ -1301,6 +1323,9 @@
     block_out,
     up_total,
     down_total,
+    normed,
+    attended,
+    kept_sem,
     grads,
     grad_proj,
     terms,
@@ -1330,6 +1355,12 @@
     own_copy.start()
     block_copy = pltpu.make_async_copy(block_own, spread.own(), own_sem.at[1])
     block_copy.start()
+    keeps = [
+        pltpu.make_async_copy(normed_kept, normed, kept_sem.at[0]),
+        pltpu.make_async_copy(attended_kept, attended, kept_sem.at[1]),
+    ]
+    for copy in keeps:
+        copy.start()
     meet(column_peers(depth) + cube_peers(depth, groups) + spread.peers_beyond(depth))
     own_copy.wait()
     gather = Gather(grads, share, depth, pieces, gather_send, gather_recv)
@@ -1436,6 +1467,8 @@
     lax.fori_loop(1, depth - 1, spread_of, 0)
     up_fold.four()
     down_fold.four()
+    for copy in keeps:
+        copy.wait()
     wide = tile_of(width)
     for shard in range(PAIR):
 
@@ -1502,9 +1535,12 @@
             shape(up_grad.shape[1:], LOW),
             shape(down_grad.shape[1:], LOW),
         ),
-        in_specs=[SM] + [VM] * 13,
+        in_specs=[SM, VM, HB, VM, HB] + [VM] * 9,
         out_specs=(VM,) * 8,
         scratch_shapes=[
+            pltpu.VMEM((rows, width), LOW),
+            pltpu.VMEM((PAIR, rows, local), LOW),
+            DMA((2,)),
             pltpu.VMEM((rows, width), LOW),
             pltpu.VMEM((PAIR, 3, rows, local), LOW),
             pltpu.VMEM((rows, width), LOW),

time: 314 us -> 312 us (level)
  no operation moved by 1% of the time
where the time goes in v8:
time: 312 us; the launch traced here: 311 us
  Pallas kernels  310 us (99%)
    pallas_call x1, Pallas kernels, ahead(): pl.pallas_call(functools.partial(ahead_kernel, sizes, groups), out_shape=...  131 us
    pallas_call x1, Pallas kernels, attend_back(): pl.pallas_call(functools.partial(attend_back_kernel, sizes, groups), out_...  94.1 us
    pallas_call x1, Pallas kernels, close(): pl.pallas_call(functools.partial(close_kernel, sizes, groups), out_shape=...  72.8 us
    pallas_call x1, Pallas kernels, settle(): pl.pallas_call(settle_kernel, grid=(steps,), out_shape=outs, in_specs=[fu...  13 us

profile of v8, /device:TPU:0, one launch (start us, length us, event | category | flops | bytes accessed | tf_op | source)
XLA Modules:
  0.0 311.2 jit_solution(7370442913339093463)
XLA Ops:
  0.6 130.5 %ahead.1 = (bf16[768,1152]{1,0:T(8,128)(2,1)}, bf16[2,3,768,144]{3,2,1,0:T(8,128)(2,1)}, bf16[2,768,144]{2,1,0:T(8,128)(2,1)}, bf16[192,1152]{1,0:T(8,128)(2,1)}...) custom-call(s32[8]{0:T(128)} %count.3, ...), custom_call_target="tpu_custom_call" | custom-call | tf_op jit(solution)/shard_map/ahead/pallas_call | solution.py:1222
  131.2 94.1 %attend_back.1 = (bf16[2,576,1152]{2,1,0:T(8,128)(2,1)}, f32[4,144]{1,0:T(4,128)}, f32[1,1152]{1,0:T(1,128)}, bf16[192,1152]{1,0:T(8,128)(2,1)}, f32[2,1152]{1,0...) custom-call(s32[8]{0:T(128)} %count.3, ...), custom_call_target="tpu_custom_call" | custom-call | tf_op jit(solution)/shard_map/attend_back/pallas_call | solution.py:1526
  225.3 72.8 %close.1 = (bf16[1536,1152]{1,0:T(8,128)(2,1)}, bf16[576,1152]{1,0:T(8,128)(2,1)}, f32[8,1152]{1,0:T(8,128)}, f32[864,32]{1,0:T(8,128)}, bf16[32,1152]{1,0:T(8,1...) custom-call(bf16[192,1152]{1,0:T(8,128)(2,1)} %get-tuple-element.67.grad_tokens, ...), custom_call_target="tpu_custom_call" | custom-call | tf_op jit(solution)/shard_map/close/pallas_call | solution.py:1801
  298.1 13.0 %settle.1 = (bf16[8,192,1152]{2,1,0:T(8,128)(2,1)}, bf16[8,256,1152]{2,1,0:T(8,128)(2,1)}, bf16[8,1152]{1,0:T(8,128)(2,1)}, f32[864,1152]{1,0:T(8,128)}, f32[864...) custom-call(s32[8,192]{1,0:T(8,128)} %index.3, ...), custom_call_target="tpu_custom_call" | custom-call | tf_op jit(solution)/shard_map/settle/pallas_call | solution.py:1923
